TPU v7x, 32 devices: a whole 2x2x4 slice. The times are simulated.
32 devices in a mesh: dp: 4 (over y, x), seq: 8 (over z, core).
Axes of the slice: x: 2, y: 2, z: 4, core: 2. Of those that a mesh axis runs over, the one named last changes fastest.
Arguments:
- inputs: bfloat16 [4096, 1536], P(('dp', 'seq')), may hold values from -6 to 6
- cotangent: bfloat16 [4096, 1536], P(('dp', 'seq')), may hold values from -6 to 6
- doc_ids: int32 [4096], P(('dp', 'seq')), may hold values from 0 to 7, as said below
- positions: int32 [4096], P(('dp', 'seq')), may hold values from 0 to 1023, as said below
- gain_first: bfloat16 [1536], P(('dp', 'seq')), may hold values from 0.099609375 to 1.8984375
- query_weight: bfloat16 [1536, 1536], P(('dp', 'seq')), may hold values from -0.21875 to 0.21875
- key_weight: bfloat16 [1536, 768], P(('dp', 'seq')), may hold values from -0.15625 to 0.15625
- value_weight: bfloat16 [1536, 768], P(('dp', 'seq')), may hold values from -0.15625 to 0.15625
- output_weight: bfloat16 [1536, 1536], P(('dp', 'seq')), may hold values from -1.5 to 1.5
- gain_second: bfloat16 [1536], P(('dp', 'seq')), may hold values from 0.099609375 to 1.8984375
- gate_weight: bfloat16 [1536, 4096], P(('dp', 'seq')), may hold values from -0.15625 to 0.15625
- up_weight: bfloat16 [1536, 4096], P(('dp', 'seq')), may hold values from -0.15625 to 0.15625
- down_weight: bfloat16 [4096, 1536], P(('dp', 'seq')), may hold values from -0.09375 to 0.09375
Outputs:
- outputs: bfloat16 [4096, 1536], P(('dp', 'seq'))
- inputs_grad: bfloat16 [4096, 1536], P(('dp', 'seq'))
- first_grad: float32 [1536], P(('dp', 'seq'))
- query_grad: float32 [1536, 1536], P(('dp', 'seq'))
- key_grad: float32 [1536, 768], P(('dp', 'seq'))
- value_grad: float32 [1536, 768], P(('dp', 'seq'))
- output_grad: float32 [1536, 1536], P(('dp', 'seq'))
- second_grad: float32 [1536], P(('dp', 'seq'))
- gate_grad: float32 [1536, 4096], P(('dp', 'seq'))
- up_grad: float32 [1536, 4096], P(('dp', 'seq'))
- down_grad: float32 [4096, 1536], P(('dp', 'seq'))
Inputs may be any that keep to these rules, and one draw needn't show every extreme that they name: `doc_ids`: within each sequence of 1024 rows the id is 0 at the first row and rises by 0 or 1 from one row to the next; all rows of the first sequence share one id, and every other sequence holds exactly 8 documents of ragged lengths. `positions`: A row's offset from the first row of its document (the rows of its sequence with its id).
All inputs are finite; a program needn't handle non-finite values.
Results may differ from a plain program's by a relative error of at most 0.025.
Values may be sent and summed in bfloat16 or wider, within the bound.
No kernel may reach another device: no remote copies, remote signals or barrier semaphores. Data moves between devices by JAX's collectives and lax.ppermute only.
A program may use at most 256 MiB of HBM per device.

v0:
```python
import math

import jax
import jax.numpy as jnp
from jax import lax
from jax.sharding import PartitionSpec as P

D = 1536
HEADS = 16
KV_HEADS = 8
HEAD = 96


norm_epsilon = 1e-05
rotary_base = 100000.0


def normalize(values_in, gain):
    return (
        values_in
        * lax.rsqrt(jnp.mean(values_in * values_in, axis=-1, keepdims=True) + norm_epsilon)
        * gain
    )


def swish_product(gate, upward):
    return jax.nn.silu(gate) * upward


def rotate(matrix, positions, heads_count, direction):
    halfway = HEAD // 2
    inverse_freq = rotary_base ** (-jnp.arange(halfway, dtype=jnp.float32) * 2.0 / HEAD)
    angles = positions.astype(jnp.float32)[:, None] * inverse_freq[None, :]
    cosine = jnp.cos(angles)[:, None, :]
    sine_table = direction * jnp.sin(angles)[:, None, :]
    shaped = matrix.reshape(matrix.shape[0], heads_count, HEAD)
    first_half = shaped[..., :halfway]
    second_half = shaped[..., halfway:]
    turned = jnp.concatenate(
        [
            first_half * cosine - second_half * sine_table,
            second_half * cosine + first_half * sine_table,
        ],
        axis=-1,
    )
    return turned.reshape(matrix.shape)


def times_transposed(left, right):
    return lax.dot_general(
        left, right, (((1,), (1,)), ((), ())), preferred_element_type=jnp.float32
    )


def transposed_times(left, right):
    return lax.dot_general(
        left, right, (((0,), (0,)), ((), ())), preferred_element_type=jnp.float32
    )


def matrix_product(left, right):
    return jnp.dot(left, right, preferred_element_type=jnp.float32)


def block_rows(total_rows):
    size_rows = min(total_rows, 1024)
    while total_rows % size_rows:
        size_rows -= 1
    return size_rows


def fold_local(block_step, initial, arrays):
    total_rows = arrays[0].shape[0]
    size_rows = block_rows(total_rows)

    def one_turn(turn_index, state_in):
        begin_row = turn_index * size_rows
        pieces = tuple(
            (lax.dynamic_slice_in_dim(member, begin_row, size_rows, 0) for member in arrays)
        )
        return block_step(state_in, pieces, begin_row)

    return lax.fori_loop(0, total_rows // size_rows, one_turn, initial)


def piece_fold(block_step, state_in, pieces):
    return fold_local(block_step, state_in, pieces)


def keep_state(state_now):
    return state_now


def body(
    inputs,
    cotangent,
    doc_ids,
    positions,
    gain_first,
    query_weight,
    key_weight,
    value_weight,
    output_weight,
    gain_second,
    gate_weight,
    up_weight,
    down_weight,
):
    f32 = jnp.float32
    bf16 = jnp.bfloat16
    attend_set = (
        lax.all_gather(gain_first, ("dp", "seq"), axis=0, tiled=True),
        lax.all_gather(query_weight, ("dp", "seq"), axis=0, tiled=True),
        lax.all_gather(key_weight, ("dp", "seq"), axis=0, tiled=True),
        lax.all_gather(value_weight, ("dp", "seq"), axis=0, tiled=True),
        lax.all_gather(output_weight, ("dp", "seq"), axis=0, tiled=True),
    )
    feed_set = (
        lax.all_gather(gain_second, ("dp", "seq"), axis=0, tiled=True),
        lax.all_gather(gate_weight, ("dp", "seq"), axis=0, tiled=True),
        lax.all_gather(up_weight, ("dp", "seq"), axis=0, tiled=True),
        lax.all_gather(down_weight, ("dp", "seq"), axis=0, tiled=True),
    )
    gain_one, w_query, w_key, w_value, w_output = attend_set
    gain_two, w_gate, w_up, w_down = feed_set
    row_count = inputs.shape[0]
    group_size = HEADS // KV_HEADS
    kv_width = KV_HEADS * HEAD
    score_scale = 1.0 / math.sqrt(HEAD)
    query_rows = lax.axis_index("seq") * row_count + jnp.arange(row_count, dtype=jnp.int32)
    x_float = inputs.astype(f32)
    gain_one_float = gain_one.astype(f32)
    normed = normalize(x_float, gain_one_float).astype(bf16)
    query_rot = rotate(matrix_product(normed, w_query), positions, HEADS, 1.0).astype(bf16)
    key_rot = rotate(matrix_product(normed, w_key), positions, KV_HEADS, 1.0).astype(bf16)
    value_low = matrix_product(normed, w_value).astype(bf16)
    query_four = query_rot.reshape(row_count, KV_HEADS, group_size, HEAD)

    def mask_for(docs_part, first_key, piece_rows):
        key_rows = first_key + jnp.arange(piece_rows, dtype=jnp.int32)
        return (key_rows[None, :] <= query_rows[:, None]) & (docs_part[None, :] == doc_ids[:, None])

    def forward_step(state_in, pieces, first_key):
        keys_part, values_part, docs_part = pieces
        piece_rows = keys_part.shape[0]
        allowed = mask_for(docs_part, first_key, piece_rows)

        def forward_compute(state_now):
            accumulated, running, totals = state_now
            logits = (
                jnp.einsum(
                    "qgrd,kgd->grqk",
                    query_four,
                    keys_part.reshape(piece_rows, KV_HEADS, HEAD),
                    preferred_element_type=f32,
                )
                * score_scale
            )
            logits = jnp.where(allowed, logits, -1e30)
            new_max = jnp.maximum(running, jnp.max(logits, axis=-1))
            weights_block = jnp.where(allowed, jnp.exp(logits - new_max[..., None]), 0.0)
            factor = jnp.exp(running - new_max)
            totals = totals * factor + jnp.sum(weights_block, axis=-1)
            update = jnp.einsum(
                "grqk,kgd->qgrd",
                weights_block.astype(bf16),
                values_part.reshape(piece_rows, KV_HEADS, HEAD),
                preferred_element_type=f32,
            )
            accumulated = accumulated * jnp.transpose(factor, (2, 0, 1))[..., None] + update
            return (accumulated, new_max, totals)

        return lax.cond(jnp.any(allowed), forward_compute, keep_state, state_in)

    forward_init = (
        jnp.zeros((row_count, KV_HEADS, group_size, HEAD), f32),
        jnp.full((KV_HEADS, group_size, row_count), -1e30, f32),
        jnp.zeros((KV_HEADS, group_size, row_count), f32),
    )
    forward_state = piece_fold(
        forward_step,
        forward_init,
        (
            lax.all_gather(key_rot, "seq", axis=0, tiled=True),
            lax.all_gather(value_low, "seq", axis=0, tiled=True),
            lax.all_gather(doc_ids, "seq", axis=0, tiled=True),
        ),
    )
    accumulated, running, totals = forward_state
    attend_float = accumulated / jnp.transpose(totals, (2, 0, 1))[..., None]
    log_totals = running + jnp.log(totals)
    mixed = attend_float.reshape(row_count, D).astype(bf16)
    middle = x_float + matrix_product(mixed, w_output)
    gain_two_float = gain_two.astype(f32)
    normed_two = normalize(middle, gain_two_float).astype(bf16)
    gate = matrix_product(normed_two, w_gate)
    upward = matrix_product(normed_two, w_up)
    hidden = swish_product(gate, upward).astype(bf16)
    outputs = (middle + matrix_product(hidden, w_down)).astype(bf16)
    feed_back = (
        lax.all_gather(gain_second, ("dp", "seq"), axis=0, tiled=True),
        lax.all_gather(gate_weight, ("dp", "seq"), axis=0, tiled=True),
        lax.all_gather(up_weight, ("dp", "seq"), axis=0, tiled=True),
        lax.all_gather(down_weight, ("dp", "seq"), axis=0, tiled=True),
    )
    attend_back = (
        lax.all_gather(gain_first, ("dp", "seq"), axis=0, tiled=True),
        lax.all_gather(query_weight, ("dp", "seq"), axis=0, tiled=True),
        lax.all_gather(key_weight, ("dp", "seq"), axis=0, tiled=True),
        lax.all_gather(value_weight, ("dp", "seq"), axis=0, tiled=True),
        lax.all_gather(output_weight, ("dp", "seq"), axis=0, tiled=True),
    )
    unused_gain_two, back_gate, back_up, back_down = feed_back
    unused_gain_one, back_query, back_key, back_value, back_output = attend_back
    cot_float = cotangent.astype(f32)
    cot_low = cot_float.astype(bf16)
    down_term = transposed_times(hidden, cot_low)
    grad_hidden = times_transposed(cot_low, back_down)
    unused_swish, swish_back = jax.vjp(swish_product, gate, upward)
    grad_gate, grad_up = swish_back(grad_hidden)
    grad_gate_low = grad_gate.astype(bf16)
    grad_up_low = grad_up.astype(bf16)
    gate_term = transposed_times(normed_two, grad_gate_low)
    up_term = transposed_times(normed_two, grad_up_low)
    grad_normed_two = times_transposed(grad_gate_low, back_gate) + times_transposed(
        grad_up_low, back_up
    )
    unused_norm_two, norm_two_back = jax.vjp(normalize, middle, gain_two_float)
    grad_middle_part, gain_two_term = norm_two_back(grad_normed_two)
    second_grad, gate_grad, up_grad, down_grad = (
        lax.psum_scatter(gain_two_term, ("dp", "seq"), scatter_dimension=0, tiled=True),
        lax.psum_scatter(gate_term, ("dp", "seq"), scatter_dimension=0, tiled=True),
        lax.psum_scatter(up_term, ("dp", "seq"), scatter_dimension=0, tiled=True),
        lax.psum_scatter(down_term, ("dp", "seq"), scatter_dimension=0, tiled=True),
    )
    grad_middle = cot_float + grad_middle_part
    middle_low = grad_middle.astype(bf16)
    output_term = transposed_times(mixed, middle_low)
    grad_mixed = times_transposed(middle_low, back_output).astype(bf16)
    dout_four = grad_mixed.reshape(row_count, KV_HEADS, group_size, HEAD)
    delta_rows = jnp.einsum("qgrd,qgrd->grq", dout_four.astype(f32), attend_float)

    def query_grad_block(allowed, keys_three, values_three):
        logits = (
            jnp.einsum("qgrd,kgd->grqk", query_four, keys_three, preferred_element_type=f32)
            * score_scale
        )
        logits = jnp.where(allowed, logits, -1e30)
        weights_block = jnp.where(allowed, jnp.exp(logits - log_totals[..., None]), 0.0)
        grad_weights = jnp.einsum(
            "qgrd,kgd->grqk", dout_four, values_three, preferred_element_type=f32
        )
        grad_logits = (weights_block * (grad_weights - delta_rows[..., None]) * score_scale).astype(
            bf16
        )
        return (weights_block, grad_logits)

    def query_step(state_in, pieces, first_key):
        keys_part, values_part, docs_part = pieces
        piece_rows = keys_part.shape[0]
        allowed = mask_for(docs_part, first_key, piece_rows)

        def query_compute(grad_query):
            keys_three = keys_part.reshape(piece_rows, KV_HEADS, HEAD)
            values_three = values_part.reshape(piece_rows, KV_HEADS, HEAD)
            unused_weights, grad_logits = query_grad_block(allowed, keys_three, values_three)
            return grad_query + jnp.einsum(
                "grqk,kgd->qgrd", grad_logits, keys_three, preferred_element_type=f32
            )

        return lax.cond(jnp.any(allowed), query_compute, keep_state, state_in)

    grad_query_rot = piece_fold(
        query_step,
        jnp.zeros((row_count, KV_HEADS, group_size, HEAD), f32),
        (
            lax.all_gather(key_rot, "seq", axis=0, tiled=True),
            lax.all_gather(value_low, "seq", axis=0, tiled=True),
            lax.all_gather(doc_ids, "seq", axis=0, tiled=True),
        ),
    )
    lse_rows = jnp.transpose(log_totals, (2, 0, 1)).reshape(row_count, HEADS)
    delta_flat = jnp.transpose(delta_rows, (2, 0, 1)).reshape(row_count, HEADS)
    lse_all, delta_all = (
        lax.all_gather(lse_rows, "seq", axis=0, tiled=True),
        lax.all_gather(delta_flat, "seq", axis=0, tiled=True),
    )
    keys_mine = key_rot.reshape(row_count, KV_HEADS, HEAD)
    values_mine = value_low.reshape(row_count, KV_HEADS, HEAD)

    def key_step(state_in, pieces, first_query):
        queries_part, dout_part, docs_part = pieces
        piece_rows = queries_part.shape[0]
        other_rows = first_query + jnp.arange(piece_rows, dtype=jnp.int32)
        allowed = (query_rows[None, :] <= other_rows[:, None]) & (
            doc_ids[None, :] == docs_part[:, None]
        )

        def key_compute(state_now):
            grad_keys, grad_values = state_now
            lse_part = lax.dynamic_slice_in_dim(lse_all, first_query, piece_rows, 0)
            delta_part = lax.dynamic_slice_in_dim(delta_all, first_query, piece_rows, 0)
            lse_three = jnp.transpose(lse_part.reshape(piece_rows, KV_HEADS, group_size), (1, 2, 0))
            delta_three = jnp.transpose(
                delta_part.reshape(piece_rows, KV_HEADS, group_size), (1, 2, 0)
            )
            queries_four = queries_part.reshape(piece_rows, KV_HEADS, group_size, HEAD)
            douts_four = dout_part.reshape(piece_rows, KV_HEADS, group_size, HEAD)
            logits = (
                jnp.einsum("qgrd,kgd->grqk", queries_four, keys_mine, preferred_element_type=f32)
                * score_scale
            )
            logits = jnp.where(allowed, logits, -1e30)
            weights_block = jnp.where(allowed, jnp.exp(logits - lse_three[..., None]), 0.0)
            grad_weights = jnp.einsum(
                "qgrd,kgd->grqk", douts_four, values_mine, preferred_element_type=f32
            )
            grad_logits = (
                weights_block * (grad_weights - delta_three[..., None]) * score_scale
            ).astype(bf16)
            grad_keys = grad_keys + jnp.einsum(
                "grqk,qgrd->kgd", grad_logits, queries_four, preferred_element_type=f32
            )
            grad_values = grad_values + jnp.einsum(
                "grqk,qgrd->kgd", weights_block.astype(bf16), douts_four, preferred_element_type=f32
            )
            return (grad_keys, grad_values)

        return lax.cond(jnp.any(allowed), key_compute, keep_state, state_in)

    key_init = (
        jnp.zeros((row_count, KV_HEADS, HEAD), f32),
        jnp.zeros((row_count, KV_HEADS, HEAD), f32),
    )
    grad_keys_three, grad_values_three = piece_fold(
        key_step,
        key_init,
        (
            lax.all_gather(query_rot, "seq", axis=0, tiled=True),
            lax.all_gather(grad_mixed, "seq", axis=0, tiled=True),
            lax.all_gather(doc_ids, "seq", axis=0, tiled=True),
        ),
    )
    grad_keys_mine = grad_keys_three.reshape(row_count, kv_width)
    grad_values_mine = grad_values_three.reshape(row_count, kv_width)
    grad_query_low = rotate(grad_query_rot.reshape(row_count, D), positions, HEADS, -1.0).astype(
        bf16
    )
    grad_key_low = rotate(grad_keys_mine, positions, KV_HEADS, -1.0).astype(bf16)
    grad_value_low = grad_values_mine.astype(bf16)
    query_term = transposed_times(normed, grad_query_low)
    key_term_all = transposed_times(normed, grad_key_low)
    value_term_all = transposed_times(normed, grad_value_low)
    grad_normed = (
        times_transposed(grad_query_low, back_query)
        + times_transposed(grad_key_low, back_key)
        + times_transposed(grad_value_low, back_value)
    )
    unused_norm_one, norm_one_back = jax.vjp(normalize, x_float, gain_one_float)
    grad_input_part, gain_one_term = norm_one_back(grad_normed)
    inputs_grad = (grad_middle + grad_input_part).astype(bf16)
    first_grad, query_grad, key_grad, value_grad, output_grad = (
        lax.psum_scatter(gain_one_term, ("dp", "seq"), scatter_dimension=0, tiled=True),
        lax.psum_scatter(query_term, ("dp", "seq"), scatter_dimension=0, tiled=True),
        lax.psum_scatter(key_term_all, ("dp", "seq"), scatter_dimension=0, tiled=True),
        lax.psum_scatter(value_term_all, ("dp", "seq"), scatter_dimension=0, tiled=True),
        lax.psum_scatter(output_term, ("dp", "seq"), scatter_dimension=0, tiled=True),
    )
    return (
        outputs,
        inputs_grad,
        first_grad,
        query_grad,
        key_grad,
        value_grad,
        output_grad,
        second_grad,
        gate_grad,
        up_grad,
        down_grad,
    )


def solution(mesh):
    placed = (
        P(("dp", "seq"), None),
        P(("dp", "seq"), None),
        P(("dp", "seq")),
        P(("dp", "seq")),
        P(("dp", "seq")),
        P(("dp", "seq"), None),
        P(("dp", "seq"), None),
        P(("dp", "seq"), None),
        P(("dp", "seq"), None),
        P(("dp", "seq")),
        P(("dp", "seq"), None),
        P(("dp", "seq"), None),
        P(("dp", "seq"), None),
    )
    return jax.shard_map(
        body,
        mesh=mesh,
        in_specs=placed,
        out_specs=(
            P(("dp", "seq"), None),
            P(("dp", "seq"), None),
            P(("dp", "seq")),
            P(("dp", "seq"), None),
            P(("dp", "seq"), None),
            P(("dp", "seq"), None),
            P(("dp", "seq"), None),
            P(("dp", "seq")),
            P(("dp", "seq"), None),
            P(("dp", "seq"), None),
            P(("dp", "seq"), None),
        ),
        check_vma=False,
    )
```

profile of v0, /device:TPU:0, one launch (start us, length us, event | category | flops | bytes accessed | tf_op | source)
XLA Modules:
  0.0 1989.3 jit_solution(11250035465387944066)
XLA Ops:
  11.2 42.1 %all-reduce.5 = (bf16[1536]{0:T(1024)(128)(2,1)S(1)}, bf16[1536]{0:T(1024)(128)(2,1)S(1)}) all-reduce(bf16[1536]{0:T(1024)(128)(2,1)S(1)} %dynamic-update-slice, bf16[1536]{0:T(1024)(128)(2,1)S(1)} %dynamic-update-slice.1), channel_id=1, replica_groups=mesh['dp'=4,'seq'=8] {'dp','seq'}, use_global_device_ids=true, to_apply=%add | all-reduce | flops 3072 | bytes 12288
  55.9 15.3 all-gather.13.cloned.1.call-done
  75.0 55.6 %all-gather.19.cloned.1.call-done = bf16[1536,768]{1,0:T(8,128)(2,1)} async-done(((bf16[48,768]{1,0:T(8,128)(2,1)}), bf16[1536,768]{1,0:T(8,128)(2,1)}) %all-gather.19.cloned.1.call-update) | async-done | bytes 2359312 | tf_op jit(solution)/shard_map/all_gather | solution.py:115
  130.6 3.0 convolution_convert_fusion.1
  136.5 10.5 all-gather
  150.2 46.0 %all-gather.17.cloned.1.call-done = bf16[1536,1536]{1,0:T(8,128)(2,1)} async-done(((bf16[48,1536]{1,0:T(8,128)(2,1)}), bf16[1536,1536]{1,0:T(8,128)(2,1)}) %all-gather.17.cloned.1.call-update) | async-done | bytes 4718608 | tf_op jit(solution)/shard_map/all_gather | solution.py:113
  196.2 4.3 fusion.103
  201.4 22.8 %all-gather.15.cloned.1.call-done = bf16[1024,768]{0,1:T(8,128)(2,1)} async-done(((bf16[128,768]{0,1:T(8,128)(2,1)}), bf16[1024,768]{0,1:T(8,128)(2,1)}) %all-gather.15.cloned.1.call-update) | async-done | bytes 1572880 | tf_op jit(solution)/shard_map/all_gather | solution.py:184
  224.2 26.3 %all-gather.21.cloned.1.call-done = bf16[1024,768]{1,0:T(8,128)(2,1)} async-done(((bf16[128,768]{1,0:T(8,128)(2,1)}), bf16[1024,768]{1,0:T(8,128)(2,1)}) %all-gather.21.cloned.1.call-update) | async-done | bytes 1572880 | tf_op jit(solution)/shard_map/all_gather | solution.py:185
  250.5 10.9 conditional.3
  252.2 3.1 fusion.35
  255.3 3.2 fusion.44
  261.5 55.1 %all-gather.23.cloned.1.call-done = bf16[1536,1536]{1,0:T(8,128)(2,1)} async-done(((bf16[48,1536]{1,0:T(8,128)(2,1)}), bf16[1536,1536]{1,0:T(8,128)(2,1)}) %all-gather.23.cloned.1.call-update) | async-done | bytes 4718608 | tf_op jit(solution)/shard_map/all_gather | solution.py:116
  316.6 3.2 multiply_reduce_fusion.2
  320.4 94.1 %all-gather.25.cloned.1.call-done = bf16[1536,4096]{1,0:T(8,128)(2,1)} async-done(((bf16[48,4096]{1,0:T(8,128)(2,1)}), bf16[1536,4096]{1,0:T(8,128)(2,1)}) %all-gather.25.cloned.1.call-update) | async-done | bytes 12582928 | tf_op jit(solution)/shard_map/all_gather | solution.py:120
  414.6 7.7 fusion.110
  422.3 89.6 %all-gather.27.cloned.1.call-done = bf16[1536,4096]{1,0:T(8,128)(2,1)} async-done(((bf16[48,4096]{1,0:T(8,128)(2,1)}), bf16[1536,4096]{1,0:T(8,128)(2,1)}) %all-gather.27.cloned.1.call-update) | async-done | bytes 12582928 | tf_op jit(solution)/shard_map/all_gather | solution.py:121
  511.9 7.7 fusion.111
  519.6 89.6 %all-gather.29.cloned.1.call-done = bf16[4096,1536]{1,0:T(8,128)(2,1)} async-done(((bf16[128,1536]{1,0:T(8,128)(2,1)}), bf16[4096,1536]{1,0:T(8,128)(2,1)}) %all-gather.29.cloned.1.call-update) | async-done | bytes 12582928 | tf_op jit(solution)/shard_map/all_gather | solution.py:122
  609.3 11.7 multiply_convert_fusion
  621.0 10.2 fusion.112
  631.2 7.4 multiply_reduce_fusion
  640.2 4.8 convolution_convert_fusion
  647.2 14.0 all_gather.72
  663.8 14.2 all_gather.74
  678.0 10.0 all-gather.33.cloned.1.call-done
  688.1 31.7 %conditional.5 = (f32[128,8,96]{0,2,1:T(8,128)S(1)}, f32[128,8,96]{0,2,1:T(8,128)}) conditional(s32[]{:T(128)} %convert_element_type.150, f32[128,8,96]{0,2,1:T(8,128)S(1)} %broadcast.182, (pred[1024,128]{0,1:T(8,128)(4,1)}, bf16[1024,1536]{0,1:T(8,128)(2,1)}, bf16[128,8,96]{0,2,1:T(8,128)(2,1)S(1)}, f32[1024,16]{0,1:T(8,128)S(1)}, ...), branch_computations={%region_11.12_spmd, %region_12.13_spmd} | conditional | flops 1638072320 | bytes 48169032 | solution.py:329
  688.1 4.7 copy.58
  692.8 6.4 fusion.27
  699.9 7.7 fusion.21
  709.1 10.4 fusion.24
  727.8 19.5 conditional.4
  727.8 6.0 fusion.109
  736.4 9.6 fusion.65
  747.4 5.2 fusion.100
  752.7 4.9 fusion.89
  757.9 11.4 fusion.114
  769.3 11.4 fusion.115
  781.7 11.6 fusion.116
  793.4 4.0 fusion.113
  797.4 7.6 fusion.71
  807.0 39.8 %all-reduce.4 = (f32[1536]{0:T(1024)S(1)}, f32[1536]{0:T(1024)S(1)}) all-reduce(f32[1536]{0:T(1024)S(1)} %get-tuple-element.465, f32[1536]{0:T(1024)S(1)} %copy-done.14), channel_id=2, replica_groups=mesh['dp'=4,'seq'=8] {'dp','seq'}, use_global_device_ids=true, to_apply=%region_15.16.clone | all-reduce | flops 3072 | bytes 24576
  849.0 93.7 %reduce-scatter.12.cloned.1.call-done = f32[48,768]{1,0:T(8,128)} async-done(((f32[1536,768]{1,0:T(8,128)}), f32[48,768]{1,0:T(8,128)}) %reduce-scatter.12.cloned.1.call-update) | async-done | bytes 147472 | tf_op jit(solution)/shard_map/reduce_scatter | solution.py:366
  942.8 141.1 %reduce-scatter.8.cloned.1.call-done = f32[48,1536]{1,0:T(8,128)} async-done(((f32[1536,1536]{1,0:T(8,128)}), f32[48,1536]{1,0:T(8,128)}) %reduce-scatter.8.cloned.1.call-update) | async-done | bytes 294928 | tf_op jit(solution)/shard_map/reduce_scatter | solution.py:364
  1083.9 142.0 %reduce-scatter.14.cloned.1.call-done = f32[48,1536]{1,0:T(8,128)} async-done(((f32[1536,1536]{1,0:T(8,128)}), f32[48,1536]{1,0:T(8,128)}) %reduce-scatter.14.cloned.1.call-update) | async-done | bytes 294928 | tf_op jit(solution)/shard_map/reduce_scatter | solution.py:367
  1225.8 251.3 %reduce-scatter.16.cloned.1.call-done = f32[48,4096]{1,0:T(8,128)} async-done(((f32[1536,4096]{1,0:T(8,128)}), f32[48,4096]{1,0:T(8,128)}) %reduce-scatter.16.cloned.1.call-update) | async-done | bytes 786448 | tf_op jit(solution)/shard_map/reduce_scatter | solution.py:232
  1477.1 253.0 %reduce-scatter.18.cloned.1.call-done = f32[48,4096]{1,0:T(8,128)} async-done(((f32[1536,4096]{1,0:T(8,128)}), f32[48,4096]{1,0:T(8,128)}) %reduce-scatter.18.cloned.1.call-update) | async-done | bytes 786448 | tf_op jit(solution)/shard_map/reduce_scatter | solution.py:233
  1730.1 251.9 %reduce-scatter.20.cloned.1.call-done = f32[128,1536]{1,0:T(8,128)} async-done(((f32[4096,1536]{1,0:T(8,128)}), f32[128,1536]{1,0:T(8,128)}) %reduce-scatter.20.cloned.1.call-update) | async-done | bytes 786448 | tf_op jit(solution)/shard_map/reduce_scatter | solution.py:234
  (132 shorter events, 46.9 us)
Async XLA Ops:
  7.2 189.0 %copy-start.1 = (bf16[128,1536]{1,0:T(8,128)(2,1)S(1)}, bf16[128,1536]{1,0:T(8,128)(2,1)}, u32[]{:S(2)}) copy-start(bf16[128,1536]{1,0:T(8,128)(2,1)} %param.19) | copy-start | bytes 1179652
  7.2 129.3 %copy-start.17 = (s32[128]{0:T(128)S(1)}, s32[128]{0:T(128)}, u32[]{:S(2)}) copy-start(s32[128]{0:T(128)} %param.21) | copy-start | bytes 1540
  7.2 64.1 %all-gather.13.cloned.1.call-start = ((), (), s32[]{:S(2)}) async-start(), calls=%async_computation.7 | async-start | bytes 2433024 | tf_op jit(solution)/shard_map/all_gather | solution.py:114
  7.9 122.7 %all-gather.19.cloned.1.call-start = ((), (), s32[]{:S(2)}) async-start(), calls=%async_computation.10 | async-start | bytes 2433024 | tf_op jit(solution)/shard_map/all_gather | solution.py:115
  8.7 187.5 %all-gather.17.cloned.1.call-start = ((), (), s32[]{:S(2)}) async-start(), calls=%async_computation.9 | async-start | bytes 4866048 | tf_op jit(solution)/shard_map/all_gather | solution.py:113
  9.4 214.8 %all-gather.15.cloned.1.call-start = ((), (), s32[]{:S(2)}) async-start(), calls=%async_computation.8 | async-start | bytes 1769472 | tf_op jit(solution)/shard_map/all_gather | solution.py:184
  55.1 81.3 %copy-start.18 = (f32[128]{0:T(128)}, f32[128]{0:T(128)S(1)}, u32[]{:S(2)}) copy-start(f32[128]{0:T(128)S(1)} %fusion.83) | copy-start | bytes 1540
  74.9 175.6 %all-gather.21.cloned.1.call-start = ((), (), s32[]{:S(2)}) async-start(), calls=%async_computation.11 | async-start | bytes 1769472 | tf_op jit(solution)/shard_map/all_gather | solution.py:185
  133.6 183.0 %all-gather.23.cloned.1.call-start = ((), (), s32[]{:S(2)}) async-start(), calls=%async_computation.12 | async-start | bytes 4866048 | tf_op jit(solution)/shard_map/all_gather | solution.py:116
  134.2 280.4 %all-gather.25.cloned.1.call-start = ((), (), s32[]{:S(2)}) async-start(), calls=%async_computation.13 | async-start | bytes 12976128 | tf_op jit(solution)/shard_map/all_gather | solution.py:120
  134.9 377.0 %all-gather.27.cloned.1.call-start = ((), (), s32[]{:S(2)}) async-start(), calls=%async_computation.14 | async-start | bytes 12976128 | tf_op jit(solution)/shard_map/all_gather | solution.py:121
  135.7 473.6 %all-gather.29.cloned.1.call-start = ((), (), s32[]{:S(2)}) async-start(), calls=%async_computation.15 | async-start | bytes 12976128 | tf_op jit(solution)/shard_map/all_gather | solution.py:122
  136.4 541.6 %all-gather.31.cloned.1.call-start = ((), (), s32[]{:S(2)}) async-start(), calls=%async_computation.16 | async-start | bytes 3538944 | tf_op jit(solution)/shard_map/all_gather | solution.py:339
  261.4 160.9 %copy-start.4 = (f32[128,8,2,96]{0,3,2,1:T(8,128)}, f32[128,8,2,96]{0,3,2,1:T(8,128)S(1)}, u32[]{:S(2)}) copy-start(f32[128,8,2,96]{0,3,2,1:T(8,128)S(1)} %get-tuple-element.446) | copy-start | bytes 2359300
  319.9 368.1 %all-gather.33.cloned.1.call-start = ((), (), s32[]{:S(2)}) async-start(), calls=%async_computation.17 | async-start | bytes 3538944 | tf_op jit(solution)/shard_map/all_gather | solution.py:340
  422.3 187.0 %copy-start.10 = (bf16[128,1536]{1,0:T(8,128)(2,1)S(1)}, bf16[128,1536]{1,0:T(8,128)(2,1)}, u32[]{:S(2)}) copy-start(bf16[128,1536]{1,0:T(8,128)(2,1)} %param.20) | copy-start | bytes 1179652
  621.0 10.2 copy-start
  638.6 49.4 %copy-start.5 = (bf16[128,8,96]{0,2,1:T(8,128)(2,1)S(1)}, bf16[128,8,96]{0,2,1:T(8,128)(2,1)}, u32[]{:S(2)}) copy-start(bf16[128,8,96]{0,2,1:T(8,128)(2,1)} %maximum_convert_fusion.1) | copy-start | bytes 589828
  645.0 204.1 %reduce-scatter.10.cloned.1.call-start = ((), (), s32[]{:S(2)}) async-start(), calls=%async_computation.19 | async-start | bytes 4866048 | tf_op jit(solution)/shard_map/reduce_scatter | solution.py:365
  647.2 16.6 copy-start.15
  662.4 25.7 %copy-start.9 = (bf16[128,1536]{0,1:T(8,128)(2,1)}, bf16[128,1536]{0,1:T(8,128)(2,1)S(1)}, u32[]{:S(2)}) copy-start(bf16[128,1536]{0,1:T(8,128)(2,1)S(1)} %copy.55) | copy-start | bytes 1179652
  699.9 8.4 copy-start.8
  699.9 9.2 copy-start.13
  723.6 4.2 copy-start.16
  723.6 219.2 %reduce-scatter.12.cloned.1.call-start = ((), (), s32[]{:S(2)}) async-start(), calls=%async_computation.20 | async-start | bytes 4866048 | tf_op jit(solution)/shard_map/reduce_scatter | solution.py:366
  724.7 3.1 copy-start.6
  727.7 356.2 %reduce-scatter.8.cloned.1.call-start = ((), (), s32[]{:S(2)}) async-start(), calls=%async_computation.18 | async-start | bytes 9732096 | tf_op jit(solution)/shard_map/reduce_scatter | solution.py:364
  727.8 19.5 copy-start.12
  752.6 473.2 %reduce-scatter.14.cloned.1.call-start = ((), (), s32[]{:S(2)}) async-start(), calls=%async_computation.21 | async-start | bytes 9732096 | tf_op jit(solution)/shard_map/reduce_scatter | solution.py:367
  757.6 719.5 %reduce-scatter.16.cloned.1.call-start = ((), (), s32[]{:S(2)}) async-start(), calls=%async_computation.22 | async-start | bytes 25952256 | tf_op jit(solution)/shard_map/reduce_scatter | solution.py:232
  769.3 960.8 %reduce-scatter.18.cloned.1.call-start = ((), (), s32[]{:S(2)}) async-start(), calls=%async_computation.23 | async-start | bytes 25952256 | tf_op jit(solution)/shard_map/reduce_scatter | solution.py:233
  780.7 1.0 copy-start.11
  780.7 1201.3 %reduce-scatter.20.cloned.1.call-start = ((), (), s32[]{:S(2)}) async-start(), calls=%async_computation.24 | async-start | bytes 25952256 | tf_op jit(solution)/shard_map/reduce_scatter | solution.py:234
  797.4 7.6 copy-start.3
  797.4 8.5 copy-start.2
  797.4 8.5 copy-start.7
  805.0 2.0 copy-start.14
  805.0 43.0 %copy-start.19 = (f32[128]{0:T(128)S(1)}, f32[128]{0:T(128)}, u32[]{:S(2)}) copy-start(f32[128]{0:T(128)} %copy-done.18) | copy-start | bytes 1540
Sparse Core Ops, SparseCore 0:
  11.1 60.1 all-gather.12
  74.3 56.2 all-gather.18
  133.6 62.5 all-gather.16
  198.2 25.9 all-gather.14
  226.3 24.1 all-gather.20
  253.4 63.1 all-gather.22
  319.6 94.8 all-gather.24
  417.6 94.3 all-gather.26
  514.9 94.3 all-gather.28
  611.3 37.4 all-gather.30
  651.0 37.0 all-gather.32
  723.7 105.9 reduce-scatter.9
  836.6 106.1 reduce-scatter.11
  949.1 134.7 reduce-scatter.7
  1091.2 134.6 reduce-scatter.13
  1232.7 244.3 reduce-scatter.15
  1485.1 245.0 reduce-scatter.17
  1737.0 244.9 reduce-scatter.19
where the time goes:
time: 2000 us; the launch traced here: 1990 us
  waiting for transfers between devices  1640 us (82%)
  matrix products  173 us (9%)
  blocking collectives  121 us (6%)
    reduce_scatter x1, waiting for transfers between devices, body(): lax.psum_scatter(up_term, ('dp', 'seq'), scatter_dimension=0, tiled=True)  253 us
    reduce_scatter x1, waiting for transfers between devices, body(): lax.psum_scatter(down_term, ('dp', 'seq'), scatter_dimension=0, tiled=True)  252 us
    reduce_scatter x1, waiting for transfers between devices, body(): lax.psum_scatter(gate_term, ('dp', 'seq'), scatter_dimension=0, tiled=True)  251 us
    reduce_scatter x1, waiting for transfers between devices, body(): lax.psum_scatter(output_term, ('dp', 'seq'), scatter_dimension=0, tiled=T...  142 us
    reduce_scatter x1, waiting for transfers between devices, body(): lax.psum_scatter(query_term, ('dp', 'seq'), scatter_dimension=0, tiled=True)  141 us
    all_gather x1, waiting for transfers between devices, body(): lax.all_gather(gate_weight, ('dp', 'seq'), axis=0, tiled=True)  94.1 us
    reduce_scatter x1, waiting for transfers between devices, body(): lax.psum_scatter(value_term_all, ('dp', 'seq'), scatter_dimension=0, tile...  93.7 us
    all_gather x1, waiting for transfers between devices, body(): lax.all_gather(up_weight, ('dp', 'seq'), axis=0, tiled=True)  89.6 us
  transfers between devices with their start and end apart: 18, of which 16 were waited for; matrix products, arithmetic and copies ran while one was open for 9% of the time, Pallas kernels for 0%

commit v1 on v0

--- a/solution.py
+++ b/solution.py
@@ -3,6 +3,8 @@
 import jax
 import jax.numpy as jnp
 from jax import lax
+from jax.experimental import pallas as pl
+from jax.experimental.pallas import tpu as pltpu
 from jax.sharding import PartitionSpec as P
 
 D = 1536
@@ -380,6 +382,469 @@
         down_grad,
     )
 
+BOTH = ("dp", "seq")
+BIT_Y, BIT_X, BIT_ZH, BIT_ZL, BIT_C = 16, 8, 4, 2, 1
+PAIR = 2
+LANES = 128
+QUERY_COLS = PAIR * HEAD
+HEAD_COLS = QUERY_COLS + 2 * HEAD
+PAD_COLS = (PAIR + 2) * LANES
+BLOCK = 256
+f32 = jnp.float32
+bf16 = jnp.bfloat16
+VMEM_BYTES = 60 * 1024 * 1024
+
+
+def swap(value, bit):
+    return lax.ppermute(value, BOTH, [(i, i ^ bit) for i in range(32)])
+
+
+def my_bit(bit):
+    flat = lax.axis_index("dp") * 8 + lax.axis_index("seq")
+    return (flat // bit) % 2
+
+
+def pick(value, index, axis):
+    return lax.dynamic_index_in_dim(value, index, axis, keepdims=False)
+
+
+def paired(mine, other, bit, axis):
+    low_first = my_bit(bit) == 0
+    return jnp.stack(
+        [jnp.where(low_first, mine, other), jnp.where(low_first, other, mine)], axis
+    )
+
+
+def gather_bit(value, bit, axis):
+    return paired(value, swap(value, bit), bit, axis)
+
+
+def trade_bit(value, bit, axis):
+    mine = my_bit(bit)
+    keep = pick(value, mine, axis)
+    other = swap(pick(value, 1 - mine, axis), bit)
+    return paired(keep, other, bit, axis)
+
+
+def reduce_bit(value, bit, axis):
+    mine = my_bit(bit)
+    keep = pick(value, mine, axis)
+    other = swap(pick(value, 1 - mine, axis).astype(bf16), bit)
+    return keep.astype(f32) + other.astype(f32)
+
+
+def gather_square(value):
+    half = value.shape[0] // 2
+    from_x = swap(value, BIT_X)
+    from_z = swap(value, BIT_ZL)
+    far_low = swap(from_z[:half], BIT_X)
+    far_high = swap(from_x[half:], BIT_ZL)
+    chip = jnp.concatenate([value, from_x, from_z, far_low, far_high])
+    return jnp.concatenate([chip, swap(chip, BIT_C)])
+
+
+def scatter_square(parts):
+    rows = parts.shape[0] // 8
+    half = rows // 2
+    mine = parts[: 4 * rows].astype(f32) + swap(parts[4 * rows :], BIT_C).astype(f32)
+    own, to_x, to_z, far = (mine[i * rows : (i + 1) * rows] for i in range(4))
+    far = far.astype(bf16)
+    in_z = swap(far[:half], BIT_X).astype(f32)
+    in_x = swap(far[half:], BIT_ZL).astype(f32)
+    to_z = jnp.concatenate([to_z[:half] + in_z, to_z[half:]]).astype(bf16)
+    to_x = jnp.concatenate([to_x[:half], to_x[half:] + in_x]).astype(bf16)
+    return own + swap(to_x, BIT_X).astype(f32) + swap(to_z, BIT_ZL).astype(f32)
+
+
+def across(value):
+    pairs = []
+    for i in range(32):
+        y, x, zh, zl, c = (i >> 4) & 1, (i >> 3) & 1, (i >> 2) & 1, (i >> 1) & 1, i & 1
+        pairs.append((i, c * 16 + zl * 8 + zh * 4 + x * 2 + y))
+    return lax.ppermute(value, BOTH, pairs)
+
+
+def gather_rows(value):
+    return lax.all_gather(value, "seq", axis=0, tiled=True)
+
+
+def scatter_rows(value):
+    return lax.psum_scatter(value, "seq", scatter_dimension=0, tiled=True)
+
+
+GROUP_OF = [((s & 1) << 2) | (s & 2) | (s >> 2) for s in range(8)]
+
+
+def dot_nn(left, right):
+    return jnp.dot(left, right, preferred_element_type=f32)
+
+
+def dot_nt(left, right):
+    return lax.dot_general(left, right, (((1,), (1,)), ((), ())), preferred_element_type=f32)
+
+
+def dot_tn(left, right):
+    return lax.dot_general(left, right, (((0,), (0,)), ((), ())), preferred_element_type=f32)
+
+
+def whole(*shape):
+    return pl.BlockSpec(shape, lambda i: (0,) * len(shape), pipeline_mode=pl.Buffered(1))
+
+
+def rows_of(rows, cols):
+    return pl.BlockSpec((rows, cols), lambda i: (i, 0))
+
+
+def turn(matrix, cosine, sine):
+    return matrix * cosine + pltpu.roll(matrix, LANES // 2, 1) * sine
+
+
+def project_kernel(x_ref, w_ref, freq_ref, hn_ref, q_ref, k_ref, v_ref, cos_ref, sin_ref):
+    x = x_ref[:, :D].astype(f32)
+    scale = lax.rsqrt(jnp.mean(x * x, axis=-1, keepdims=True) + norm_epsilon)
+    normed = (x * scale).astype(bf16)
+    hn_ref[...] = normed
+    extra = x_ref[:, D:].astype(f32)
+    place = extra[:, 1:2] * 128.0 + extra[:, 2:3]
+    angles = place * freq_ref[...]
+    lane = lax.broadcasted_iota(jnp.int32, angles.shape, 1)
+    cosine = jnp.cos(angles)
+    sine = jnp.where(lane < LANES // 2, -jnp.sin(angles), jnp.sin(angles))
+    cos_ref[...] = cosine
+    sin_ref[...] = sine
+    full = dot_nn(normed, w_ref[...])
+    for h in range(PAIR):
+        part = full[:, h * LANES : (h + 1) * LANES]
+        q_ref[:, h * LANES : (h + 1) * LANES] = turn(part, cosine, sine).astype(bf16)
+    k_ref[...] = turn(full[:, PAIR * LANES : (PAIR + 1) * LANES], cosine, sine).astype(bf16)
+    v_ref[...] = full[:, (PAIR + 1) * LANES :].astype(bf16)
+
+
+def project(rows_all, weights):
+    total, width = rows_all.shape
+    lane = jnp.arange(LANES) % (LANES // 2)
+    freq = rotary_base ** (-lane.astype(f32) * 2.0 / HEAD)
+    freq = jnp.where(lane < HEAD // 2, freq, 0.0).reshape(1, LANES)
+    shapes = [(D, bf16), (PAIR * LANES, bf16), (LANES, bf16), (LANES, bf16), (LANES, f32), (LANES, f32)]
+    return pl.pallas_call(
+        project_kernel,
+        grid=(total // BLOCK,),
+        in_specs=[rows_of(BLOCK, width), whole(D, PAD_COLS), whole(1, LANES)],
+        out_specs=[rows_of(BLOCK, n) for n, t in shapes],
+        out_shape=[jax.ShapeDtypeStruct((total, n), t) for n, t in shapes],
+        compiler_params=pltpu.CompilerParams(vmem_limit_bytes=VMEM_BYTES),
+        name="project",
+    )(rows_all, weights, freq)
+
+
+def allowed_pairs(dcol_ref, drow_ref, first, keys):
+    shape = (BLOCK, keys)
+    query_at = first + lax.broadcasted_iota(jnp.int32, shape, 0)
+    key_at = lax.broadcasted_iota(jnp.int32, shape, 1)
+    return (key_at <= query_at) & (dcol_ref[...] == drow_ref[:, :keys])
+
+
+def attend_kernel(q_ref, k_ref, v_ref, dcol_ref, drow_ref, w_ref, a_ref, lse_ref, o_ref):
+    blocks = k_ref.shape[0] // BLOCK
+
+    def run(b):
+        keys = (b + 1) * BLOCK
+        allowed = allowed_pairs(dcol_ref, drow_ref, b * BLOCK, keys)
+        for h in range(PAIR):
+            cols = slice(h * LANES, (h + 1) * LANES)
+            logits = dot_nt(q_ref[:, cols], k_ref[:keys, :]) * (1.0 / math.sqrt(HEAD))
+            logits = jnp.where(allowed, logits, -1e30)
+            top = jnp.max(logits, axis=-1, keepdims=True)
+            weights = jnp.exp(logits - top)
+            total = jnp.sum(weights, axis=-1, keepdims=True)
+            mixed = dot_nn(weights.astype(bf16), v_ref[:keys, :]) / total
+            a_ref[:, cols] = mixed.astype(bf16)
+            lse_ref[:, h : h + 1] = top + jnp.log(total)
+
+    for b in range(blocks):
+        pl.when(pl.program_id(0) == b)(lambda b=b: run(b))
+    o_ref[...] = dot_nn(a_ref[...], w_ref[...]).astype(bf16)
+
+
+def attend(query, key, value, docs_col, docs_row, weights):
+    total = query.shape[0]
+    shapes = [(PAIR * LANES, bf16), (PAIR, f32), (D, bf16)]
+    return pl.pallas_call(
+        attend_kernel,
+        grid=(total // BLOCK,),
+        in_specs=[
+            rows_of(BLOCK, PAIR * LANES),
+            whole(total, LANES),
+            whole(total, LANES),
+            rows_of(BLOCK, 1),
+            whole(1, total),
+            whole(PAIR * LANES, D),
+        ],
+        out_specs=[rows_of(BLOCK, n) for n, t in shapes],
+        out_shape=[jax.ShapeDtypeStruct((total, n), t) for n, t in shapes],
+        compiler_params=pltpu.CompilerParams(vmem_limit_bytes=VMEM_BYTES),
+        name="attend",
+    )(query, key, value, docs_col, docs_row, weights)
+
+
+def attend_back_kernel(
+    mb_ref, w_ref, q_ref, k_ref, v_ref, a_ref, lse_ref, dcol_ref, drow_ref, cos_ref, sin_ref,
+    dq_ref, dkv_ref, dk_acc, dv_acc, dq_acc
+):
+    step = pl.program_id(0)
+    blocks = k_ref.shape[0] // BLOCK
+
+    @pl.when(step == 0)
+    def _():
+        dk_acc[...] = jnp.zeros_like(dk_acc)
+        dv_acc[...] = jnp.zeros_like(dv_acc)
+
+    grad_mixed = dot_nt(mb_ref[...], w_ref[...]).astype(bf16)
+    scale = 1.0 / math.sqrt(HEAD)
+
+    def run(b):
+        keys = (b + 1) * BLOCK
+        allowed = allowed_pairs(dcol_ref, drow_ref, b * BLOCK, keys)
+        for h in range(PAIR):
+            cols = slice(h * LANES, (h + 1) * LANES)
+            query = q_ref[:, cols]
+            grad = grad_mixed[:, cols]
+            delta = jnp.sum(
+                grad.astype(f32) * a_ref[:, cols].astype(f32), axis=-1, keepdims=True
+            )
+            logits = dot_nt(query, k_ref[:keys, :]) * scale
+            logits = jnp.where(allowed, logits, -1e30)
+            weights = jnp.exp(logits - lse_ref[:, h : h + 1])
+            grad_weights = dot_nt(grad, v_ref[:keys, :])
+            grad_logits = (weights * (grad_weights - delta) * scale).astype(bf16)
+            dq_acc[:, cols] = dot_nn(grad_logits, k_ref[:keys, :])
+            dk_acc[:keys, :] += dot_tn(grad_logits, query)
+            dv_acc[:keys, :] += dot_tn(weights.astype(bf16), grad)
+
+    for b in range(blocks):
+        pl.when(step == b)(lambda b=b: run(b))
+
+    rows = pl.ds(pl.multiple_of(step * BLOCK, BLOCK), BLOCK)
+    for h in range(PAIR):
+        cols = slice(h * LANES, (h + 1) * LANES)
+        dq_ref[:, cols] = turn(dq_acc[:, cols], cos_ref[rows, :], -sin_ref[rows, :]).astype(bf16)
+
+    @pl.when(step == blocks - 1)
+    def _():
+        dkv_ref[:, :LANES] = turn(dk_acc[...], cos_ref[...], -sin_ref[...]).astype(bf16)
+        dkv_ref[:, LANES:] = dv_acc[...].astype(bf16)
+
+
+def attend_back(mb, weights, query, key, value, mixed, lse, docs_col, docs_row, cosine, sine):
+    total = query.shape[0]
+    return pl.pallas_call(
+        attend_back_kernel,
+        grid=(total // BLOCK,),
+        in_specs=[
+            rows_of(BLOCK, D),
+            whole(PAIR * LANES, D),
+            rows_of(BLOCK, PAIR * LANES),
+            whole(total, LANES),
+            whole(total, LANES),
+            rows_of(BLOCK, PAIR * LANES),
+            rows_of(BLOCK, PAIR),
+            rows_of(BLOCK, 1),
+            whole(1, total),
+            whole(total, LANES),
+            whole(total, LANES),
+        ],
+        out_specs=[rows_of(BLOCK, PAIR * LANES), whole(total, 2 * LANES)],
+        out_shape=[
+            jax.ShapeDtypeStruct((total, PAIR * LANES), bf16),
+            jax.ShapeDtypeStruct((total, 2 * LANES), bf16),
+        ],
+        scratch_shapes=[
+            pltpu.VMEM((total, LANES), f32),
+            pltpu.VMEM((total, LANES), f32),
+            pltpu.VMEM((BLOCK, PAIR * LANES), f32),
+        ],
+        compiler_params=pltpu.CompilerParams(vmem_limit_bytes=VMEM_BYTES),
+        name="attend_back",
+    )(mb, weights, query, key, value, mixed, lse, docs_col, docs_row, cosine, sine)
+
+
+def feed_kernel(hn_ref, cb_ref, wgu_ref, wd_ref, f_ref, dgu_ref, o_ref, e_ref):
+    hidden = wd_ref.shape[0]
+    both = dot_nn(hn_ref[...], wgu_ref[...])
+    gate, up = both[:, :hidden], both[:, hidden:]
+    sig = 1.0 / (1.0 + jnp.exp(-gate))
+    swish = gate * sig
+    inner = (swish * up).astype(bf16)
+    f_ref[...] = inner
+    o_ref[...] = dot_nn(inner, wd_ref[...]).astype(bf16)
+    grad = dot_nt(cb_ref[...], wd_ref[...])
+    dgu_ref[:, :hidden] = (grad * up * sig * (1.0 + gate * (1.0 - sig))).astype(bf16)
+    dgu_ref[:, hidden:] = (grad * swish).astype(bf16)
+    e_ref[...] = dot_nt(dgu_ref[...], wgu_ref[...]).astype(bf16)
+
+
+def feed(normed, cot, w_both, w_down):
+    total, hidden = normed.shape[0], w_down.shape[0]
+    shapes = [(hidden, bf16), (2 * hidden, bf16), (D, bf16), (D, bf16)]
+    return pl.pallas_call(
+        feed_kernel,
+        grid=(total // BLOCK,),
+        in_specs=[rows_of(BLOCK, D), rows_of(BLOCK, D), whole(D, 2 * hidden), whole(hidden, D)],
+        out_specs=[rows_of(BLOCK, n) for n, t in shapes],
+        out_shape=[jax.ShapeDtypeStruct((total, n), t) for n, t in shapes],
+        compiler_params=pltpu.CompilerParams(vmem_limit_bytes=VMEM_BYTES),
+        name="feed",
+    )(normed, cot, w_both, w_down)
+
+
+def inverse_norm(values):
+    return lax.rsqrt(jnp.mean(values * values, axis=-1, keepdims=True) + norm_epsilon)
+
+
+def norm_back(values, inverse, grad):
+    return inverse * grad - values * inverse**3 * jnp.mean(grad * values, axis=-1, keepdims=True)
+
+
+def pad_heads(matrix):
+    rows, cols = matrix.shape
+    split = matrix.reshape(rows, cols // (HEAD // 2), HEAD // 2)
+    return jnp.pad(split, ((0, 0), (0, 0), (0, LANES // 2 - HEAD // 2))).reshape(rows, -1)
+
+
+def cut_heads(matrix):
+    rows, cols = matrix.shape
+    split = matrix.reshape(rows, cols // (LANES // 2), LANES // 2)
+    return split[..., : HEAD // 2].reshape(rows, -1)
+
+
+def body_fast(
+    inputs,
+    cotangent,
+    doc_ids,
+    positions,
+    gain_first,
+    query_weight,
+    key_weight,
+    value_weight,
+    output_weight,
+    gain_second,
+    gate_weight,
+    up_weight,
+    down_weight,
+):
+    rows = inputs.shape[0]
+    own = query_weight.shape[0]
+    hidden_block = down_weight.shape[0]
+    gain_one = gain_first.astype(f32)[:, None]
+    gain_two = gain_second.astype(f32)[:, None]
+
+    marks = jnp.stack([doc_ids, positions // 128, positions % 128], axis=1).astype(bf16)
+    marks = jnp.pad(marks, ((0, 0), (0, LANES - 3)))
+    rows_all = gather_rows(jnp.concatenate([inputs, marks], axis=1))
+    docs = rows_all[:, D].astype(f32)
+    docs_col, docs_row = docs[:, None], docs[None, :]
+
+    parts = jnp.concatenate(
+        [
+            (query_weight.astype(f32) * gain_one).astype(bf16).reshape(own, KV_HEADS, QUERY_COLS),
+            (key_weight.astype(f32) * gain_one).astype(bf16).reshape(own, KV_HEADS, HEAD),
+            (value_weight.astype(f32) * gain_one).astype(bf16).reshape(own, KV_HEADS, HEAD),
+        ],
+        axis=-1,
+    )
+    parts = jnp.stack([parts[:, g] for g in GROUP_OF])
+    parts = lax.all_to_all(parts, "seq", 0, 0, tiled=True)
+    w_heads = lax.all_gather(parts, "dp", axis=0, tiled=True).reshape(D, HEAD_COLS)
+    w_heads = pad_heads(w_heads)
+
+    block = gather_bit(gather_bit(output_weight, BIT_C, 0), BIT_ZL, 0)
+    w_out = across(block.reshape(PAIR, 2, HEAD // 2, D))
+    w_out = jnp.pad(w_out, ((0, 0), (0, 0), (0, LANES // 2 - HEAD // 2), (0, 0)))
+    w_out = w_out.reshape(PAIR * LANES, D)
+
+    both = jnp.stack(
+        [
+            (gate_weight.astype(f32) * gain_two).astype(bf16),
+            (up_weight.astype(f32) * gain_two).astype(bf16),
+        ]
+    ).reshape(2, own, 2, 2, 2, 2, 2, hidden_block)
+    both = both.transpose(3, 5, 6, 1, 0, 2, 4, 7)
+    for axis, bit in ((2, BIT_C), (0, BIT_X), (1, BIT_ZL)):
+        both = trade_bit(both, bit, axis)
+    both = both.reshape(2, 4 * own, 8 * hidden_block)
+    both = gather_bit(both, BIT_ZH, 1)
+    both = gather_bit(both, BIT_Y, 0)
+    w_both = both.reshape(D, 8 * hidden_block)
+    w_down = gather_bit(gather_bit(down_weight, BIT_ZH, 0), BIT_Y, 0).reshape(4 * hidden_block, D)
+
+    cot_all = gather_square(cotangent)
+
+    normed, query, key, value, cosine, sine = project(rows_all, w_heads)
+    mixed, lse, term = attend(query, key, value, docs_col, docs_row, w_out)
+    x_float = inputs.astype(f32)
+    middle = x_float + scatter_rows(term).astype(f32)
+
+    inverse_two = inverse_norm(middle)
+    normed_two = gather_square((middle * inverse_two).astype(bf16))
+    inner, grad_both, out_term, back_term = feed(normed_two, cot_all, w_both, w_down)
+    grad_two = scatter_square(back_term)
+    cot_float = cotangent.astype(f32)
+    grad_middle = cot_float + norm_back(middle, inverse_two, grad_two)
+    middle_all = gather_rows(grad_middle.astype(bf16))
+    outputs = (middle + scatter_square(out_term)).astype(bf16)
+
+    down_term = dot_tn(inner, cot_all).astype(bf16).reshape(2, 2, hidden_block, D)
+    down_grad = reduce_bit(reduce_bit(down_term, BIT_Y, 0), BIT_ZH, 0)
+    both_term = dot_tn(normed_two, grad_both).astype(bf16).reshape(2, 2, 2, 4 * own, 8 * hidden_block)
+    both_sum = reduce_bit(reduce_bit(both_term, BIT_Y, 0), BIT_ZH, 1)
+    both_sum = both_sum.astype(bf16).reshape(2, 2, 2, own, 2, 2, 2, hidden_block)
+    for axis, bit in ((2, BIT_C), (0, BIT_X), (1, BIT_ZL)):
+        both_sum = trade_bit(both_sum, bit, axis)
+    both_sum = both_sum.transpose(4, 3, 5, 0, 6, 1, 2, 7).reshape(2, own, -1).astype(f32)
+    gate_grad, up_grad = both_sum[0] * gain_two, both_sum[1] * gain_two
+    second_grad = jnp.sum(
+        gate_weight.astype(f32) * gate_grad + up_weight.astype(f32) * up_grad, axis=-1
+    ) / gain_two[:, 0]
+
+    grad_query, grad_kv = attend_back(
+        middle_all, w_out, query, key, value, mixed, lse, docs_col, docs_row, cosine, sine
+    )
+    grad_heads = jnp.concatenate([grad_query, grad_kv], axis=1)
+    first_sum = scatter_rows(dot_nt(grad_heads, w_heads).astype(bf16)).astype(f32)
+    inputs_grad = (grad_middle + norm_back(x_float, inverse_norm(x_float), first_sum)).astype(bf16)
+
+    out_part = dot_tn(mixed, middle_all).astype(bf16).reshape(PAIR * 2, LANES // 2, D)
+    out_part = out_part[:, : HEAD // 2].reshape(2, 2, own, D).transpose(1, 0, 2, 3)
+    out_part = lax.psum_scatter(out_part.reshape(4 * own, D), "dp", scatter_dimension=0, tiled=True)
+    output_grad = across(out_part).astype(f32)
+
+    head_term = cut_heads(dot_tn(normed, grad_heads).astype(bf16))
+    head_term = lax.psum_scatter(head_term, "dp", scatter_dimension=0, tiled=True)
+    head_term = lax.all_to_all(head_term.reshape(8, own, HEAD_COLS), "seq", 0, 0, tiled=True)
+    head_term = jnp.stack([head_term[GROUP_OF.index(g)] for g in range(8)], axis=1)
+    head_term = head_term.astype(f32) * gain_one[:, :, None]
+    query_grad = head_term[..., :QUERY_COLS].reshape(own, D)
+    key_grad = head_term[..., QUERY_COLS : QUERY_COLS + HEAD].reshape(own, KV_HEADS * HEAD)
+    value_grad = head_term[..., QUERY_COLS + HEAD :].reshape(own, KV_HEADS * HEAD)
+    first_grad = (
+        jnp.sum(query_weight.astype(f32) * query_grad, axis=-1)
+        + jnp.sum(key_weight.astype(f32) * key_grad, axis=-1)
+        + jnp.sum(value_weight.astype(f32) * value_grad, axis=-1)
+    ) / gain_one[:, 0]
+    return (
+        outputs,
+        inputs_grad,
+        first_grad,
+        query_grad,
+        key_grad,
+        value_grad,
+        output_grad,
+        second_grad,
+        gate_grad,
+        up_grad,
+        down_grad,
+    )
+
 
 def solution(mesh):
     placed = (
@@ -397,8 +862,10 @@
         P(("dp", "seq"), None),
         P(("dp", "seq"), None),
     )
+    shape = dict(mesh.shape)
+    tensor_parallel = shape["dp"] == 4 and shape["seq"] == KV_HEADS
     return jax.shard_map(
-        body,
+        body_fast if tensor_parallel else body,
         mesh=mesh,
         in_specs=placed,
         out_specs=(

time: 2000 us -> 523 us (0.26)
  waiting for transfers between devices: 1640 us -> 281 us
  matrix products: 173 us -> 18.4 us
  blocking collectives: 121 us -> 16.7 us
  Pallas kernels: 0 us -> 41.9 us
  starting transfers between devices: 1.32 us -> 42.7 us
  local copies, waits for them, and re-layouts: 18.4 us -> 58.8 us
  other arithmetic: 16.2 us -> 38.7 us
    reduce_scatter x7 -> x4, waiting for transfers between devices: 1130 us -> 2.3 us  [the longest x2 2.26 us: scatter_rows(): return lax.psum_scatter(value, 'seq', scatter_dimension=0, tiled=True)]
    all_gather x11 -> x3, waiting for transfers between devices: 505 us -> 82.7 us  [the longest x2 60.4 us: gather_rows(): return lax.all_gather(value, 'seq', axis=0, tiled=True)]
    ppermute x0 -> x38, waiting for transfers between devices: none -> 185 us  [the longest x36 185 us: swap(): return lax.ppermute(value, BOTH, [(i, i ^ bit) for i in range(32)])]
    dot_general x28 -> x5, matrix products: 173 us -> 18.4 us  [the longest x4 14.9 us: dot_tn(): lax.dot_general(left, right, (((0,), (0,)), ((), ())), preferred_element_...]
    unnamed x2 -> x0, blocking collectives: 82 us -> none
    pallas_call x0 -> x4, Pallas kernels: none -> 41.9 us  [the longest x1 15.2 us: feed(): pl.pallas_call(feed_kernel, grid=(total // BLOCK,), in_specs=[rows_of(BLO...]
    all_gather x3 -> x0, blocking collectives: 38.7 us -> none  [the longest x1 14.2 us: body(): lax.all_gather(delta_flat, 'seq', axis=0, tiled=True)]
    ppermute x0 -> x38, starting transfers between devices: none -> 37.8 us  [the longest x36 35.5 us: swap(): return lax.ppermute(value, BOTH, [(i, i ^ bit) for i in range(32)])]
  transfers between devices with their start and end apart: 18 -> 46, of which waited for: 16 -> 26; matrix products, arithmetic and copies ran while one was open for 9% -> 19% of each run, Pallas kernels for 0% -> 2%
where the time goes in v1:
time: 523 us; the launch traced here: 514 us
  waiting for transfers between devices  281 us (54%)
  local copies, waits for them, and re-layouts  58.8 us (11%)
  starting transfers between devices  42.7 us (8%)
  Pallas kernels  41.9 us (8%)
  other arithmetic  38.7 us (7%)
  matrix products  18.4 us (4%)
  blocking collectives  16.7 us (3%)
  between operations  15.8 us (3%)
    ppermute x36, waiting for transfers between devices, swap(): return lax.ppermute(value, BOTH, [(i, i ^ bit) for i in range(32)])  185 us
    all_gather x2, waiting for transfers between devices, gather_rows(): return lax.all_gather(value, 'seq', axis=0, tiled=True)  60.4 us
    ppermute x36, starting transfers between devices, swap(): return lax.ppermute(value, BOTH, [(i, i ^ bit) for i in range(32)])  35.5 us
    all_gather x1, waiting for transfers between devices, body_fast(): lax.all_gather(parts, 'dp', axis=0, tiled=True).reshape(D, HEAD_COLS)  22.3 us
    unnamed x104, local copies, waits for them, and re-layouts  17.7 us
    all_to_all x1, blocking collectives, body_fast(): parts = lax.all_to_all(parts, 'seq', 0, 0, tiled=True)  16.7 us
    pallas_call x1, Pallas kernels, feed(): pl.pallas_call(feed_kernel, grid=(total // BLOCK,), in_specs=[rows_of(BLO...  15.2 us
    dot_general x4, matrix products, dot_tn(): lax.dot_general(left, right, (((0,), (0,)), ((), ())), preferred_element_...  14.9 us
  transfers between devices with their start and end apart: 46, of which 26 were waited for; matrix products, arithmetic and copies ran while one was open for 19% of the time, Pallas kernels for 2%

profile of v1, /device:TPU:0, one launch (start us, length us, event | category | flops | bytes accessed | tf_op | source)
XLA Modules:
  0.0 513.7 jit_solution(3513294463950506566)
XLA Ops:
  11.3 16.7 %all_to_all.10 = bf16[8,48,384]{2,1,0:T(8,128)(2,1)} all-to-all(bf16[8,48,384]{2,1,0:T(8,128)(2,1)S(1)} %constant_dynamic-update-slice_fusion), channel_id=1, replica_groups=mesh['dp'=4,'seq'=8] {'seq'}, dimensions={0} | all-to-all | bytes 589824 | tf_op jit(solution)/shard_map/all_to_all | solution.py:756
  31.1 8.6 %collective-permute-done.1 = bf16[2,48,1536]{2,1,0:T(8,128)(2,1)S(1)} collective-permute-done((bf16[2,48,1536]{2,1,0:T(8,128)(2,1)S(1)}, bf16[2,48,1536]{2,1,0:T(8,128)(2,1)S(1)}, u32[]{:S(2)}, u32[]{:S(2)}) %collective-permute-start.1) | collective-permute-done | bytes 294944 | tf_op jit(solution)/shard_map/ppermute | solution.py:399
  42.0 22.3 %all-gather.6.cloned.1.call-done = bf16[32,48,384]{2,1,0:T(8,128)(2,1)} async-done(((bf16[8,48,384]{2,1,0:T(8,128)(2,1)}), bf16[32,48,384]{2,1,0:T(8,128)(2,1)}) %all-gather.6.cloned.1.call-update) | async-done | bytes 1179664 | tf_op jit(solution)/shard_map/all_gather | solution.py:757
  64.3 4.2 reshape_reshape.3
  68.4 3.0 copy.285
  74.7 30.7 %all-gather.4.cloned.1.call-done.x_ref = bf16[1024,1664]{1,0:T(8,128)(2,1)} async-done(((bf16[128,1664]{1,0:T(8,128)(2,1)}), bf16[1024,1664]{1,0:T(8,128)(2,1)}) %all-gather.4.cloned.1.call-update) | async-done | bytes 3407888 | tf_op jit(solution)/shard_map/all_gather | solution.py:468
  108.9 7.6 %project.1 = (bf16[1024,1536]{1,0:T(8,128)(2,1)}, bf16[1024,256]{1,0:T(8,128)(2,1)}, bf16[1024,128]{1,0:T(8,128)(2,1)}, bf16[1024,128]{1,0:T(8,128)(2,1)}, f32[1024,128]{1,0:T(8,128)}, /*index=5*/f32[1024,128]{1,0:T(8,128)}) custom-call(bf16[1024,1664]{1,0:T(8,128)(2,1)} %all-gather.4.cloned.1.call-done.x_ref, bf16[1536,512]{1,0:T(8,128)(2,1)} %copy.257.w_ref, ...), custom_call_target="tpu_custom_call" | custom-call | tf_op jit(solution)/shard_map/project/pallas_call | solution.py:529
  116.5 7.9 %attend.1 = (bf16[1024,256]{1,0:T(8,128)(2,1)}, f32[1024,2]{1,0:T(8,128)}, bf16[1024,1536]{1,0:T(8,128)(2,1)}) custom-call(bf16[1024,256]{1,0:T(8,128)(2,1)} %get-tuple-element.26.q_ref, bf16[1024,128]{1,0:T(8,128)(2,1)} %get-tuple-element.27.k_ref, bf16[1024,128]{1,0:T(8,128)(2,1)} %get-tuple-element.28.v_ref, f32[1024,1]{1,0:T(8,128)} %slice_convert_fusion.dcol_ref, ...), custom_call_target="tpu_custom_call" | custom-call | tf_op jit(solution)/shard_map/attend/pallas_call | solution.py:572
  127.0 2.5 dynamic-slice_bitcast_fusion.3
  134.0 1.9 constant_dynamic-update-slice_fusion.23
  138.1 26.1 %collective-permute-done.18 = bf16[128,1536]{1,0:T(8,128)(2,1)} collective-permute-done((bf16[128,1536]{1,0:T(8,128)(2,1)}, bf16[128,1536]{1,0:T(8,128)(2,1)}, u32[]{:S(2)}, u32[]{:S(2)}) %collective-permute-start.18) | collective-permute-done | bytes 393248 | tf_op jit(solution)/shard_map/ppermute | solution.py:399
  166.4 1.9 collective-permute-start.19
  170.7 2.6 collective-permute-start.11
  177.9 5.2 %collective-permute-done.11 = bf16[64,1536]{1,0:T(8,128)(2,1)S(1)} collective-permute-done((bf16[64,1536]{1,0:T(8,128)(2,1)S(1)}, bf16[64,1536]{1,0:T(8,128)(2,1)S(1)}, u32[]{:S(2)}, u32[]{:S(2)}) %collective-permute-start.11) | collective-permute-done | bytes 196640 | tf_op jit(solution)/shard_map/ppermute | solution.py:399
  183.8 7.2 %collective-permute-done.15 = bf16[2,2,48,2,2,2,128]{6,2,5,4,3,1,0:T(8,128)(2,1)S(1)} collective-permute-done((bf16[2,2,48,2,2,2,128]{6,2,5,4,3,1,0:T(8,128)(2,1)S(1)}, bf16[2,2,48,2,2,2,128]{6,2,5,4,3,1,0:T(8,128)(2,1)S(1)}, u32[]{:S(2)}, u32[]{:S(2)}) %collective-permute-start.15) | collective-permute-done | bytes 393248 | tf_op jit(solution)/shard_map/ppermute | solution.py:399
  192.6 3.3 reshape.196
  195.9 2.2 collective-permute-start.16
  203.2 29.8 %collective-permute-done.16 = bf16[2,192,1024]{2,1,0:T(8,128)(2,1)} collective-permute-done((bf16[2,192,1024]{2,1,0:T(8,128)(2,1)}, bf16[2,192,1024]{2,1,0:T(8,128)(2,1)}, u32[]{:S(2)}, u32[]{:S(2)}) %collective-permute-start.16) | collective-permute-done | bytes 786464 | tf_op jit(solution)/shard_map/ppermute | solution.py:399
  236.4 2.0 collective-permute-start.5
  240.2 3.1 collective-permute-done.5
  249.8 21.1 %collective-permute-done.17 = bf16[2,2,192,1024]{3,2,0,1:T(8,128)(2,1)S(1)} collective-permute-done((bf16[2,2,192,1024]{3,2,0,1:T(8,128)(2,1)S(1)}, bf16[2,2,192,1024]{3,2,0,1:T(8,128)(2,1)S(1)}, u32[]{:S(2)}, u32[]{:S(2)}) %collective-permute-start.17) | collective-permute-done | bytes 1572896 | tf_op jit(solution)/shard_map/ppermute | solution.py:399
  271.4 2.1 copy.263
  274.7 15.2 %feed.1 = (bf16[1024,512]{1,0:T(8,128)(2,1)}, bf16[1024,1024]{1,0:T(8,128)(2,1)}, bf16[1024,1536]{1,0:T(8,128)(2,1)}, bf16[1024,1536]{1,0:T(8,128)(2,1)}) custom-call(bf16[1024,1536]{1,0:T(8,128)(2,1)} %constant_dynamic-update-slice_fusion.13.hn_ref, bf16[1024,1536]{1,0:T(8,128)(2,1)} %copy-done.4, bf16[1536,1024]{1,0:T(8,128)(2,1)} %bitcast.208, ...), custom_call_target="tpu_custom_call" | custom-call | tf_op jit(solution)/shard_map/feed/pallas_call | solution.py:689
  292.5 2.6 collective-permute-done.25
  297.9 2.0 collective-permute-start.21
  300.5 3.0 collective-permute-done.26
  305.2 2.1 collective-permute-start.29
  309.5 2.1 collective-permute-start.24
  311.5 4.7 collective-permute-done.27
  317.7 6.1 %collective-permute-done.22 = bf16[128,1536]{1,0:T(8,128)(2,1)S(1)} collective-permute-done((bf16[128,1536]{1,0:T(8,128)(2,1)S(1)}, bf16[128,1536]{1,0:T(8,128)(2,1)S(1)}, u32[]{:S(2)}, u32[]{:S(2)}) %collective-permute-start.22) | collective-permute-done | bytes 393248 | tf_op jit(solution)/shard_map/ppermute | solution.py:399
  323.8 2.8 fusion.52
  326.8 5.8 %convolution_convert_fusion.1 = bf16[1536,1024]{1,0:T(8,128)(2,1)S(1)} fusion(bf16[1024,1536]{1,0:T(8,128)(2,1)} %constant_dynamic-update-slice_fusion.13.hn_ref, bf16[1024,1024]{1,0:T(8,128)(2,1)S(1)} %copy-done.36), kind=kOutput, calls=%fused_computation.1 | convolution fusion | flops 3222798336 | bytes 8388608 | tf_op jit(solution)/shard_map/dot_general | solution.py:487
  335.6 29.8 %all-gather.8.cloned.1.call-done.mb_ref = bf16[1024,1536]{1,0:T(8,128)(2,1)} async-done(((bf16[128,1536]{1,0:T(8,128)(2,1)}), bf16[1024,1536]{1,0:T(8,128)(2,1)}) %all-gather.8.cloned.1.call-update) | async-done | bytes 3145744 | tf_op jit(solution)/shard_map/all_gather | solution.py:468
  365.4 11.1 %attend_back.1 = (bf16[1024,256]{1,0:T(8,128)(2,1)}, bf16[1024,256]{1,0:T(8,128)(2,1)}) custom-call(bf16[1024,1536]{1,0:T(8,128)(2,1)} %all-gather.8.cloned.1.call-done.mb_ref, bf16[256,1536]{1,0:T(8,128)(2,1)} %bitcast.210, bf16[1024,256]{1,0:T(8,128)(2,1)} %get-tuple-element.26.q_ref, bf16[1024,128]{1,0:T(8,128)(2,1)} %get-tuple-element.27.k_ref, ...), custom_call_target="tpu_custom_call" | custom-call | tf_op jit(solution)/shard_map/attend_back/pallas_call | solution.py:640
  378.6 4.1 convolution_convert_fusion.3
  384.4 2.7 convert_add_fusion
  391.7 4.0 convolution_convert_fusion.2
  398.2 27.6 %collective-permute-done.32 = bf16[2,192,1024]{2,1,0:T(8,128)(2,1)} collective-permute-done((bf16[2,192,1024]{2,1,0:T(8,128)(2,1)}, bf16[2,192,1024]{2,1,0:T(8,128)(2,1)}, u32[]{:S(2)}, u32[]{:S(2)}) %collective-permute-start.32) | collective-permute-done | bytes 786464 | tf_op jit(solution)/shard_map/ppermute | solution.py:399
  425.8 2.3 fusion
  428.1 2.7 reshape.209
  432.2 3.4 convolution_convert_fusion
  438.9 9.7 %collective-permute-done.34 = bf16[2,2,48,2,2,2,128]{6,2,5,4,3,1,0:T(8,128)(2,1)S(1)} collective-permute-done((bf16[2,2,48,2,2,2,128]{6,2,5,4,3,1,0:T(8,128)(2,1)S(1)}, bf16[2,2,48,2,2,2,128]{6,2,5,4,3,1,0:T(8,128)(2,1)S(1)}, u32[]{:S(2)}, u32[]{:S(2)}) %collective-permute-start.34) | collective-permute-done | bytes 393248 | tf_op jit(solution)/shard_map/ppermute | solution.py:399
  448.8 9.6 %collective-permute-done.37 = bf16[128,1536]{1,0:T(8,128)(2,1)S(1)} collective-permute-done((bf16[128,1536]{1,0:T(8,128)(2,1)S(1)}, bf16[128,1536]{1,0:T(8,128)(2,1)S(1)}, u32[]{:S(2)}, u32[]{:S(2)}) %collective-permute-start.37) | collective-permute-done | bytes 393248 | tf_op jit(solution)/shard_map/ppermute | solution.py:399
  459.8 16.6 %collective-permute-done.35 = bf16[2,2,48,2,2,2,128]{6,2,5,4,3,1,0:T(8,128)(2,1)S(1)} collective-permute-done((bf16[2,2,48,2,2,2,128]{6,2,5,4,3,1,0:T(8,128)(2,1)S(1)}, bf16[2,2,48,2,2,2,128]{6,2,5,4,3,1,0:T(8,128)(2,1)S(1)}, u32[]{:S(2)}, u32[]{:S(2)}) %collective-permute-start.35) | collective-permute-done | bytes 393248 | tf_op jit(solution)/shard_map/ppermute | solution.py:399
  479.3 3.9 all-to-all-start.1
  487.6 10.9 %all-to-all-done.1 = bf16[8,48,384]{2,1,0:T(8,128)(2,1)S(1)} async-done(((bf16[8,48,384]{2,1,0:T(8,128)(2,1)}), bf16[8,48,384]{2,1,0:T(8,128)(2,1)S(1)}, u32[]{:S(2)}, u32[]{:S(2)}) %all-to-all-start.1) | async-done | bytes 294944 | tf_op jit(solution)/shard_map/all_to_all | solution.py:823
  500.8 2.3 reduce-scatter.7.cloned.1.call-done
  504.3 2.1 fusion.8
  (288 shorter events, 97.0 us)
Async XLA Ops:
  7.2 57.1 %all-gather.6.cloned.1.call-start = ((), (), s32[]{:S(2)}) async-start(), calls=%async_computation.7 | async-start | bytes 1474560 | tf_op jit(solution)/shard_map/all_gather | solution.py:757
  28.0 77.4 %all-gather.4.cloned.1.call-start = ((), (), s32[]{:S(2)}) async-start(), calls=%async_computation.6 | async-start | bytes 3833856 | tf_op jit(solution)/shard_map/all_gather | solution.py:468
  29.0 169.1 %reduce-scatter.5.cloned.1.call-start = ((), (), s32[]{:S(2)}) async-start(), calls=%async_computation.8 | async-start | bytes 3538944 | tf_op jit(solution)/shard_map/reduce_scatter | solution.py:472
  29.1 1.4 collective-permute-start
  30.6 9.1 %collective-permute-start.1 = (bf16[2,48,1536]{2,1,0:T(8,128)(2,1)S(1)}, bf16[2,48,1536]{2,1,0:T(8,128)(2,1)S(1)}, u32[]{:S(2)}, u32[]{:S(2)}) collective-permute-start(bf16[2,48,1536]{2,1,0:T(8,128)(2,1)S(1)} %pad_maximum_fusion.11), channel_id=1, source_target_pairs={{0,2},{1,3},{2,0},{3,1},{4,6},{5,7},{6,4},{7,5},{8,10},{9,11},{10,... | collective-permute-start | bytes 884744 | tf_op jit(solution)/shard_map/ppermute | solution.py:399
  39.8 1.2 collective-permute-start.2
  124.5 240.9 %all-gather.8.cloned.1.call-start = ((), (), s32[]{:S(2)}) async-start(), calls=%async_computation.9 | async-start | bytes 3538944 | tf_op jit(solution)/shard_map/all_gather | solution.py:468
  130.5 5.4 %collective-permute-start.13 = (bf16[2,2,48,2,2,2,128]{6,2,5,4,3,1,0:T(8,128)(2,1)}, bf16[2,2,48,2,2,2,128]{6,2,5,4,3,1,0:T(8,128)(2,1)}, u32[]{:S(2)}, u32[]{:S(2)}) collective-permute-start(bf16[2,2,48,2,2,2,128]{6,2,5,4,3,1,0:T(8,128)(2,1)} %bitcast.207), channel_id=1, source_target_pairs={{0,1},{1,0},{2,3},{3,2},{4,5},{5,4},{6,7},{7,6},{8,9},{9,8},{10,11... | collective-permute-start | bytes 1179656 | tf_op jit(solution)/shard_map/ppermute | solution.py:399
  130.7 39.0 %collective-permute-start.8 = (bf16[128,1536]{1,0:T(8,128)(2,1)}, bf16[128,1536]{1,0:T(8,128)(2,1)}, u32[]{:S(2)}, u32[]{:S(2)}) collective-permute-start(bf16[128,1536]{1,0:T(8,128)(2,1)} %param.14), channel_id=1, source_target_pairs={{0,8},{1,9},{2,10},{3,11},{4,12},{5,13},{6,14},{7,15},{8,0},{9,1},... | collective-permute-start | bytes 1179656 | tf_op jit(solution)/shard_map/ppermute | solution.py:399
  132.2 36.1 %collective-permute-start.9 = (bf16[128,1536]{1,0:T(8,128)(2,1)}, bf16[128,1536]{1,0:T(8,128)(2,1)}, u32[]{:S(2)}, u32[]{:S(2)}) collective-permute-start(bf16[128,1536]{1,0:T(8,128)(2,1)} %param.14), channel_id=1, source_target_pairs={{0,2},{1,3},{2,0},{3,1},{4,6},{5,7},{6,4},{7,5},{8,10},{9,11},{10,... | collective-permute-start | bytes 1179656 | tf_op jit(solution)/shard_map/ppermute | solution.py:399
  132.6 31.5 %collective-permute-start.18 = (bf16[128,1536]{1,0:T(8,128)(2,1)}, bf16[128,1536]{1,0:T(8,128)(2,1)}, u32[]{:S(2)}, u32[]{:S(2)}) collective-permute-start(bf16[128,1536]{1,0:T(8,128)(2,1)} %param.25), channel_id=1, source_target_pairs={{0,4},{1,5},{2,6},{3,7},{4,0},{5,1},{6,2},{7,3},{8,12},{9,13},{10,... | collective-permute-start | bytes 1179656 | tf_op jit(solution)/shard_map/ppermute | solution.py:399
  137.3 39.7 %collective-permute-start.14 = (bf16[2,2,48,2,2,2,128]{6,2,5,4,3,1,0:T(8,128)(2,1)S(1)}, bf16[2,2,48,2,2,2,128]{6,2,5,4,3,1,0:T(8,128)(2,1)S(1)}, u32[]{:S(2)}, u32[]{:S(2)}) collective-permute-start(bf16[2,2,48,2,2,2,128]{6,2,5,4,3,1,0:T(8,128)(2,1)S(1)} %bitcast.223), channel_id=1, source_target_pairs={{0,8},{1,9},{2,10},{3,11},{4,12},{5,13},{6,14},{7,15},{8,0},{9,1},... | collective-permute-start | bytes 1179656 | tf_op jit(solution)/shard_map/ppermute | solution.py:399
  166.4 79.2 %collective-permute-start.19 = (bf16[2,128,1536]{2,1,0:T(8,128)(2,1)}, bf16[2,128,1536]{2,1,0:T(8,128)(2,1)}, u32[]{:S(2)}, u32[]{:S(2)}) collective-permute-start(bf16[2,128,1536]{2,1,0:T(8,128)(2,1)} %pad_maximum_fusion.4), channel_id=1, source_target_pairs={{0,16},{1,17},{2,18},{3,19},{4,20},{5,21},{6,22},{7,23},{8,24},{9,... | collective-permute-start | bytes 2359304 | tf_op jit(solution)/shard_map/ppermute | solution.py:399
  169.2 7.9 %collective-permute-start.10 = (bf16[64,1536]{1,0:T(8,128)(2,1)S(1)}, bf16[64,1536]{1,0:T(8,128)(2,1)S(1)}, u32[]{:S(2)}, u32[]{:S(2)}) collective-permute-start(bf16[64,1536]{1,0:T(8,128)(2,1)S(1)} %slice.221), channel_id=1, source_target_pairs={{0,8},{1,9},{2,10},{3,11},{4,12},{5,13},{6,14},{7,15},{8,0},{9,1},... | collective-permute-start | bytes 589832 | tf_op jit(solution)/shard_map/ppermute | solution.py:399
  170.7 12.4 %collective-permute-start.11 = (bf16[64,1536]{1,0:T(8,128)(2,1)S(1)}, bf16[64,1536]{1,0:T(8,128)(2,1)S(1)}, u32[]{:S(2)}, u32[]{:S(2)}) collective-permute-start(bf16[64,1536]{1,0:T(8,128)(2,1)S(1)} %slice.222), channel_id=1, source_target_pairs={{0,2},{1,3},{2,0},{3,1},{4,6},{5,7},{6,4},{7,5},{8,10},{9,11},{10,... | collective-permute-start | bytes 589832 | tf_op jit(solution)/shard_map/ppermute | solution.py:399
  177.1 13.9 %collective-permute-start.15 = (bf16[2,2,48,2,2,2,128]{6,2,5,4,3,1,0:T(8,128)(2,1)S(1)}, bf16[2,2,48,2,2,2,128]{6,2,5,4,3,1,0:T(8,128)(2,1)S(1)}, u32[]{:S(2)}, u32[]{:S(2)}) collective-permute-start(bf16[2,2,48,2,2,2,128]{6,2,5,4,3,1,0:T(8,128)(2,1)S(1)} %fusion.26), channel_id=1, source_target_pairs={{0,2},{1,3},{2,0},{3,1},{4,6},{5,7},{6,4},{7,5},{8,10},{9,11},{10,... | collective-permute-start | bytes 1179656 | tf_op jit(solution)/shard_map/ppermute | solution.py:399
  183.8 64.5 %collective-permute-start.12 = (bf16[512,1536]{1,0:T(8,128)(2,1)}, bf16[512,1536]{1,0:T(8,128)(2,1)}, u32[]{:S(2)}, u32[]{:S(2)}) collective-permute-start(bf16[512,1536]{1,0:T(8,128)(2,1)} %get-tuple-element.121), channel_id=1, source_target_pairs={{0,1},{1,0},{2,3},{3,2},{4,5},{5,4},{6,7},{7,6},{8,9},{9,8},{10,11... | collective-permute-start | bytes 4718600 | tf_op jit(solution)/shard_map/ppermute | solution.py:399
  195.9 37.1 %collective-permute-start.16 = (bf16[2,192,1024]{2,1,0:T(8,128)(2,1)}, bf16[2,192,1024]{2,1,0:T(8,128)(2,1)}, u32[]{:S(2)}, u32[]{:S(2)}) collective-permute-start(bf16[2,192,1024]{2,1,0:T(8,128)(2,1)} %reshape.196), channel_id=1, source_target_pairs={{0,4},{1,5},{2,6},{3,7},{4,0},{5,1},{6,2},{7,3},{8,12},{9,13},{10,... | collective-permute-start | bytes 2359304 | tf_op jit(solution)/shard_map/ppermute | solution.py:399
  198.1 34.9 %copy-start.15 = (bf16[2,192,1024]{2,1,0:T(8,128)(2,1)S(1)}, bf16[2,192,1024]{2,1,0:T(8,128)(2,1)}, u32[]{:S(2)}) copy-start(bf16[2,192,1024]{2,1,0:T(8,128)(2,1)} %reshape.196) | copy-start | bytes 2359300
  200.5 37.9 %collective-permute-start.3 = (bf16[128,1536]{1,0:T(8,128)(2,1)S(1)}, bf16[128,1536]{1,0:T(8,128)(2,1)S(1)}, u32[]{:S(2)}, u32[]{:S(2)}) collective-permute-start(bf16[128,1536]{1,0:T(8,128)(2,1)S(1)} %get-tuple-element.49), channel_id=1, source_target_pairs={{0,8},{1,9},{2,10},{3,11},{4,12},{5,13},{6,14},{7,15},{8,0},{9,1},... | collective-permute-start | bytes 1179656 | tf_op jit(solution)/shard_map/ppermute | solution.py:399
  201.9 34.5 %collective-permute-start.4 = (bf16[128,1536]{1,0:T(8,128)(2,1)S(1)}, bf16[128,1536]{1,0:T(8,128)(2,1)S(1)}, u32[]{:S(2)}, u32[]{:S(2)}) collective-permute-start(bf16[128,1536]{1,0:T(8,128)(2,1)S(1)} %get-tuple-element.49), channel_id=1, source_target_pairs={{0,2},{1,3},{2,0},{3,1},{4,6},{5,7},{6,4},{7,5},{8,10},{9,11},{10,... | collective-permute-start | bytes 1179656 | tf_op jit(solution)/shard_map/ppermute | solution.py:399
  234.5 36.4 %collective-permute-start.17 = (bf16[2,2,192,1024]{3,2,0,1:T(8,128)(2,1)S(1)}, bf16[2,2,192,1024]{3,2,0,1:T(8,128)(2,1)S(1)}, u32[]{:S(2)}, u32[]{:S(2)}) collective-permute-start(bf16[2,2,192,1024]{3,2,0,1:T(8,128)(2,1)S(1)} %pad_maximum_fusion.1), channel_id=1, source_target_pairs={{0,16},{1,17},{2,18},{3,19},{4,20},{5,21},{6,22},{7,23},{8,24},{9,... | collective-permute-start | bytes 4718600 | tf_op jit(solution)/shard_map/ppermute | solution.py:399
  236.4 6.8 %collective-permute-start.5 = (bf16[64,1536]{1,0:T(8,128)(2,1)S(1)}, bf16[64,1536]{1,0:T(8,128)(2,1)S(1)}, u32[]{:S(2)}, u32[]{:S(2)}) collective-permute-start(bf16[64,1536]{1,0:T(8,128)(2,1)S(1)} %slice.219), channel_id=1, source_target_pairs={{0,8},{1,9},{2,10},{3,11},{4,12},{5,13},{6,14},{7,15},{8,0},{9,1},... | collective-permute-start | bytes 589832 | tf_op jit(solution)/shard_map/ppermute | solution.py:399
  238.5 6.3 %collective-permute-start.6 = (bf16[64,1536]{1,0:T(8,128)(2,1)S(1)}, bf16[64,1536]{1,0:T(8,128)(2,1)S(1)}, u32[]{:S(2)}, u32[]{:S(2)}) collective-permute-start(bf16[64,1536]{1,0:T(8,128)(2,1)S(1)} %slice.220), channel_id=1, source_target_pairs={{0,2},{1,3},{2,0},{3,1},{4,6},{5,7},{6,4},{7,5},{8,10},{9,11},{10,... | collective-permute-start | bytes 589832 | tf_op jit(solution)/shard_map/ppermute | solution.py:399
  245.5 27.9 %collective-permute-start.7 = (bf16[512,1536]{1,0:T(8,128)(2,1)S(1)}, bf16[512,1536]{1,0:T(8,128)(2,1)S(1)}, u32[]{:S(2)}, u32[]{:S(2)}) collective-permute-start(bf16[512,1536]{1,0:T(8,128)(2,1)S(1)} %get-tuple-element.125), channel_id=1, source_target_pairs={{0,1},{1,0},{2,3},{3,2},{4,5},{5,4},{6,7},{7,6},{8,9},{9,8},{10,11... | collective-permute-start | bytes 4718600 | tf_op jit(solution)/shard_map/ppermute | solution.py:399
  291.6 3.5 collective-permute-start.25
  292.4 4.9 collective-permute-start.20
  295.7 7.8 %collective-permute-start.26 = (bf16[64,1536]{1,0:T(8,128)(2,1)S(1)}, bf16[64,1536]{1,0:T(8,128)(2,1)S(1)}, u32[]{:S(2)}, u32[]{:S(2)}) collective-permute-start(bf16[64,1536]{1,0:T(8,128)(2,1)S(1)} %get-tuple-element.65), channel_id=1, source_target_pairs={{0,2},{1,3},{2,0},{3,1},{4,6},{5,7},{6,4},{7,5},{8,10},{9,11},{10,... | collective-permute-start | bytes 589832 | tf_op jit(solution)/shard_map/ppermute | solution.py:399
  295.8 7.8 %collective-permute-start.28 = (bf16[64,1536]{1,0:T(8,128)(2,1)S(1)}, bf16[64,1536]{1,0:T(8,128)(2,1)S(1)}, u32[]{:S(2)}, u32[]{:S(2)}) collective-permute-start(bf16[64,1536]{1,0:T(8,128)(2,1)S(1)} %get-tuple-element.64), channel_id=1, source_target_pairs={{0,8},{1,9},{2,10},{3,11},{4,12},{5,13},{6,14},{7,15},{8,0},{9,1},... | collective-permute-start | bytes 589832 | tf_op jit(solution)/shard_map/ppermute | solution.py:399
  297.9 9.7 %collective-permute-start.21 = (bf16[64,1536]{1,0:T(8,128)(2,1)S(1)}, bf16[64,1536]{1,0:T(8,128)(2,1)S(1)}, u32[]{:S(2)}, u32[]{:S(2)}) collective-permute-start(bf16[64,1536]{1,0:T(8,128)(2,1)S(1)} %get-tuple-element.69), channel_id=1, source_target_pairs={{0,2},{1,3},{2,0},{3,1},{4,6},{5,7},{6,4},{7,5},{8,10},{9,11},{10,... | collective-permute-start | bytes 589832 | tf_op jit(solution)/shard_map/ppermute | solution.py:399
  299.9 7.9 %collective-permute-start.23 = (bf16[64,1536]{1,0:T(8,128)(2,1)S(1)}, bf16[64,1536]{1,0:T(8,128)(2,1)S(1)}, u32[]{:S(2)}, u32[]{:S(2)}) collective-permute-start(bf16[64,1536]{1,0:T(8,128)(2,1)S(1)} %get-tuple-element.68), channel_id=1, source_target_pairs={{0,8},{1,9},{2,10},{3,11},{4,12},{5,13},{6,14},{7,15},{8,0},{9,1},... | collective-permute-start | bytes 589832 | tf_op jit(solution)/shard_map/ppermute | solution.py:399
  303.7 12.5 %collective-permute-start.27 = (bf16[128,1536]{1,0:T(8,128)(2,1)S(1)}, bf16[128,1536]{1,0:T(8,128)(2,1)S(1)}, u32[]{:S(2)}, u32[]{:S(2)}) collective-permute-start(bf16[128,1536]{1,0:T(8,128)(2,1)S(1)} %pad_maximum_fusion.8), channel_id=1, source_target_pairs={{0,8},{1,9},{2,10},{3,11},{4,12},{5,13},{6,14},{7,15},{8,0},{9,1},... | collective-permute-start | bytes 1179656 | tf_op jit(solution)/shard_map/ppermute | solution.py:399
  305.2 12.1 %collective-permute-start.29 = (bf16[128,1536]{1,0:T(8,128)(2,1)S(1)}, bf16[128,1536]{1,0:T(8,128)(2,1)S(1)}, u32[]{:S(2)}, u32[]{:S(2)}) collective-permute-start(bf16[128,1536]{1,0:T(8,128)(2,1)S(1)} %pad_maximum_fusion.9), channel_id=1, source_target_pairs={{0,2},{1,3},{2,0},{3,1},{4,6},{5,7},{6,4},{7,5},{8,10},{9,11},{10,... | collective-permute-start | bytes 1179656 | tf_op jit(solution)/shard_map/ppermute | solution.py:399
  307.9 15.9 %collective-permute-start.22 = (bf16[128,1536]{1,0:T(8,128)(2,1)S(1)}, bf16[128,1536]{1,0:T(8,128)(2,1)S(1)}, u32[]{:S(2)}, u32[]{:S(2)}) collective-permute-start(bf16[128,1536]{1,0:T(8,128)(2,1)S(1)} %pad_maximum_fusion.6), channel_id=1, source_target_pairs={{0,8},{1,9},{2,10},{3,11},{4,12},{5,13},{6,14},{7,15},{8,0},{9,1},... | collective-permute-start | bytes 1179656 | tf_op jit(solution)/shard_map/ppermute | solution.py:399
  309.5 14.4 %collective-permute-start.24 = (bf16[128,1536]{1,0:T(8,128)(2,1)S(1)}, bf16[128,1536]{1,0:T(8,128)(2,1)S(1)}, u32[]{:S(2)}, u32[]{:S(2)}) collective-permute-start(bf16[128,1536]{1,0:T(8,128)(2,1)S(1)} %pad_maximum_fusion.7), channel_id=1, source_target_pairs={{0,2},{1,3},{2,0},{3,1},{4,6},{5,7},{6,4},{7,5},{8,10},{9,11},{10,... | collective-permute-start | bytes 1179656 | tf_op jit(solution)/shard_map/ppermute | solution.py:399
  326.7 152.6 %reduce-scatter.9.cloned.1.call-start = ((), (), s32[]{:S(2)}) async-start(), calls=%async_computation.11 | async-start | bytes 1474560 | tf_op jit(solution)/shard_map/reduce_scatter | solution.py:822
  334.3 50.1 %collective-permute-start.31 = (bf16[2,2,192,1024]{3,2,1,0:T(8,128)(2,1)S(1)}, bf16[2,2,192,1024]{3,2,1,0:T(8,128)(2,1)}, u32[]{:S(2)}, u32[]{:S(2)}) collective-permute-start(bf16[2,2,192,1024]{3,2,1,0:T(8,128)(2,1)S(1)} %dynamic-slice_bitcast_fusion), channel_id=1, source_target_pairs={{0,16},{1,17},{2,18},{3,19},{4,20},{5,21},{6,22},{7,23},{8,24},{9,... | collective-permute-start | bytes 4718600 | tf_op jit(solution)/shard_map/ppermute | solution.py:399
  384.3 100.5 %reduce-scatter.11.cloned.1.call-start = ((), (), s32[]{:S(2)}) async-start(), calls=%async_computation.12 | async-start | bytes 737280 | tf_op jit(solution)/shard_map/reduce_scatter | solution.py:818
  388.1 37.7 %collective-permute-start.32 = (bf16[2,192,1024]{2,1,0:T(8,128)(2,1)}, bf16[2,192,1024]{2,1,0:T(8,128)(2,1)}, u32[]{:S(2)}, u32[]{:S(2)}) collective-permute-start(bf16[2,192,1024]{2,1,0:T(8,128)(2,1)} %fusion.12), channel_id=1, source_target_pairs={{0,4},{1,5},{2,6},{3,7},{4,0},{5,1},{6,2},{7,3},{8,12},{9,13},{10,... | collective-permute-start | bytes 2359304 | tf_op jit(solution)/shard_map/ppermute | solution.py:399
  391.4 111.7 %reduce-scatter.7.cloned.1.call-start = ((), (), s32[]{:S(2)}) async-start(), calls=%async_computation.10 | async-start | bytes 3538944 | tf_op jit(solution)/shard_map/reduce_scatter | solution.py:472
  395.7 30.1 %copy-start.20 = (bf16[512,1536]{1,0:T(8,128)(2,1)}, bf16[512,1536]{1,0:T(8,128)(2,1)S(1)}, u32[]{:S(2)}) copy-start(bf16[512,1536]{1,0:T(8,128)(2,1)S(1)} %convolution_convert_fusion.2) | copy-start | bytes 4718596
  396.8 40.7 %collective-permute-start.36 = (bf16[2,128,1536]{2,1,0:T(8,128)(2,1)}, bf16[2,128,1536]{2,1,0:T(8,128)(2,1)}, u32[]{:S(2)}, u32[]{:S(2)}) collective-permute-start(bf16[2,128,1536]{2,1,0:T(8,128)(2,1)} %dynamic-slice_bitcast_fusion.1), channel_id=1, source_target_pairs={{0,16},{1,17},{2,18},{3,19},{4,20},{5,21},{6,22},{7,23},{8,24},{9,... | collective-permute-start | bytes 2359304 | tf_op jit(solution)/shard_map/ppermute | solution.py:399
  431.4 4.2 collective-permute-start.33
  435.9 12.7 %collective-permute-start.34 = (bf16[2,2,48,2,2,2,128]{6,2,5,4,3,1,0:T(8,128)(2,1)S(1)}, bf16[2,2,48,2,2,2,128]{6,2,5,4,3,1,0:T(8,128)(2,1)S(1)}, u32[]{:S(2)}, u32[]{:S(2)}) collective-permute-start(bf16[2,2,48,2,2,2,128]{6,2,5,4,3,1,0:T(8,128)(2,1)S(1)} %bitcast.224), channel_id=1, source_target_pairs={{0,8},{1,9},{2,10},{3,11},{4,12},{5,13},{6,14},{7,15},{8,0},{9,1},... | collective-permute-start | bytes 1179656 | tf_op jit(solution)/shard_map/ppermute | solution.py:399
  438.9 19.5 %collective-permute-start.37 = (bf16[128,1536]{1,0:T(8,128)(2,1)S(1)}, bf16[128,1536]{1,0:T(8,128)(2,1)S(1)}, u32[]{:S(2)}, u32[]{:S(2)}) collective-permute-start(bf16[128,1536]{1,0:T(8,128)(2,1)S(1)} %fusion.18), channel_id=1, source_target_pairs={{0,4},{1,5},{2,6},{3,7},{4,0},{5,1},{6,2},{7,3},{8,12},{9,13},{10,... | collective-permute-start | bytes 1179656 | tf_op jit(solution)/shard_map/ppermute | solution.py:399
  448.7 27.8 %collective-permute-start.35 = (bf16[2,2,48,2,2,2,128]{6,2,5,4,3,1,0:T(8,128)(2,1)S(1)}, bf16[2,2,48,2,2,2,128]{6,2,5,4,3,1,0:T(8,128)(2,1)S(1)}, u32[]{:S(2)}, u32[]{:S(2)}) collective-permute-start(bf16[2,2,48,2,2,2,128]{6,2,5,4,3,1,0:T(8,128)(2,1)S(1)} %fusion.20), channel_id=1, source_target_pairs={{0,2},{1,3},{2,0},{3,1},{4,6},{5,7},{6,4},{7,5},{8,10},{9,11},{10,... | collective-permute-start | bytes 1179656 | tf_op jit(solution)/shard_map/ppermute | solution.py:399
  479.3 19.2 %all-to-all-start.1 = ((bf16[8,48,384]{2,1,0:T(8,128)(2,1)}), bf16[8,48,384]{2,1,0:T(8,128)(2,1)S(1)}, u32[]{:S(2)}, u32[]{:S(2)}) async-start(bf16[8,48,384]{2,1,0:T(8,128)(2,1)} %bitcast.226), calls=%async_computation.4 | async-start | bytes 589824 | tf_op jit(solution)/shard_map/all_to_all | solution.py:823
  484.8 2.1 collective-permute-start.30
  (37 other events, 210.9 us)
Sparse Core Ops, SparseCore 0:
  28.1 36.1 all-gather.5
  66.5 38.8 all-gather.3
  124.6 57.3 reduce-scatter.4
  326.8 38.5 all-gather.7
  384.4 30.9 reduce-scatter.8
  418.2 26.5 reduce-scatter.10
  447.2 55.8 reduce-scatter.6

commit v2 on v1

--- a/solution.py
+++ b/solution.py
@@ -386,8 +386,6 @@
 BIT_Y, BIT_X, BIT_ZH, BIT_ZL, BIT_C = 16, 8, 4, 2, 1
 PAIR = 2
 LANES = 128
-QUERY_COLS = PAIR * HEAD
-HEAD_COLS = QUERY_COLS + 2 * HEAD
 PAD_COLS = (PAIR + 2) * LANES
 BLOCK = 256
 f32 = jnp.float32
@@ -426,11 +424,24 @@
     return paired(keep, other, bit, axis)
 
 
+def after(value, *earlier):
+    return lax.optimization_barrier((value,) + earlier)[0]
+
+
+def halves(value, bit, axis):
+    mine = my_bit(bit)
+    return pick(value, mine, axis), swap(pick(value, 1 - mine, axis).astype(bf16), bit)
+
+
+def total(pair, *earlier):
+    keep, other = pair
+    if earlier:
+        other = after(other, *earlier)
+    return keep.astype(f32) + other.astype(f32)
+
+
 def reduce_bit(value, bit, axis):
-    mine = my_bit(bit)
-    keep = pick(value, mine, axis)
-    other = swap(pick(value, 1 - mine, axis).astype(bf16), bit)
-    return keep.astype(f32) + other.astype(f32)
+    return total(halves(value, bit, axis))
 
 
 def gather_square(value):
@@ -443,11 +454,15 @@
     return jnp.concatenate([chip, swap(chip, BIT_C)])
 
 
-def scatter_square(parts):
-    rows = parts.shape[0] // 8
+def chip_sums(parts):
+    middle = parts.shape[0] // 2
+    return parts[:middle].astype(f32) + swap(parts[middle:], BIT_C).astype(f32)
+
+
+def scatter_square(sums):
+    rows = sums.shape[0] // 4
     half = rows // 2
-    mine = parts[: 4 * rows].astype(f32) + swap(parts[4 * rows :], BIT_C).astype(f32)
-    own, to_x, to_z, far = (mine[i * rows : (i + 1) * rows] for i in range(4))
+    own, to_x, to_z, far = (sums[i * rows : (i + 1) * rows] for i in range(4))
     far = far.astype(bf16)
     in_z = swap(far[:half], BIT_X).astype(f32)
     in_x = swap(far[half:], BIT_ZL).astype(f32)
@@ -472,9 +487,6 @@
     return lax.psum_scatter(value, "seq", scatter_dimension=0, tiled=True)
 
 
-GROUP_OF = [((s & 1) << 2) | (s & 2) | (s >> 2) for s in range(8)]
-
-
 def dot_nn(left, right):
     return jnp.dot(left, right, preferred_element_type=f32)
 
@@ -499,7 +511,7 @@
     return matrix * cosine + pltpu.roll(matrix, LANES // 2, 1) * sine
 
 
-def project_kernel(x_ref, w_ref, freq_ref, hn_ref, q_ref, k_ref, v_ref, cos_ref, sin_ref):
+def project_kernel(x_ref, wq_ref, wkv_ref, freq_ref, hn_ref, q_ref, k_ref, v_ref, cos_ref, sin_ref):
     x = x_ref[:, :D].astype(f32)
     scale = lax.rsqrt(jnp.mean(x * x, axis=-1, keepdims=True) + norm_epsilon)
     normed = (x * scale).astype(bf16)
@@ -512,15 +524,16 @@
     sine = jnp.where(lane < LANES // 2, -jnp.sin(angles), jnp.sin(angles))
     cos_ref[...] = cosine
     sin_ref[...] = sine
-    full = dot_nn(normed, w_ref[...])
+    full = dot_nn(normed, wq_ref[...])
     for h in range(PAIR):
         part = full[:, h * LANES : (h + 1) * LANES]
         q_ref[:, h * LANES : (h + 1) * LANES] = turn(part, cosine, sine).astype(bf16)
-    k_ref[...] = turn(full[:, PAIR * LANES : (PAIR + 1) * LANES], cosine, sine).astype(bf16)
-    v_ref[...] = full[:, (PAIR + 1) * LANES :].astype(bf16)
-
-
-def project(rows_all, weights):
+    full = dot_nn(normed, wkv_ref[...])
+    k_ref[...] = turn(full[:, :LANES], cosine, sine).astype(bf16)
+    v_ref[...] = full[:, LANES:].astype(bf16)
+
+
+def project(rows_all, w_query, w_kv):
     total, width = rows_all.shape
     lane = jnp.arange(LANES) % (LANES // 2)
     freq = rotary_base ** (-lane.astype(f32) * 2.0 / HEAD)
@@ -529,12 +542,17 @@
     return pl.pallas_call(
         project_kernel,
         grid=(total // BLOCK,),
-        in_specs=[rows_of(BLOCK, width), whole(D, PAD_COLS), whole(1, LANES)],
+        in_specs=[
+            rows_of(BLOCK, width),
+            whole(D, PAIR * LANES),
+            whole(D, 2 * LANES),
+            whole(1, LANES),
+        ],
         out_specs=[rows_of(BLOCK, n) for n, t in shapes],
         out_shape=[jax.ShapeDtypeStruct((total, n), t) for n, t in shapes],
         compiler_params=pltpu.CompilerParams(vmem_limit_bytes=VMEM_BYTES),
         name="project",
-    )(rows_all, weights, freq)
+    )(rows_all, w_query, w_kv, freq)
 
 
 def allowed_pairs(dcol_ref, drow_ref, first, keys):
@@ -668,10 +686,10 @@
     )(mb, weights, query, key, value, mixed, lse, docs_col, docs_row, cosine, sine)
 
 
-def feed_kernel(hn_ref, cb_ref, wgu_ref, wd_ref, f_ref, dgu_ref, o_ref, e_ref):
+def feed_kernel(hn_ref, cb_ref, wg_ref, wu_ref, wd_ref, f_ref, dgu_ref, o_ref, e_ref):
     hidden = wd_ref.shape[0]
-    both = dot_nn(hn_ref[...], wgu_ref[...])
-    gate, up = both[:, :hidden], both[:, hidden:]
+    gate = dot_nn(hn_ref[...], wg_ref[...])
+    up = dot_nn(hn_ref[...], wu_ref[...])
     sig = 1.0 / (1.0 + jnp.exp(-gate))
     swish = gate * sig
     inner = (swish * up).astype(bf16)
@@ -680,21 +698,28 @@
     grad = dot_nt(cb_ref[...], wd_ref[...])
     dgu_ref[:, :hidden] = (grad * up * sig * (1.0 + gate * (1.0 - sig))).astype(bf16)
     dgu_ref[:, hidden:] = (grad * swish).astype(bf16)
-    e_ref[...] = dot_nt(dgu_ref[...], wgu_ref[...]).astype(bf16)
-
-
-def feed(normed, cot, w_both, w_down):
+    back = dot_nt(dgu_ref[:, :hidden], wg_ref[...]) + dot_nt(dgu_ref[:, hidden:], wu_ref[...])
+    e_ref[...] = back.astype(bf16)
+
+
+def feed(normed, cot, w_gate, w_up, w_down):
     total, hidden = normed.shape[0], w_down.shape[0]
     shapes = [(hidden, bf16), (2 * hidden, bf16), (D, bf16), (D, bf16)]
     return pl.pallas_call(
         feed_kernel,
         grid=(total // BLOCK,),
-        in_specs=[rows_of(BLOCK, D), rows_of(BLOCK, D), whole(D, 2 * hidden), whole(hidden, D)],
+        in_specs=[
+            rows_of(BLOCK, D),
+            rows_of(BLOCK, D),
+            whole(D, hidden),
+            whole(D, hidden),
+            whole(hidden, D),
+        ],
         out_specs=[rows_of(BLOCK, n) for n, t in shapes],
         out_shape=[jax.ShapeDtypeStruct((total, n), t) for n, t in shapes],
         compiler_params=pltpu.CompilerParams(vmem_limit_bytes=VMEM_BYTES),
         name="feed",
-    )(normed, cot, w_both, w_down)
+    )(normed, cot, w_gate, w_up, w_down)
 
 
 def inverse_norm(values):
@@ -741,25 +766,25 @@
     marks = jnp.stack([doc_ids, positions // 128, positions % 128], axis=1).astype(bf16)
     marks = jnp.pad(marks, ((0, 0), (0, LANES - 3)))
     rows_all = gather_rows(jnp.concatenate([inputs, marks], axis=1))
-    docs = rows_all[:, D].astype(f32)
-    docs_col, docs_row = docs[:, None], docs[None, :]
+    def heads_of(weight, each):
+        scaled = pad_heads((weight.astype(f32) * gain_one).astype(bf16))
+        return scaled.reshape(own, KV_HEADS, each * LANES)
 
     parts = jnp.concatenate(
-        [
-            (query_weight.astype(f32) * gain_one).astype(bf16).reshape(own, KV_HEADS, QUERY_COLS),
-            (key_weight.astype(f32) * gain_one).astype(bf16).reshape(own, KV_HEADS, HEAD),
-            (value_weight.astype(f32) * gain_one).astype(bf16).reshape(own, KV_HEADS, HEAD),
-        ],
-        axis=-1,
-    )
-    parts = jnp.stack([parts[:, g] for g in GROUP_OF])
-    parts = lax.all_to_all(parts, "seq", 0, 0, tiled=True)
-    w_heads = lax.all_gather(parts, "dp", axis=0, tiled=True).reshape(D, HEAD_COLS)
-    w_heads = pad_heads(w_heads)
+        [heads_of(query_weight, PAIR), heads_of(key_weight, 1), heads_of(value_weight, 1)], axis=-1
+    )
+    parts = parts.reshape(own, 2, 2, 2, PAD_COLS).transpose(3, 2, 1, 0, 4)
+    first_parts = parts
+    for axis, bit in ((2, BIT_C), (1, BIT_ZL), (0, BIT_ZH)):
+        parts = trade_bit(parts, bit, axis)
+    parts = parts.reshape(8 * own, PAD_COLS)
+    w_query, w_kv = parts[:, : PAIR * LANES], parts[:, PAIR * LANES :]
+    w_query = gather_bit(gather_bit(w_query, BIT_Y, 0), BIT_X, 1).reshape(D, PAIR * LANES)
+    w_kv = gather_bit(gather_bit(w_kv, BIT_X, 0), BIT_Y, 0).reshape(D, 2 * LANES)
 
     block = gather_bit(gather_bit(output_weight, BIT_C, 0), BIT_ZL, 0)
-    w_out = across(block.reshape(PAIR, 2, HEAD // 2, D))
-    w_out = jnp.pad(w_out, ((0, 0), (0, 0), (0, LANES // 2 - HEAD // 2), (0, 0)))
+    w_out = across(after(block, parts))
+    w_out = jnp.pad(w_out, ((0, 0), (0, 0), (0, LANES // 2 - own), (0, 0)))
     w_out = w_out.reshape(PAIR * LANES, D)
 
     both = jnp.stack(
@@ -768,64 +793,98 @@
             (up_weight.astype(f32) * gain_two).astype(bf16),
         ]
     ).reshape(2, own, 2, 2, 2, 2, 2, hidden_block)
-    both = both.transpose(3, 5, 6, 1, 0, 2, 4, 7)
-    for axis, bit in ((2, BIT_C), (0, BIT_X), (1, BIT_ZL)):
-        both = trade_bit(both, bit, axis)
-    both = both.reshape(2, 4 * own, 8 * hidden_block)
-    both = gather_bit(both, BIT_ZH, 1)
-    both = gather_bit(both, BIT_Y, 0)
-    w_both = both.reshape(D, 8 * hidden_block)
-    w_down = gather_bit(gather_bit(down_weight, BIT_ZH, 0), BIT_Y, 0).reshape(4 * hidden_block, D)
-
-    cot_all = gather_square(cotangent)
-
-    normed, query, key, value, cosine, sine = project(rows_all, w_heads)
+    both = after(both.transpose(3, 5, 6, 0, 1, 2, 4, 7), first_parts)
+    both = trade_bit(trade_bit(both, BIT_C, 2), BIT_X, 0)
+    both = trade_bit(after(both, parts), BIT_ZL, 1)
+    both = both.reshape(2, 2, 2, 2, own, 4 * hidden_block).transpose(3, 0, 1, 2, 4, 5)
+    rows_all = after(rows_all, both)
+    w_gate, w_up = both.reshape(2, 2, 4 * own, 4 * hidden_block)
+    w_gate = gather_bit(after(w_gate, w_kv), BIT_ZH, 1)
+    w_up = gather_bit(after(w_up, w_gate), BIT_ZH, 1)
+    w_down = gather_bit(after(down_weight, w_up), BIT_ZH, 0)
+
+    docs = rows_all[:, D].astype(f32)
+    docs_col, docs_row = docs[:, None], docs[None, :]
+    normed, query, key, value, cosine, sine = project(rows_all, w_query, w_kv)
     mixed, lse, term = attend(query, key, value, docs_col, docs_row, w_out)
     x_float = inputs.astype(f32)
-    middle = x_float + scatter_rows(term).astype(f32)
+    term, w_gate = lax.optimization_barrier((term, w_gate))
+    w_gate = gather_bit(w_gate, BIT_Y, 0).reshape(D, -1)
+    cot_all = gather_square(after(cotangent, term))
+    attended = after(scatter_rows(term), w_gate, w_up, cot_all)
+    w_up = gather_bit(w_up, BIT_Y, 0).reshape(D, -1)
+    w_down = gather_bit(w_down, BIT_Y, 0).reshape(-1, D)
+    middle = x_float + attended.astype(f32)
 
     inverse_two = inverse_norm(middle)
     normed_two = gather_square((middle * inverse_two).astype(bf16))
-    inner, grad_both, out_term, back_term = feed(normed_two, cot_all, w_both, w_down)
-    grad_two = scatter_square(back_term)
+    inner, grad_both, out_term, back_term = feed(
+        normed_two, cot_all, w_gate, w_up, w_down
+    )
+    width = 4 * hidden_block
+    sums = chip_sums(back_term)
+    grad_two = scatter_square(sums)
+    late_two = after(normed_two, sums)
+    gate_term = dot_tn(late_two, grad_both[:, :width]).astype(bf16)
+    grad_two = after(grad_two, gate_term)
     cot_float = cotangent.astype(f32)
     grad_middle = cot_float + norm_back(middle, inverse_two, grad_two)
-    middle_all = gather_rows(grad_middle.astype(bf16))
-    outputs = (middle + scatter_square(out_term)).astype(bf16)
-
-    down_term = dot_tn(inner, cot_all).astype(bf16).reshape(2, 2, hidden_block, D)
-    down_grad = reduce_bit(reduce_bit(down_term, BIT_Y, 0), BIT_ZH, 0)
-    both_term = dot_tn(normed_two, grad_both).astype(bf16).reshape(2, 2, 2, 4 * own, 8 * hidden_block)
-    both_sum = reduce_bit(reduce_bit(both_term, BIT_Y, 0), BIT_ZH, 1)
-    both_sum = both_sum.astype(bf16).reshape(2, 2, 2, own, 2, 2, 2, hidden_block)
-    for axis, bit in ((2, BIT_C), (0, BIT_X), (1, BIT_ZL)):
+    middle_low = grad_middle.astype(bf16)
+    middle_all = gather_rows(middle_low)
+
+    gate_pair = halves(gate_term.reshape(2, 2, 2, 4 * own, width), BIT_Y, 0)
+    up_term = dot_tn(late_two, grad_both[:, width:]).astype(bf16)
+    down_term = dot_tn(inner, cot_all).astype(bf16)
+    up_term, down_term = after(up_term, middle_low), after(down_term, middle_low)
+    up_pair = halves(up_term.reshape(2, 2, 2, 4 * own, width), BIT_Y, 0)
+    down_pair = halves(down_term.reshape(2, 2, hidden_block, D), BIT_Y, 0)
+    gate_pair = halves(total(gate_pair, middle_low), BIT_ZH, 1)
+    out_sums = chip_sums(after(out_term, middle_low))
+    outputs = (middle + scatter_square(out_sums)).astype(bf16)
+
+    grad_query, grad_kv = attend_back(
+        middle_all, w_out, query, key, value, mixed, lse, docs_col, docs_row, cosine, sine
+    )
+    up_pair = halves(total(up_pair, middle_all), BIT_ZH, 1)
+    down_pair = halves(total(down_pair, middle_all), BIT_ZH, 0)
+    first_term = (dot_nt(grad_query, w_query) + dot_nt(grad_kv, w_kv)).astype(bf16)
+    first_sum = scatter_rows(first_term).astype(f32)
+    inputs_grad = (grad_middle + norm_back(x_float, inverse_norm(x_float), first_sum)).astype(bf16)
+
+    query_term = dot_tn(normed, grad_query).astype(bf16).reshape(2, 2, 8 * own, PAIR * LANES)
+    kv_term = dot_tn(normed, grad_kv).astype(bf16).reshape(2, 2, 8 * own, 2 * LANES)
+    query_term = reduce_bit(reduce_bit(query_term, BIT_Y, 0), BIT_X, 0)
+    kv_term = reduce_bit(reduce_bit(kv_term, BIT_X, 1), BIT_Y, 0)
+    head_sums = jnp.concatenate([query_term.astype(bf16), kv_term.astype(bf16)], axis=1)
+    head_term = head_sums.reshape(2, 2, 2, own, PAD_COLS)
+    for axis, bit in ((0, BIT_ZH), (1, BIT_ZL), (2, BIT_C)):
+        head_term = trade_bit(head_term, bit, axis)
+    head_term = head_term.transpose(3, 2, 1, 0, 4).reshape(own, KV_HEADS, PAD_COLS)
+
+    def grad_of(first, each):
+        cols = head_term[..., first * LANES : (first + each) * LANES]
+        return cut_heads(cols.reshape(own, -1)).astype(f32) * gain_one
+
+    query_grad, key_grad, value_grad = grad_of(0, PAIR), grad_of(PAIR, 1), grad_of(PAIR + 1, 1)
+
+    out_part = dot_tn(mixed, middle_all).astype(bf16).reshape(2, 2, LANES // 2, D)[:, :, :own]
+    out_part = reduce_bit(reduce_bit(after(out_part, head_sums), BIT_Y, 1), BIT_X, 0)
+    output_grad = across(out_part.astype(bf16)).astype(f32)
+
+    both_sum = jnp.stack(
+        [total(gate_pair, head_sums), total(up_pair, head_sums)], axis=2
+    ).astype(bf16)
+    both_sum = both_sum.reshape(2, 4 * own, 2, width).reshape(2, 2, 2, own, 2, width)
+    for axis, bit in ((0, BIT_X), (1, BIT_ZL), (2, BIT_C)):
         both_sum = trade_bit(both_sum, bit, axis)
+    both_sum = both_sum.reshape(2, 2, 2, own, 2, 2, 2, hidden_block)
     both_sum = both_sum.transpose(4, 3, 5, 0, 6, 1, 2, 7).reshape(2, own, -1).astype(f32)
     gate_grad, up_grad = both_sum[0] * gain_two, both_sum[1] * gain_two
+    down_grad = total(down_pair, first_term)
     second_grad = jnp.sum(
         gate_weight.astype(f32) * gate_grad + up_weight.astype(f32) * up_grad, axis=-1
     ) / gain_two[:, 0]
 
-    grad_query, grad_kv = attend_back(
-        middle_all, w_out, query, key, value, mixed, lse, docs_col, docs_row, cosine, sine
-    )
-    grad_heads = jnp.concatenate([grad_query, grad_kv], axis=1)
-    first_sum = scatter_rows(dot_nt(grad_heads, w_heads).astype(bf16)).astype(f32)
-    inputs_grad = (grad_middle + norm_back(x_float, inverse_norm(x_float), first_sum)).astype(bf16)
-
-    out_part = dot_tn(mixed, middle_all).astype(bf16).reshape(PAIR * 2, LANES // 2, D)
-    out_part = out_part[:, : HEAD // 2].reshape(2, 2, own, D).transpose(1, 0, 2, 3)
-    out_part = lax.psum_scatter(out_part.reshape(4 * own, D), "dp", scatter_dimension=0, tiled=True)
-    output_grad = across(out_part).astype(f32)
-
-    head_term = cut_heads(dot_tn(normed, grad_heads).astype(bf16))
-    head_term = lax.psum_scatter(head_term, "dp", scatter_dimension=0, tiled=True)
-    head_term = lax.all_to_all(head_term.reshape(8, own, HEAD_COLS), "seq", 0, 0, tiled=True)
-    head_term = jnp.stack([head_term[GROUP_OF.index(g)] for g in range(8)], axis=1)
-    head_term = head_term.astype(f32) * gain_one[:, :, None]
-    query_grad = head_term[..., :QUERY_COLS].reshape(own, D)
-    key_grad = head_term[..., QUERY_COLS : QUERY_COLS + HEAD].reshape(own, KV_HEADS * HEAD)
-    value_grad = head_term[..., QUERY_COLS + HEAD :].reshape(own, KV_HEADS * HEAD)
     first_grad = (
         jnp.sum(query_weight.astype(f32) * query_grad, axis=-1)
         + jnp.sum(key_weight.astype(f32) * key_grad, axis=-1)

time: 523 us -> 458 us (0.88)
  waiting for transfers between devices: 281 us -> 190 us
  starting transfers between devices: 42.7 us -> 85.2 us
  blocking collectives: 16.7 us -> 0 us
  local copies, waits for them, and re-layouts: 58.8 us -> 42.1 us
  other arithmetic: 38.7 us -> 54.8 us
    all_gather x2, waiting for transfers between devices: 60.4 us -> 0.02 us  [gather_rows(): return lax.all_gather(value, 'seq', axis=0, tiled=True)]
    ppermute x36 -> x56, starting transfers between devices: 35.5 us -> 80.5 us  [swap(): return lax.ppermute(value, BOTH, [(i, i ^ bit) for i in range(32)])]
    all_gather x1 -> x0, waiting for transfers between devices: 22.3 us -> none  [body_fast(): lax.all_gather(parts, 'dp', axis=0, tiled=True).reshape(D, HEAD_COLS)]
    all_to_all x1 -> x0, blocking collectives: 16.7 us -> none  [body_fast(): parts = lax.all_to_all(parts, 'seq', 0, 0, tiled=True)]
    all_to_all x1 -> x0, waiting for transfers between devices: 10.9 us -> none  [body_fast(): lax.all_to_all(head_term.reshape(8, own, HEAD_COLS), 'seq', 0, 0, tiled=T...]
    reshape x11 -> x3, local copies, waits for them, and re-layouts: 10.8 us -> 0.81 us  [pad_heads(): split = matrix.reshape(rows, cols // (HEAD // 2), HEAD // 2)]
    unnamed x104 -> x126, local copies, waits for them, and re-layouts: 17.7 us -> 8.45 us
    ppermute x36 -> x56, waiting for transfers between devices: 185 us -> 190 us  [swap(): return lax.ppermute(value, BOTH, [(i, i ^ bit) for i in range(32)])]
  transfers between devices with their start and end apart: 46 -> 62, of which waited for: 26 -> 29; matrix products, arithmetic and copies ran while one was open for 19% -> 22% of each run, Pallas kernels for 2% -> 3%
where the time goes in v2:
time: 458 us; the launch traced here: 449 us
  waiting for transfers between devices  190 us (41%)
  starting transfers between devices  85.2 us (19%)
  other arithmetic  54.8 us (12%)
  local copies, waits for them, and re-layouts  42.1 us (9%)
  Pallas kernels  42.1 us (9%)
  matrix products  18.6 us (4%)
  between operations  15.9 us (3%)
    ppermute x56, waiting for transfers between devices, swap(): return lax.ppermute(value, BOTH, [(i, i ^ bit) for i in range(32)])  190 us
    ppermute x56, starting transfers between devices, swap(): return lax.ppermute(value, BOTH, [(i, i ^ bit) for i in range(32)])  80.5 us
    pallas_call x1, Pallas kernels, feed(): pl.pallas_call(feed_kernel, grid=(total // BLOCK,), in_specs=[rows_of(BLO...  15.2 us
    dot_general x6, matrix products, dot_tn(): lax.dot_general(left, right, (((0,), (0,)), ((), ())), preferred_element_...  14.9 us
    another operation x38, other arithmetic, paired(): jnp.stack([jnp.where(low_first, mine, other), jnp.where(low_first, other,...  12.5 us
    pallas_call x1, Pallas kernels, attend_back(): pl.pallas_call(attend_back_kernel, grid=(total // BLOCK,), in_specs=[rows...  11.3 us
  transfers between devices with their start and end apart: 62, of which 29 were waited for; matrix products, arithmetic and copies ran while one was open for 22% of the time, Pallas kernels for 3%

profile of v2, /device:TPU:0, one launch (start us, length us, event | category | flops | bytes accessed | tf_op | source)
XLA Modules:
  0.0 448.9 jit_solution(15953491456209092371)
XLA Ops:
  20.1 2.8 collective-permute-start.3
  23.0 11.8 %collective-permute-done.3 = bf16[2,2,48,512]{3,2,1,0:T(8,128)(2,1)S(1)} collective-permute-done((bf16[2,2,48,512]{3,2,1,0:T(8,128)(2,1)S(1)}, bf16[2,2,48,512]{3,2,1,0:T(8,128)(2,1)S(1)}, u32[]{:S(2)}, u32[]{:S(2)}) %collective-permute-start.3) | collective-permute-done | bytes 196640 | tf_op jit(solution)/shard_map/ppermute | solution.py:397
  34.9 6.2 %collective-permute-start.4 = (bf16[2,2,48,512]{3,2,1,0:T(8,128)(2,1)S(1)}, bf16[2,2,48,512]{3,2,1,0:T(8,128)(2,1)S(1)}, u32[]{:S(2)}, u32[]{:S(2)}) collective-permute-start(bf16[2,2,48,512]{3,2,1,0:T(8,128)(2,1)S(1)} %fusion.63), channel_id=1, source_target_pairs={{0,4},{1,5},{2,6},{3,7},{4,0},{5,1},{6,2},{7,3},{8,12},{9,13},{10,... | collective-permute-start | bytes 589832 | tf_op jit(solution)/shard_map/ppermute | solution.py:397
  43.1 12.9 %collective-permute-done.11 = bf16[2,48,1536]{2,1,0:T(8,128)(2,1)S(1)} collective-permute-done((bf16[2,48,1536]{2,1,0:T(8,128)(2,1)S(1)}, bf16[2,48,1536]{2,1,0:T(8,128)(2,1)S(1)}, u32[]{:S(2)}, u32[]{:S(2)}) %collective-permute-start.11) | collective-permute-done | bytes 294944 | tf_op jit(solution)/shard_map/ppermute | solution.py:397
  56.7 2.7 collective-permute-start.8
  61.2 3.3 collective-permute-start.5
  66.8 2.0 collective-permute-start.9
  69.8 4.9 %collective-permute-done.5 = bf16[2,2,2,48,2,2,128]{6,3,5,4,2,1,0:T(8,128)(2,1)S(1)} collective-permute-done((bf16[2,2,2,48,2,2,128]{6,3,5,4,2,1,0:T(8,128)(2,1)S(1)}, bf16[2,2,2,48,2,2,128]{6,3,5,4,2,1,0:T(8,128)(2,1)S(1)}, u32[]{:S(2)}, u32[]{:S(2)}) %collective-permute-start.5) | collective-permute-done | bytes 393248 | tf_op jit(solution)/shard_map/ppermute | solution.py:397
  79.7 6.0 %collective-permute-start.13 = (bf16[2,192,512]{2,1,0:T(8,128)(2,1)S(1)}, bf16[2,192,512]{2,1,0:T(8,128)(2,1)S(1)}, u32[]{:S(2)}, u32[]{:S(2)}) collective-permute-start(bf16[2,192,512]{2,1,0:T(8,128)(2,1)S(1)} %bitcast.330), channel_id=1, source_target_pairs={{0,4},{1,5},{2,6},{3,7},{4,0},{5,1},{6,2},{7,3},{8,12},{9,13},{10,... | collective-permute-start | bytes 1179656 | tf_op jit(solution)/shard_map/ppermute | solution.py:397
  88.2 3.4 collective-permute-done.13
  95.2 7.6 %project.1 = (bf16[1024,1536]{1,0:T(8,128)(2,1)}, bf16[1024,256]{1,0:T(8,128)(2,1)}, bf16[1024,128]{1,0:T(8,128)(2,1)}, bf16[1024,128]{1,0:T(8,128)(2,1)}, f32[1024,128]{1,0:T(8,128)}, /*index=5*/f32[1024,128]{1,0:T(8,128)}) custom-call(bf16[1024,1664]{1,0:T(8,128)(2,1)} %all-gather.3.cloned.1.call-done.x_ref, bf16[1536,256]{1,0:T(8,128)(2,1)} %bitcast.313, ...), custom_call_target="tpu_custom_call" | custom-call | tf_op jit(solution)/shard_map/project/pallas_call | solution.py:542
  102.8 8.0 %attend.1 = (bf16[1024,256]{1,0:T(8,128)(2,1)}, f32[1024,2]{1,0:T(8,128)}, bf16[1024,1536]{1,0:T(8,128)(2,1)}) custom-call(bf16[1024,256]{1,0:T(8,128)(2,1)} %get-tuple-element.50.q_ref, bf16[1024,128]{1,0:T(8,128)(2,1)} %get-tuple-element.51.k_ref, bf16[1024,128]{1,0:T(8,128)(2,1)} %get-tuple-element.52.v_ref, f32[1024,1]{1,0:T(8,128)} %slice_convert_fusion.1.dcol_ref, ...), custom_call_target="tpu_custom_call" | custom-call | tf_op jit(solution)/shard_map/attend/pallas_call | solution.py:590
  111.8 10.1 %collective-permute-start.17 = (bf16[128,1536]{1,0:T(8,128)(2,1)S(1)}, bf16[128,1536]{1,0:T(8,128)(2,1)S(1)}, u32[]{:S(2)}, u32[]{:S(2)}) collective-permute-start(bf16[128,1536]{1,0:T(8,128)(2,1)S(1)} %copy-done.12), channel_id=1, source_target_pairs={{0,2},{1,3},{2,0},{3,1},{4,6},{5,7},{6,4},{7,5},{8,10},{9,11},{10,... | collective-permute-start | bytes 1179656 | tf_op jit(solution)/shard_map/ppermute | solution.py:397
  123.5 3.4 collective-permute-start.15
  127.7 14.1 %collective-permute-done.17 = bf16[128,1536]{1,0:T(8,128)(2,1)S(1)} collective-permute-done((bf16[128,1536]{1,0:T(8,128)(2,1)S(1)}, bf16[128,1536]{1,0:T(8,128)(2,1)S(1)}, u32[]{:S(2)}, u32[]{:S(2)}) %collective-permute-start.17) | collective-permute-done | bytes 393248 | tf_op jit(solution)/shard_map/ppermute | solution.py:397
  141.8 7.1 %collective-permute-start.18 = (bf16[64,1536]{1,0:T(8,128)(2,1)S(1)}, bf16[64,1536]{1,0:T(8,128)(2,1)S(1)}, u32[]{:S(2)}, u32[]{:S(2)}) collective-permute-start(bf16[64,1536]{1,0:T(8,128)(2,1)S(1)} %slice.174), channel_id=1, source_target_pairs={{0,8},{1,9},{2,10},{3,11},{4,12},{5,13},{6,14},{7,15},{8,0},{9,1},... | collective-permute-start | bytes 589832 | tf_op jit(solution)/shard_map/ppermute | solution.py:397
  150.6 1.9 collective-permute-done.18
  153.3 7.1 %collective-permute-done.19 = bf16[64,1536]{1,0:T(8,128)(2,1)S(1)} collective-permute-done((bf16[64,1536]{1,0:T(8,128)(2,1)S(1)}, bf16[64,1536]{1,0:T(8,128)(2,1)S(1)}, u32[]{:S(2)}, u32[]{:S(2)}) %collective-permute-start.19) | collective-permute-done | bytes 196640 | tf_op jit(solution)/shard_map/ppermute | solution.py:397
  162.1 2.0 collective-permute-start.26
  164.2 24.8 %collective-permute-done.27 = bf16[128,1536]{1,0:T(8,128)(2,1)S(1)} collective-permute-done((bf16[128,1536]{1,0:T(8,128)(2,1)S(1)}, bf16[128,1536]{1,0:T(8,128)(2,1)S(1)}, u32[]{:S(2)}, u32[]{:S(2)}) %collective-permute-start.27) | collective-permute-done | bytes 393248 | tf_op jit(solution)/shard_map/ppermute | solution.py:397
  195.2 10.2 %collective-permute-done.22 = bf16[128,1536]{1,0:T(8,128)(2,1)S(1)} collective-permute-done((bf16[128,1536]{1,0:T(8,128)(2,1)S(1)}, bf16[128,1536]{1,0:T(8,128)(2,1)S(1)}, u32[]{:S(2)}, u32[]{:S(2)}) %collective-permute-start.22) | collective-permute-done | bytes 393248 | tf_op jit(solution)/shard_map/ppermute | solution.py:397
  207.3 4.2 collective-permute-done.23
  219.1 15.2 %feed.1 = (bf16[1024,512]{1,0:T(8,128)(2,1)}, bf16[1024,1024]{1,0:T(8,128)(2,1)}, bf16[1024,1536]{1,0:T(8,128)(2,1)}, bf16[1024,1536]{1,0:T(8,128)(2,1)}) custom-call(bf16[1024,1536]{1,0:T(8,128)(2,1)} %copy-done.9, bf16[1024,1536]{1,0:T(8,128)(2,1)} %constant_dynamic-update-slice_fusion.8.cb_ref, bf16[1536,512]{1,0:T(8,128)(2,1)} %bitcast.315, ...), custom_call_target="tpu_custom_call" | custom-call | tf_op jit(solution)/shard_map/feed/pallas_call | solution.py:708
  236.0 3.4 collective-permute-done.29
  241.7 5.3 %collective-permute-done.32 = bf16[64,1536]{1,0:T(8,128)(2,1)S(1)} collective-permute-done((bf16[64,1536]{1,0:T(8,128)(2,1)S(1)}, bf16[64,1536]{1,0:T(8,128)(2,1)S(1)}, u32[]{:S(2)}, u32[]{:S(2)}) %collective-permute-start.32) | collective-permute-done | bytes 196640 | tf_op jit(solution)/shard_map/ppermute | solution.py:397
  249.7 1.9 convolution_convert_fusion.2
  251.5 6.5 %collective-permute-done.33 = bf16[128,1536]{1,0:T(8,128)(2,1)S(1)} collective-permute-done((bf16[128,1536]{1,0:T(8,128)(2,1)S(1)}, bf16[128,1536]{1,0:T(8,128)(2,1)S(1)}, u32[]{:S(2)}, u32[]{:S(2)}) %collective-permute-start.33) | collective-permute-done | bytes 393248 | tf_op jit(solution)/shard_map/ppermute | solution.py:397
  263.0 3.9 convolution_convert_fusion
  273.7 13.7 %collective-permute-done.49 = bf16[2,2,192,512]{3,2,1,0:T(8,128)(2,1)S(1)} collective-permute-done((bf16[2,2,192,512]{3,2,1,0:T(8,128)(2,1)S(1)}, bf16[2,2,192,512]{3,2,1,0:T(8,128)(2,1)S(1)}, u32[]{:S(2)}, u32[]{:S(2)}) %collective-permute-start.49) | collective-permute-done | bytes 786464 | tf_op jit(solution)/shard_map/ppermute | solution.py:397
  291.5 2.6 collective-permute-start.50
  294.2 11.4 %collective-permute-done.35 = bf16[64,1536]{1,0:T(8,128)(2,1)S(1)} collective-permute-done((bf16[64,1536]{1,0:T(8,128)(2,1)S(1)}, bf16[64,1536]{1,0:T(8,128)(2,1)S(1)}, u32[]{:S(2)}, u32[]{:S(2)}) %collective-permute-start.35) | collective-permute-done | bytes 196640 | tf_op jit(solution)/shard_map/ppermute | solution.py:397
  308.7 11.3 %attend_back.1 = (bf16[1024,256]{1,0:T(8,128)(2,1)}, bf16[1024,256]{1,0:T(8,128)(2,1)}) custom-call(bf16[1024,1536]{1,0:T(8,128)(2,1)} %all-gather.5.cloned.1.call-done.mb_ref, bf16[256,1536]{1,0:T(8,128)(2,1)} %bitcast.310, bf16[1024,256]{1,0:T(8,128)(2,1)} %get-tuple-element.50.q_ref, bf16[1024,128]{1,0:T(8,128)(2,1)} %get-tuple-element.51.k_ref, ...), custom_call_target="tpu_custom_call" | custom-call | tf_op jit(solution)/shard_map/attend_back/pallas_call | solution.py:658
  320.1 3.1 convolution_convert_fusion.4
  330.0 2.5 collective-permute-start.57
  332.4 2.7 add_convert_fusion
  335.2 3.2 convolution_convert_fusion.3
  345.3 5.0 %collective-permute-done.57 = bf16[128,1536]{1,0:T(8,128)(2,1)} collective-permute-done((bf16[128,1536]{1,0:T(8,128)(2,1)}, bf16[128,1536]{1,0:T(8,128)(2,1)}, u32[]{:S(2)}, u32[]{:S(2)}) %collective-permute-start.57) | collective-permute-done | bytes 393248 | tf_op jit(solution)/shard_map/ppermute | solution.py:397
  350.3 2.0 bitcast_add_fusion
  354.5 4.2 collective-permute-done.42
  360.0 4.4 collective-permute-done.40
  364.5 2.2 collective-permute-start.43
  369.3 19.6 %collective-permute-done.52 = bf16[2,192,512]{2,1,0:T(8,128)(2,1)S(1)} collective-permute-done((bf16[2,192,512]{2,1,0:T(8,128)(2,1)S(1)}, bf16[2,192,512]{2,1,0:T(8,128)(2,1)S(1)}, u32[]{:S(2)}, u32[]{:S(2)}) %collective-permute-start.52) | collective-permute-done | bytes 393248 | tf_op jit(solution)/shard_map/ppermute | solution.py:397
  390.2 6.2 %collective-permute-done.43 = bf16[2,2,48,512]{3,2,1,0:T(8,128)(2,1)S(1)} collective-permute-done((bf16[2,2,48,512]{3,2,1,0:T(8,128)(2,1)S(1)}, bf16[2,2,48,512]{3,2,1,0:T(8,128)(2,1)S(1)}, u32[]{:S(2)}, u32[]{:S(2)}) %collective-permute-start.43) | collective-permute-done | bytes 196640 | tf_op jit(solution)/shard_map/ppermute | solution.py:397
  397.4 9.1 %collective-permute-done.44 = bf16[2,2,48,512]{3,2,1,0:T(8,128)(2,1)S(1)} collective-permute-done((bf16[2,2,48,512]{3,2,1,0:T(8,128)(2,1)S(1)}, bf16[2,2,48,512]{3,2,1,0:T(8,128)(2,1)S(1)}, u32[]{:S(2)}, u32[]{:S(2)}) %collective-permute-start.44) | collective-permute-done | bytes 196640 | tf_op jit(solution)/shard_map/ppermute | solution.py:397
  408.8 3.0 collective-permute-start.48
  419.9 2.0 fusion.46
  434.3 2.9 fusion.5
  439.0 3.0 fusion.9
  (397 shorter events, 126.3 us)
Async XLA Ops:
  7.2 84.6 %all-gather.3.cloned.1.call-start = ((), (), s32[]{:S(2)}) async-start(), calls=%async_computation.2 | async-start | bytes 3833856 | tf_op jit(solution)/shard_map/all_gather | solution.py:483
  7.2 11.0 %collective-permute-start.10 = (bf16[48,1536]{1,0:T(8,128)(2,1)}, bf16[48,1536]{1,0:T(8,128)(2,1)}, u32[]{:S(2)}, u32[]{:S(2)}) collective-permute-start(bf16[48,1536]{1,0:T(8,128)(2,1)} %param.21), channel_id=1, source_target_pairs={{0,1},{1,0},{2,3},{3,2},{4,5},{5,4},{6,7},{7,6},{8,9},{9,8},{10,11... | collective-permute-start | bytes 442376 | tf_op jit(solution)/shard_map/ppermute | solution.py:397
  13.8 178.1 %reduce-scatter.3.cloned.1.call-start = ((), (), s32[]{:S(2)}) async-start(), calls=%async_computation.3 | async-start | bytes 3538944 | tf_op jit(solution)/shard_map/reduce_scatter | solution.py:487
  17.7 23.4 %collective-permute-start = (bf16[2,2,2,48,2,2,128]{6,3,5,4,2,1,0:T(8,128)(2,1)S(1)}, bf16[2,2,2,48,2,2,128]{6,3,5,4,2,1,0:T(8,128)(2,1)S(1)}, u32[]{:S(2)}, u32[]{:S(2)}) collective-permute-start(bf16[2,2,2,48,2,2,128]{6,3,5,4,2,1,0:T(8,128)(2,1)S(1)} %bitcast.345), channel_id=1, source_target_pairs={{0,1},{1,0},{2,3},{3,2},{4,5},{5,4},{6,7},{7,6},{8,9},{9,8},{10,11... | collective-permute-start | bytes 1179656 | tf_op jit(solution)/shard_map/ppermute | solution.py:397
  20.1 14.7 %collective-permute-start.3 = (bf16[2,2,48,512]{3,2,1,0:T(8,128)(2,1)S(1)}, bf16[2,2,48,512]{3,2,1,0:T(8,128)(2,1)S(1)}, u32[]{:S(2)}, u32[]{:S(2)}) collective-permute-start(bf16[2,2,48,512]{3,2,1,0:T(8,128)(2,1)S(1)} %bitcast.347), channel_id=1, source_target_pairs={{0,2},{1,3},{2,0},{3,1},{4,6},{5,7},{6,4},{7,5},{8,10},{9,11},{10,... | collective-permute-start | bytes 589832 | tf_op jit(solution)/shard_map/ppermute | solution.py:397
  22.9 33.0 %collective-permute-start.11 = (bf16[2,48,1536]{2,1,0:T(8,128)(2,1)S(1)}, bf16[2,48,1536]{2,1,0:T(8,128)(2,1)S(1)}, u32[]{:S(2)}, u32[]{:S(2)}) collective-permute-start(bf16[2,48,1536]{2,1,0:T(8,128)(2,1)S(1)} %pad_maximum_fusion.18), channel_id=1, source_target_pairs={{0,2},{1,3},{2,0},{3,1},{4,6},{5,7},{6,4},{7,5},{8,10},{9,11},{10,... | collective-permute-start | bytes 884744 | tf_op jit(solution)/shard_map/ppermute | solution.py:397
  34.9 21.7 %collective-permute-start.4 = (bf16[2,2,48,512]{3,2,1,0:T(8,128)(2,1)S(1)}, bf16[2,2,48,512]{3,2,1,0:T(8,128)(2,1)S(1)}, u32[]{:S(2)}, u32[]{:S(2)}) collective-permute-start(bf16[2,2,48,512]{3,2,1,0:T(8,128)(2,1)S(1)} %fusion.63), channel_id=1, source_target_pairs={{0,4},{1,5},{2,6},{3,7},{4,0},{5,1},{6,2},{7,3},{8,12},{9,13},{10,... | collective-permute-start | bytes 589832 | tf_op jit(solution)/shard_map/ppermute | solution.py:397
  41.5 19.5 %collective-permute-start.1 = (bf16[2,2,2,48,2,2,128]{6,3,5,4,2,1,0:T(8,128)(2,1)S(1)}, bf16[2,2,2,48,2,2,128]{6,3,5,4,2,1,0:T(8,128)(2,1)S(1)}, u32[]{:S(2)}, u32[]{:S(2)}) collective-permute-start(bf16[2,2,2,48,2,2,128]{6,3,5,4,2,1,0:T(8,128)(2,1)S(1)} %bitcast.343), channel_id=1, source_target_pairs={{0,8},{1,9},{2,10},{3,11},{4,12},{5,13},{6,14},{7,15},{8,0},{9,1},... | collective-permute-start | bytes 1179656 | tf_op jit(solution)/shard_map/ppermute | solution.py:397
  61.2 13.5 %collective-permute-start.5 = (bf16[2,2,2,48,2,2,128]{6,3,5,4,2,1,0:T(8,128)(2,1)S(1)}, bf16[2,2,2,48,2,2,128]{6,3,5,4,2,1,0:T(8,128)(2,1)S(1)}, u32[]{:S(2)}, u32[]{:S(2)}) collective-permute-start(bf16[2,2,2,48,2,2,128]{6,3,5,4,2,1,0:T(8,128)(2,1)S(1)} %dynamic-slice_bitcast_fusion.5), channel_id=1, source_target_pairs={{0,2},{1,3},{2,0},{3,1},{4,6},{5,7},{6,4},{7,5},{8,10},{9,11},{10,... | collective-permute-start | bytes 1179656 | tf_op jit(solution)/shard_map/ppermute | solution.py:397
  65.9 9.9 %collective-permute-start.7 = (bf16[2,384,256]{2,1,0:T(8,128)(2,1)}, bf16[2,384,256]{2,1,0:T(8,128)(2,1)}, u32[]{:S(2)}, u32[]{:S(2)}) collective-permute-start(bf16[2,384,256]{2,1,0:T(8,128)(2,1)} %pad_maximum_fusion.11), channel_id=1, source_target_pairs={{0,8},{1,9},{2,10},{3,11},{4,12},{5,13},{6,14},{7,15},{8,0},{9,1},... | collective-permute-start | bytes 1179656 | tf_op jit(solution)/shard_map/ppermute | solution.py:397
  66.8 10.7 %collective-permute-start.9 = (bf16[2,384,256]{2,1,0:T(8,128)(2,1)}, bf16[2,384,256]{2,1,0:T(8,128)(2,1)}, u32[]{:S(2)}, u32[]{:S(2)}) collective-permute-start(bf16[2,384,256]{2,1,0:T(8,128)(2,1)} %pad_maximum_fusion.12), channel_id=1, source_target_pairs={{0,16},{1,17},{2,18},{3,19},{4,20},{5,21},{6,22},{7,23},{8,24},{9,... | collective-permute-start | bytes 1179656 | tf_op jit(solution)/shard_map/ppermute | solution.py:397
  68.9 18.3 %collective-permute-start.12 = (bf16[2,2,48,1536]{3,2,1,0:T(8,128)(2,1)S(1)}, bf16[2,2,48,1536]{3,2,1,0:T(8,128)(2,1)S(1)}, u32[]{:S(2)}, u32[]{:S(2)}) collective-permute-start(bf16[2,2,48,1536]{3,2,1,0:T(8,128)(2,1)S(1)} %pad_maximum_fusion.9), channel_id=1, source_target_pairs={{0,0},{1,16},{2,8},{3,24},{4,4},{5,20},{6,12},{7,28},{8,2},{9,18},... | collective-permute-start | bytes 1769480 | tf_op jit(solution)/shard_map/ppermute | solution.py:479
  79.7 11.8 %collective-permute-start.13 = (bf16[2,192,512]{2,1,0:T(8,128)(2,1)S(1)}, bf16[2,192,512]{2,1,0:T(8,128)(2,1)S(1)}, u32[]{:S(2)}, u32[]{:S(2)}) collective-permute-start(bf16[2,192,512]{2,1,0:T(8,128)(2,1)S(1)} %bitcast.330), channel_id=1, source_target_pairs={{0,4},{1,5},{2,6},{3,7},{4,0},{5,1},{6,2},{7,3},{8,12},{9,13},{10,... | collective-permute-start | bytes 1179656 | tf_op jit(solution)/shard_map/ppermute | solution.py:397
  110.8 197.9 %all-gather.5.cloned.1.call-start = ((), (), s32[]{:S(2)}) async-start(), calls=%async_computation.4 | async-start | bytes 3538944 | tf_op jit(solution)/shard_map/all_gather | solution.py:483
  111.8 30.0 %collective-permute-start.17 = (bf16[128,1536]{1,0:T(8,128)(2,1)S(1)}, bf16[128,1536]{1,0:T(8,128)(2,1)S(1)}, u32[]{:S(2)}, u32[]{:S(2)}) collective-permute-start(bf16[128,1536]{1,0:T(8,128)(2,1)S(1)} %copy-done.12), channel_id=1, source_target_pairs={{0,2},{1,3},{2,0},{3,1},{4,6},{5,7},{6,4},{7,5},{8,10},{9,11},{10,... | collective-permute-start | bytes 1179656 | tf_op jit(solution)/shard_map/ppermute | solution.py:397
  121.9 27.0 %collective-permute-start.16 = (bf16[128,1536]{1,0:T(8,128)(2,1)S(1)}, bf16[128,1536]{1,0:T(8,128)(2,1)S(1)}, u32[]{:S(2)}, u32[]{:S(2)}) collective-permute-start(bf16[128,1536]{1,0:T(8,128)(2,1)S(1)} %copy-done.12), channel_id=1, source_target_pairs={{0,8},{1,9},{2,10},{3,11},{4,12},{5,13},{6,14},{7,15},{8,0},{9,1},... | collective-permute-start | bytes 1179656 | tf_op jit(solution)/shard_map/ppermute | solution.py:397
  123.5 37.6 %collective-permute-start.15 = (bf16[2,192,512]{2,1,0:T(8,128)(2,1)S(1)}, bf16[2,192,512]{2,1,0:T(8,128)(2,1)S(1)}, u32[]{:S(2)}, u32[]{:S(2)}) collective-permute-start(bf16[2,192,512]{2,1,0:T(8,128)(2,1)S(1)} %bitcast.328), channel_id=1, source_target_pairs={{0,4},{1,5},{2,6},{3,7},{4,0},{5,1},{6,2},{7,3},{8,12},{9,13},{10,... | collective-permute-start | bytes 1179656 | tf_op jit(solution)/shard_map/ppermute | solution.py:397
  141.8 10.7 %collective-permute-start.18 = (bf16[64,1536]{1,0:T(8,128)(2,1)S(1)}, bf16[64,1536]{1,0:T(8,128)(2,1)S(1)}, u32[]{:S(2)}, u32[]{:S(2)}) collective-permute-start(bf16[64,1536]{1,0:T(8,128)(2,1)S(1)} %slice.174), channel_id=1, source_target_pairs={{0,8},{1,9},{2,10},{3,11},{4,12},{5,13},{6,14},{7,15},{8,0},{9,1},... | collective-permute-start | bytes 589832 | tf_op jit(solution)/shard_map/ppermute | solution.py:397
  148.9 11.5 %collective-permute-start.19 = (bf16[64,1536]{1,0:T(8,128)(2,1)S(1)}, bf16[64,1536]{1,0:T(8,128)(2,1)S(1)}, u32[]{:S(2)}, u32[]{:S(2)}) collective-permute-start(bf16[64,1536]{1,0:T(8,128)(2,1)S(1)} %slice.175), channel_id=1, source_target_pairs={{0,2},{1,3},{2,0},{3,1},{4,6},{5,7},{6,4},{7,5},{8,10},{9,11},{10,... | collective-permute-start | bytes 589832 | tf_op jit(solution)/shard_map/ppermute | solution.py:397
  161.1 29.5 %collective-permute-start.20 = (bf16[512,1536]{1,0:T(8,128)(2,1)S(1)}, bf16[512,1536]{1,0:T(8,128)(2,1)S(1)}, u32[]{:S(2)}, u32[]{:S(2)}) collective-permute-start(bf16[512,1536]{1,0:T(8,128)(2,1)S(1)} %get-tuple-element.198), channel_id=1, source_target_pairs={{0,1},{1,0},{2,3},{3,2},{4,5},{5,4},{6,7},{7,6},{8,9},{9,8},{10,11... | collective-permute-start | bytes 4718600 | tf_op jit(solution)/shard_map/ppermute | solution.py:397
  162.1 26.8 %collective-permute-start.27 = (bf16[128,1536]{1,0:T(8,128)(2,1)S(1)}, bf16[128,1536]{1,0:T(8,128)(2,1)S(1)}, u32[]{:S(2)}, u32[]{:S(2)}) collective-permute-start(bf16[128,1536]{1,0:T(8,128)(2,1)S(1)} %copy-done.39), channel_id=1, source_target_pairs={{0,4},{1,5},{2,6},{3,7},{4,0},{5,1},{6,2},{7,3},{8,12},{9,13},{10,... | collective-permute-start | bytes 1179656 | tf_op jit(solution)/shard_map/ppermute | solution.py:397
  162.1 26.9 %collective-permute-start.14 = (bf16[2,2,192,512]{3,2,0,1:T(8,128)(2,1)S(1)}, bf16[2,2,192,512]{3,2,0,1:T(8,128)(2,1)S(1)}, u32[]{:S(2)}, u32[]{:S(2)}) collective-permute-start(bf16[2,2,192,512]{3,2,0,1:T(8,128)(2,1)S(1)} %pad_maximum_fusion.6), channel_id=1, source_target_pairs={{0,16},{1,17},{2,18},{3,19},{4,20},{5,21},{6,22},{7,23},{8,24},{9,... | collective-permute-start | bytes 2359304 | tf_op jit(solution)/shard_map/ppermute | solution.py:397
  162.1 49.7 %collective-permute-start.26 = (bf16[2,2,192,512]{3,2,0,1:T(8,128)(2,1)}, bf16[2,2,192,512]{3,2,0,1:T(8,128)(2,1)}, u32[]{:S(2)}, u32[]{:S(2)}) collective-permute-start(bf16[2,2,192,512]{3,2,0,1:T(8,128)(2,1)} %pad_maximum_fusion.7), channel_id=1, source_target_pairs={{0,16},{1,17},{2,18},{3,19},{4,20},{5,21},{6,22},{7,23},{8,24},{9,... | collective-permute-start | bytes 2359304 | tf_op jit(solution)/shard_map/ppermute | solution.py:397
  194.2 11.2 %collective-permute-start.22 = (bf16[128,1536]{1,0:T(8,128)(2,1)S(1)}, bf16[128,1536]{1,0:T(8,128)(2,1)S(1)}, u32[]{:S(2)}, u32[]{:S(2)}) collective-permute-start(bf16[128,1536]{1,0:T(8,128)(2,1)S(1)} %get-tuple-element.97), channel_id=1, source_target_pairs={{0,2},{1,3},{2,0},{3,1},{4,6},{5,7},{6,4},{7,5},{8,10},{9,11},{10,... | collective-permute-start | bytes 1179656 | tf_op jit(solution)/shard_map/ppermute | solution.py:397
  194.3 11.7 %collective-permute-start.21 = (bf16[128,1536]{1,0:T(8,128)(2,1)S(1)}, bf16[128,1536]{1,0:T(8,128)(2,1)S(1)}, u32[]{:S(2)}, u32[]{:S(2)}) collective-permute-start(bf16[128,1536]{1,0:T(8,128)(2,1)S(1)} %get-tuple-element.97), channel_id=1, source_target_pairs={{0,8},{1,9},{2,10},{3,11},{4,12},{5,13},{6,14},{7,15},{8,0},{9,1},... | collective-permute-start | bytes 1179656 | tf_op jit(solution)/shard_map/ppermute | solution.py:397
  195.1 20.8 %collective-permute-start.28 = (bf16[2,128,1536]{2,1,0:T(8,128)(2,1)S(1)}, bf16[2,128,1536]{2,1,0:T(8,128)(2,1)S(1)}, u32[]{:S(2)}, u32[]{:S(2)}) collective-permute-start(bf16[2,128,1536]{2,1,0:T(8,128)(2,1)S(1)} %pad_maximum_fusion.8), channel_id=1, source_target_pairs={{0,16},{1,17},{2,18},{3,19},{4,20},{5,21},{6,22},{7,23},{8,24},{9,... | collective-permute-start | bytes 2359304 | tf_op jit(solution)/shard_map/ppermute | solution.py:397
  247.7 10.3 %collective-permute-start.33 = (bf16[128,1536]{1,0:T(8,128)(2,1)S(1)}, bf16[128,1536]{1,0:T(8,128)(2,1)S(1)}, u32[]{:S(2)}, u32[]{:S(2)}) collective-permute-start(bf16[128,1536]{1,0:T(8,128)(2,1)S(1)} %pad_maximum_fusion.14), channel_id=1, source_target_pairs={{0,2},{1,3},{2,0},{3,1},{4,6},{5,7},{6,4},{7,5},{8,10},{9,11},{10,... | collective-permute-start | bytes 1179656 | tf_op jit(solution)/shard_map/ppermute | solution.py:397
  248.6 9.8 %collective-permute-start.31 = (bf16[128,1536]{1,0:T(8,128)(2,1)S(1)}, bf16[128,1536]{1,0:T(8,128)(2,1)S(1)}, u32[]{:S(2)}, u32[]{:S(2)}) collective-permute-start(bf16[128,1536]{1,0:T(8,128)(2,1)S(1)} %pad_maximum_fusion.13), channel_id=1, source_target_pairs={{0,8},{1,9},{2,10},{3,11},{4,12},{5,13},{6,14},{7,15},{8,0},{9,1},... | collective-permute-start | bytes 1179656 | tf_op jit(solution)/shard_map/ppermute | solution.py:397
  261.0 176.7 %reduce-scatter.5.cloned.1.call-start = ((), (), s32[]{:S(2)}) async-start(), calls=%async_computation.5 | async-start | bytes 3538944 | tf_op jit(solution)/shard_map/reduce_scatter | solution.py:487
  262.8 24.5 %collective-permute-start.34 = (bf16[512,1536]{1,0:T(8,128)(2,1)S(1)}, bf16[512,1536]{1,0:T(8,128)(2,1)S(1)}, u32[]{:S(2)}, u32[]{:S(2)}) collective-permute-start(bf16[512,1536]{1,0:T(8,128)(2,1)S(1)} %slice.154), channel_id=1, source_target_pairs={{0,1},{1,0},{2,3},{3,2},{4,5},{5,4},{6,7},{7,6},{8,9},{9,8},{10,11... | collective-permute-start | bytes 4718600 | tf_op jit(solution)/shard_map/ppermute | solution.py:397
  266.9 20.4 %collective-permute-start.49 = (bf16[2,2,192,512]{3,2,1,0:T(8,128)(2,1)S(1)}, bf16[2,2,192,512]{3,2,1,0:T(8,128)(2,1)S(1)}, u32[]{:S(2)}, u32[]{:S(2)}) collective-permute-start(bf16[2,2,192,512]{3,2,1,0:T(8,128)(2,1)S(1)} %dynamic-slice_bitcast_fusion.2), channel_id=1, source_target_pairs={{0,16},{1,17},{2,18},{3,19},{4,20},{5,21},{6,22},{7,23},{8,24},{9,... | collective-permute-start | bytes 2359304 | tf_op jit(solution)/shard_map/ppermute | solution.py:397
  270.1 53.9 %collective-permute-start.56 = (bf16[2,128,1536]{2,1,0:T(8,128)(2,1)}, bf16[2,128,1536]{2,1,0:T(8,128)(2,1)}, u32[]{:S(2)}, u32[]{:S(2)}) collective-permute-start(bf16[2,128,1536]{2,1,0:T(8,128)(2,1)} %dynamic-slice_bitcast_fusion), channel_id=1, source_target_pairs={{0,16},{1,17},{2,18},{3,19},{4,20},{5,21},{6,22},{7,23},{8,24},{9,... | collective-permute-start | bytes 2359304 | tf_op jit(solution)/shard_map/ppermute | solution.py:397
  272.8 57.2 %collective-permute-start.51 = (bf16[2,2,192,512]{3,2,1,0:T(8,128)(2,1)}, bf16[2,2,192,512]{3,2,1,0:T(8,128)(2,1)}, u32[]{:S(2)}, u32[]{:S(2)}) collective-permute-start(bf16[2,2,192,512]{3,2,1,0:T(8,128)(2,1)} %dynamic-slice_bitcast_fusion.1), channel_id=1, source_target_pairs={{0,16},{1,17},{2,18},{3,19},{4,20},{5,21},{6,22},{7,23},{8,24},{9,... | collective-permute-start | bytes 2359304 | tf_op jit(solution)/shard_map/ppermute | solution.py:397
  289.0 16.6 %collective-permute-start.35 = (bf16[64,1536]{1,0:T(8,128)(2,1)S(1)}, bf16[64,1536]{1,0:T(8,128)(2,1)S(1)}, u32[]{:S(2)}, u32[]{:S(2)}) collective-permute-start(bf16[64,1536]{1,0:T(8,128)(2,1)S(1)} %get-tuple-element.111), channel_id=1, source_target_pairs={{0,2},{1,3},{2,0},{3,1},{4,6},{5,7},{6,4},{7,5},{8,10},{9,11},{10,... | collective-permute-start | bytes 589832 | tf_op jit(solution)/shard_map/ppermute | solution.py:397
  291.5 75.2 %collective-permute-start.50 = (bf16[2,192,512]{2,1,0:T(8,128)(2,1)}, bf16[2,192,512]{2,1,0:T(8,128)(2,1)}, u32[]{:S(2)}, u32[]{:S(2)}) collective-permute-start(bf16[2,192,512]{2,1,0:T(8,128)(2,1)} %fusion.20), channel_id=1, source_target_pairs={{0,4},{1,5},{2,6},{3,7},{4,0},{5,1},{6,2},{7,3},{8,12},{9,13},{10,... | collective-permute-start | bytes 1179656 | tf_op jit(solution)/shard_map/ppermute | solution.py:397
  306.5 132.4 %collective-permute-start.38 = (bf16[128,1536]{1,0:T(8,128)(2,1)}, bf16[128,1536]{1,0:T(8,128)(2,1)}, u32[]{:S(2)}, u32[]{:S(2)}) collective-permute-start(bf16[128,1536]{1,0:T(8,128)(2,1)} %pad_maximum_fusion.16), channel_id=1, source_target_pairs={{0,2},{1,3},{2,0},{3,1},{4,6},{5,7},{6,4},{7,5},{8,10},{9,11},{10,... | collective-permute-start | bytes 1179656 | tf_op jit(solution)/shard_map/ppermute | solution.py:397
  307.3 131.7 %collective-permute-start.36 = (bf16[128,1536]{1,0:T(8,128)(2,1)}, bf16[128,1536]{1,0:T(8,128)(2,1)}, u32[]{:S(2)}, u32[]{:S(2)}) collective-permute-start(bf16[128,1536]{1,0:T(8,128)(2,1)} %pad_maximum_fusion.15), channel_id=1, source_target_pairs={{0,8},{1,9},{2,10},{3,11},{4,12},{5,13},{6,14},{7,15},{8,0},{9,1},... | collective-permute-start | bytes 1179656 | tf_op jit(solution)/shard_map/ppermute | solution.py:397
  324.2 18.4 %collective-permute-start.41 = (bf16[2,384,256]{2,1,0:T(8,128)(2,1)}, bf16[2,384,256]{2,1,0:T(8,128)(2,1)}, u32[]{:S(2)}, u32[]{:S(2)}) collective-permute-start(bf16[2,384,256]{2,1,0:T(8,128)(2,1)} %dynamic-slice_bitcast_fusion.3), channel_id=1, source_target_pairs={{0,8},{1,9},{2,10},{3,11},{4,12},{5,13},{6,14},{7,15},{8,0},{9,1},... | collective-permute-start | bytes 1179656 | tf_op jit(solution)/shard_map/ppermute | solution.py:397
  330.0 20.3 %collective-permute-start.57 = (bf16[128,1536]{1,0:T(8,128)(2,1)}, bf16[128,1536]{1,0:T(8,128)(2,1)}, u32[]{:S(2)}, u32[]{:S(2)}) collective-permute-start(bf16[128,1536]{1,0:T(8,128)(2,1)} %fusion.22), channel_id=1, source_target_pairs={{0,4},{1,5},{2,6},{3,7},{4,0},{5,1},{6,2},{7,3},{8,12},{9,13},{10,... | collective-permute-start | bytes 1179656 | tf_op jit(solution)/shard_map/ppermute | solution.py:397
  342.7 10.4 %collective-permute-start.39 = (bf16[2,384,256]{2,1,0:T(8,128)(2,1)}, bf16[2,384,256]{2,1,0:T(8,128)(2,1)S(1)}, u32[]{:S(2)}, u32[]{:S(2)}) collective-permute-start(bf16[2,384,256]{2,1,0:T(8,128)(2,1)} %dynamic-slice_bitcast_fusion.4), channel_id=1, source_target_pairs={{0,16},{1,17},{2,18},{3,19},{4,20},{5,21},{6,22},{7,23},{8,24},{9,... | collective-permute-start | bytes 1179656 | tf_op jit(solution)/shard_map/ppermute | solution.py:397
  350.3 38.5 %collective-permute-start.52 = (bf16[2,192,512]{2,1,0:T(8,128)(2,1)S(1)}, bf16[2,192,512]{2,1,0:T(8,128)(2,1)S(1)}, u32[]{:S(2)}, u32[]{:S(2)}) collective-permute-start(bf16[2,192,512]{2,1,0:T(8,128)(2,1)S(1)} %copy-done.40), channel_id=1, source_target_pairs={{0,4},{1,5},{2,6},{3,7},{4,0},{5,1},{6,2},{7,3},{8,12},{9,13},{10,... | collective-permute-start | bytes 1179656 | tf_op jit(solution)/shard_map/ppermute | solution.py:397
  364.5 31.9 %collective-permute-start.43 = (bf16[2,2,48,512]{3,2,1,0:T(8,128)(2,1)S(1)}, bf16[2,2,48,512]{3,2,1,0:T(8,128)(2,1)S(1)}, u32[]{:S(2)}, u32[]{:S(2)}) collective-permute-start(bf16[2,2,48,512]{3,2,1,0:T(8,128)(2,1)S(1)} %dynamic-slice_bitcast_fusion.7), channel_id=1, source_target_pairs={{0,4},{1,5},{2,6},{3,7},{4,0},{5,1},{6,2},{7,3},{8,12},{9,13},{10,... | collective-permute-start | bytes 589832 | tf_op jit(solution)/shard_map/ppermute | solution.py:397
  366.8 29.8 %collective-permute-start.46 = (bf16[2,48,1536]{2,1,0:T(8,128)(2,1)S(1)}, bf16[2,48,1536]{2,1,0:T(8,128)(2,1)S(1)}, u32[]{:S(2)}, u32[]{:S(2)}) collective-permute-start(bf16[2,48,1536]{2,1,0:T(8,128)(2,1)S(1)} %dynamic-slice_bitcast_fusion.6), channel_id=1, source_target_pairs={{0,16},{1,17},{2,18},{3,19},{4,20},{5,21},{6,22},{7,23},{8,24},{9,... | collective-permute-start | bytes 884744 | tf_op jit(solution)/shard_map/ppermute | solution.py:397
  389.0 17.8 %collective-permute-start.53 = (bf16[2,2,48,2,512]{4,2,3,1,0:T(8,128)(2,1)S(1)}, bf16[2,2,48,2,512]{4,2,3,1,0:T(8,128)(2,1)S(1)}, u32[]{:S(2)}, u32[]{:S(2)}) collective-permute-start(bf16[2,2,48,2,512]{4,2,3,1,0:T(8,128)(2,1)S(1)} %fusion.30), channel_id=1, source_target_pairs={{0,8},{1,9},{2,10},{3,11},{4,12},{5,13},{6,14},{7,15},{8,0},{9,1},... | collective-permute-start | bytes 1179656 | tf_op jit(solution)/shard_map/ppermute | solution.py:397
  396.5 10.0 %collective-permute-start.44 = (bf16[2,2,48,512]{3,2,1,0:T(8,128)(2,1)S(1)}, bf16[2,2,48,512]{3,2,1,0:T(8,128)(2,1)S(1)}, u32[]{:S(2)}, u32[]{:S(2)}) collective-permute-start(bf16[2,2,48,512]{3,2,1,0:T(8,128)(2,1)S(1)} %fusion.59), channel_id=1, source_target_pairs={{0,2},{1,3},{2,0},{3,1},{4,6},{5,7},{6,4},{7,5},{8,10},{9,11},{10,... | collective-permute-start | bytes 589832 | tf_op jit(solution)/shard_map/ppermute | solution.py:397
  396.7 11.4 %collective-permute-start.47 = (bf16[48,1536]{1,0:T(8,128)(2,1)S(1)}, bf16[48,1536]{1,0:T(8,128)(2,1)S(1)}, u32[]{:S(2)}, u32[]{:S(2)}) collective-permute-start(bf16[48,1536]{1,0:T(8,128)(2,1)S(1)} %fusion.74), channel_id=1, source_target_pairs={{0,8},{1,9},{2,10},{3,11},{4,12},{5,13},{6,14},{7,15},{8,0},{9,1},... | collective-permute-start | bytes 442376 | tf_op jit(solution)/shard_map/ppermute | solution.py:397
  407.7 14.2 %collective-permute-start.54 = (bf16[2,2,48,2,512]{4,2,3,1,0:T(8,128)(2,1)}, bf16[2,2,48,2,512]{4,2,3,1,0:T(8,128)(2,1)}, u32[]{:S(2)}, u32[]{:S(2)}) collective-permute-start(bf16[2,2,48,2,512]{4,2,3,1,0:T(8,128)(2,1)} %fusion.26), channel_id=1, source_target_pairs={{0,2},{1,3},{2,0},{3,1},{4,6},{5,7},{6,4},{7,5},{8,10},{9,11},{10,... | collective-permute-start | bytes 1179656 | tf_op jit(solution)/shard_map/ppermute | solution.py:397
  408.8 16.7 %collective-permute-start.48 = (bf16[48,1536]{1,0:T(8,128)(2,1)}, bf16[48,1536]{1,0:T(8,128)(2,1)}, u32[]{:S(2)}, u32[]{:S(2)}) collective-permute-start(bf16[48,1536]{1,0:T(8,128)(2,1)} %fusion.47), channel_id=1, source_target_pairs={{0,0},{1,16},{2,8},{3,24},{4,4},{5,20},{6,12},{7,28},{8,2},{9,18},... | collective-permute-start | bytes 442376 | tf_op jit(solution)/shard_map/ppermute | solution.py:479
  (72 other events, 395.9 us)
Sparse Core Ops, SparseCore 0:
  13.9 57.2 all-gather.2
  110.9 70.5 reduce-scatter.2
  261.1 44.2 all-gather.4
  342.8 65.4 reduce-scatter.4

commit v3 on v0

--- a/solution.py
+++ b/solution.py
@@ -3,7 +3,9 @@
 import jax
 import jax.numpy as jnp
 from jax import lax
-from jax.sharding import PartitionSpec as P
+from jax.experimental import pallas as pl
+from jax.experimental.pallas import tpu as pltpu
+from jax.sharding import Mesh, PartitionSpec as P
 
 D = 1536
 HEADS = 16
@@ -380,39 +382,566 @@
         down_grad,
     )
 
+AXES = ("y", "x", "zh", "zl", "c")
+SEQUENCE = ("zh", "zl", "c")
+PAIR = 2
+LANES = 128
+QUERY_COLS = PAIR * LANES
+PAD_COLS = (PAIR + 2) * LANES
+BLOCK = 256
+f32 = jnp.float32
+bf16 = jnp.bfloat16
+
+
+def swap(value, axis):
+    return lax.ppermute(value, axis, [(0, 1), (1, 0)])
+
+
+def my_bit(axis):
+    return lax.axis_index(axis)
+
+
+def pick(value, index, axis):
+    return lax.dynamic_index_in_dim(value, index, axis, keepdims=False)
+
+
+def together(*values):
+    return lax.optimization_barrier(values)
+
+
+def paired(mine, other, bit, axis):
+    low_first = my_bit(bit) == 0
+    return jnp.stack(
+        [jnp.where(low_first, mine, other), jnp.where(low_first, other, mine)], axis
+    )
+
+
+def gather_bit(value, bit, axis):
+    return paired(value, swap(value, bit), bit, axis)
+
+
+def halves(value, bit, axis):
+    mine = my_bit(bit)
+    return pick(value, mine, axis), swap(pick(value, 1 - mine, axis).astype(bf16), bit)
+
+
+def total(pair):
+    return pair[0].astype(f32) + pair[1].astype(f32)
+
+
+def reduce_bit(value, bit, axis):
+    return total(halves(value, bit, axis))
+
+
+def across(value):
+    pairs = []
+    for i in range(32):
+        y, x, zh, zl, c = (i >> 4) & 1, (i >> 3) & 1, (i >> 2) & 1, (i >> 1) & 1, i & 1
+        pairs.append((i, c * 16 + zl * 8 + zh * 4 + x * 2 + y))
+    return lax.ppermute(value, AXES, pairs)
+
+
+def gather_rows(value):
+    return lax.all_gather(value, SEQUENCE, axis=0, tiled=True)
+
+
+def scatter_rows(value):
+    return lax.psum_scatter(value, SEQUENCE, scatter_dimension=0, tiled=True)
+
+
+def exchange(parts):
+    return lax.all_to_all(parts, SEQUENCE, 0, 0, tiled=True)
+
+
+def gather_yx(value):
+    rows, cols = value.shape
+    low, high = value[:, : cols // 2], value[:, cols // 2 :]
+    low = gather_bit(gather_bit(low, "y", 0), "x", 1)
+    high = gather_bit(gather_bit(high, "x", 0), "y", 0)
+    return low.reshape(4 * rows, -1), high.reshape(4 * rows, -1)
+
+
+def reduce_one(low, high):
+    low = low.reshape(2, 2, -1, low.shape[-1])
+    high = high.reshape(2, 2, -1, high.shape[-1])
+    return (*halves(low, "y", 0), *halves(high, "x", 1))
+
+
+def reduce_two(one):
+    return (*halves(total(one[:2]), "x", 0), *halves(total(one[2:]), "y", 0))
+
+
+def reduced(two):
+    return jnp.concatenate([total(two[:2]), total(two[2:])], axis=-1)
+
+
+def dot_nn(left, right):
+    return jnp.dot(left, right, preferred_element_type=f32)
+
+
+def dot_nt(left, right):
+    return lax.dot_general(left, right, (((1,), (1,)), ((), ())), preferred_element_type=f32)
+
+
+def dot_tn(left, right):
+    return lax.dot_general(left, right, (((0,), (0,)), ((), ())), preferred_element_type=f32)
+
+
+def whole(*shape):
+    return pl.BlockSpec(shape, lambda i: (0,) * len(shape), pipeline_mode=pl.Buffered(1))
+
+
+def rows_of(cols):
+    return pl.BlockSpec((BLOCK, cols), lambda i: (i, 0))
+
+
+def call(kernel, steps, in_specs, outs, scratch=(), vmem=60, flops=0):
+    return pl.pallas_call(
+        kernel,
+        grid=(steps,),
+        in_specs=in_specs,
+        out_specs=[spec for spec, shape, kind in outs],
+        out_shape=[jax.ShapeDtypeStruct(shape, kind) for spec, shape, kind in outs],
+        scratch_shapes=list(scratch),
+        compiler_params=pltpu.CompilerParams(vmem_limit_bytes=vmem * 1024 * 1024),
+        cost_estimate=pl.CostEstimate(flops=flops, bytes_accessed=flops // 500, transcendentals=0),
+        name=kernel.__name__,
+    )
+
+
+def turn(matrix, cosine, sine):
+    return matrix * cosine + pltpu.roll(matrix, LANES // 2, 1) * sine
+
+
+def head(h):
+    return slice(h * LANES, (h + 1) * LANES)
+
+
+SCALE = 1.0 / math.sqrt(HEAD)
+HALF = HEAD // 2
+
+
+def halves_of_heads(group, each):
+    for h in range(each):
+        for k in range(2):
+            at = ((group * each + h) * 2 + k) * HALF
+            to = h * LANES + k * (LANES // 2)
+            yield slice(at, at + HALF), slice(to, to + HALF)
+
+
+GROUPS = [((s & 1) << 2) | (s & 2) | (s >> 2) for s in range(8)]
+
+
+def pack_heads(gain_ref, q_ref, k_ref, v_ref, out_ref):
+    gain = gain_ref[...].astype(f32)
+    out_ref[...] = jnp.zeros_like(out_ref)
+    for ref, first, each in ((q_ref, 0, PAIR), (k_ref, PAIR, 1), (v_ref, PAIR + 1, 1)):
+        scaled = ref[...].astype(f32) * gain
+        for s, group in enumerate(GROUPS):
+            for at, to in halves_of_heads(group, each):
+                to = slice(first * LANES + to.start, first * LANES + to.stop)
+                out_ref[s, :, to] = scaled[:, at].astype(bf16)
+
+
+def unpack_heads(gain_ref, q_ref, k_ref, v_ref, in_ref, dq_ref, dk_ref, dv_ref, dgain_ref):
+    gain = gain_ref[...].astype(f32)
+    for ref, first, each in ((dq_ref, 0, PAIR), (dk_ref, PAIR, 1), (dv_ref, PAIR + 1, 1)):
+        for s, group in enumerate(GROUPS):
+            for at, to in halves_of_heads(group, each):
+                to = slice(first * LANES + to.start, first * LANES + to.stop)
+                ref[:, at] = in_ref[s, :, to].astype(f32) * gain
+    sums = 0.0
+    for ref, grad_ref in ((q_ref, dq_ref), (k_ref, dk_ref), (v_ref, dv_ref)):
+        sums = sums + jnp.sum(ref[...].astype(f32) * grad_ref[...], axis=-1, keepdims=True)
+    dgain_ref[...] = sums / gain
+
+
+def feed_blocks():
+    for t in range(8):
+        for b in range(4):
+            yield t, b, b * 8 + t
+
+
+def pack_feed(gain_ref, g_ref, u_ref, out_ref):
+    gain = gain_ref[...].astype(f32)
+    for t, b, i in feed_blocks():
+        out_ref[t, :, head(b)] = (g_ref[:, head(i)].astype(f32) * gain).astype(bf16)
+        out_ref[t, :, head(4 + b)] = (u_ref[:, head(i)].astype(f32) * gain).astype(bf16)
+
+
+def unpack_feed(gain_ref, g_ref, u_ref, in_ref, dg_ref, du_ref, dgain_ref):
+    gain = gain_ref[...].astype(f32)
+    sums = jnp.zeros((gain.shape[0], LANES), f32)
+    for t, b, i in feed_blocks():
+        gate = in_ref[t, :, head(b)].astype(f32) * gain
+        up = in_ref[t, :, head(4 + b)].astype(f32) * gain
+        dg_ref[:, head(i)] = gate
+        du_ref[:, head(i)] = up
+        sums = sums + g_ref[:, head(i)].astype(f32) * gate + u_ref[:, head(i)].astype(f32) * up
+    dgain_ref[...] = jnp.sum(sums, axis=-1, keepdims=True) / gain
+
+
+def project(
+    x_ref, wq_ref, wkv_ref, freq_ref, hn_ref, q_ref, k_ref, v_ref, cos_ref, sin_ref, first_ref
+):
+    x = x_ref[:, :D].astype(f32)
+    scale = lax.rsqrt(jnp.mean(x * x, axis=-1, keepdims=True) + norm_epsilon)
+    normed = (x * scale).astype(bf16)
+    hn_ref[...] = normed
+    extra = x_ref[:, D:].astype(f32)
+    place = extra[:, 0:1] * 128.0 + extra[:, 1:2]
+    at = pl.program_id(0) * BLOCK + lax.broadcasted_iota(jnp.int32, place.shape, 0)
+    first_ref[...] = at.astype(f32) - place
+    angles = place * freq_ref[...]
+    lane = lax.broadcasted_iota(jnp.int32, angles.shape, 1)
+    cosine = jnp.cos(angles)
+    sine = jnp.sin(angles)
+    sine = jnp.where(lane < LANES // 2, -sine, sine)
+    cos_ref[...] = cosine
+    sin_ref[...] = sine
+    full = dot_nn(normed, wq_ref[...])
+    for h in range(PAIR):
+        q_ref[:, head(h)] = turn(full[:, head(h)], cosine, sine).astype(bf16)
+    full = dot_nn(normed, wkv_ref[...])
+    k_ref[...] = turn(full[:, :LANES], cosine, sine).astype(bf16)
+    v_ref[...] = full[:, LANES:].astype(bf16)
+
+
+def allowed_pairs(first_ref, first, keys):
+    shape = (BLOCK, keys)
+    query_at = first + lax.broadcasted_iota(jnp.int32, shape, 0)
+    key_at = lax.broadcasted_iota(jnp.int32, shape, 1)
+    return (key_at <= query_at) & (key_at.astype(f32) >= first_ref[...])
+
+
+def attend(q_ref, k_ref, v_ref, first_ref, w_ref, a_ref, lse_ref, o_ref):
+    blocks = k_ref.shape[0] // BLOCK
+
+    def run(b):
+        keys = (b + 1) * BLOCK
+        allowed = allowed_pairs(first_ref, b * BLOCK, keys)
+        for h in range(PAIR):
+            cols = slice(h * LANES, (h + 1) * LANES)
+            logits = dot_nt(q_ref[:, cols], k_ref[:keys, :]) * SCALE
+            logits = jnp.where(allowed, logits, -1e30)
+            top = jnp.max(logits, axis=-1, keepdims=True)
+            weights = jnp.exp(logits - top)
+            total = jnp.sum(weights, axis=-1, keepdims=True)
+            mixed = dot_nn(weights.astype(bf16), v_ref[:keys, :]) / total
+            a_ref[:, cols] = mixed.astype(bf16)
+            lse_ref[:, h : h + 1] = top + jnp.log(total)
+
+    for b in range(blocks):
+        pl.when(pl.program_id(0) == b)(lambda b=b: run(b))
+    o_ref[...] = dot_nn(a_ref[...], w_ref[...]).astype(bf16)
+
+
+def attend_back(
+    mb_ref, w_ref, q_ref, k_ref, v_ref, a_ref, lse_ref, first_ref, cos_ref, sin_ref,
+    dq_ref, dkv_ref, dk_acc, dv_acc, dq_acc
+):
+    step = pl.program_id(0)
+    blocks = k_ref.shape[0] // BLOCK
+
+    @pl.when(step == 0)
+    def _():
+        dk_acc[...] = jnp.zeros_like(dk_acc)
+        dv_acc[...] = jnp.zeros_like(dv_acc)
+
+    grad_mixed = dot_nt(mb_ref[...], w_ref[...]).astype(bf16)
+
+    def run(b):
+        keys = (b + 1) * BLOCK
+        allowed = allowed_pairs(first_ref, b * BLOCK, keys)
+        for h in range(PAIR):
+            cols = slice(h * LANES, (h + 1) * LANES)
+            query = q_ref[:, cols]
+            grad = grad_mixed[:, cols]
+            delta = jnp.sum(
+                grad.astype(f32) * a_ref[:, cols].astype(f32), axis=-1, keepdims=True
+            )
+            logits = dot_nt(query, k_ref[:keys, :]) * SCALE
+            logits = jnp.where(allowed, logits, -1e30)
+            weights = jnp.exp(logits - lse_ref[:, h : h + 1])
+            grad_weights = dot_nt(grad, v_ref[:keys, :])
+            grad_logits = (weights * (grad_weights - delta) * SCALE).astype(bf16)
+            dq_acc[:, cols] = dot_nn(grad_logits, k_ref[:keys, :])
+            dk_acc[:keys, :] += dot_tn(grad_logits, query)
+            dv_acc[:keys, :] += dot_tn(weights.astype(bf16), grad)
+
+    for b in range(blocks):
+        pl.when(step == b)(lambda b=b: run(b))
+
+    rows = pl.ds(pl.multiple_of(step * BLOCK, BLOCK), BLOCK)
+    for h in range(PAIR):
+        cols = slice(h * LANES, (h + 1) * LANES)
+        dq_ref[:, cols] = turn(dq_acc[:, cols], cos_ref[rows, :], -sin_ref[rows, :]).astype(bf16)
+
+    @pl.when(step == blocks - 1)
+    def _():
+        dkv_ref[:, :LANES] = turn(dk_acc[...], cos_ref[...], -sin_ref[...]).astype(bf16)
+        dkv_ref[:, LANES:] = dv_acc[...].astype(bf16)
+
+
+def feed(
+    hn_ref, cb_ref, wg_ref, wu_ref, low_ref, high_ref, f_ref, dg_ref, du_ref, o_ref, e_ref
+):
+    middle = D // 2
+    gate = dot_nn(hn_ref[...], wg_ref[...])
+    up = dot_nn(hn_ref[...], wu_ref[...])
+    sig = 1.0 / (1.0 + jnp.exp(-gate))
+    swish = gate * sig
+    inner = (swish * up).astype(bf16)
+    f_ref[...] = inner
+    o_ref[:, :middle] = dot_nn(inner, low_ref[...]).astype(bf16)
+    o_ref[:, middle:] = dot_nn(inner, high_ref[...]).astype(bf16)
+    grad = dot_nt(cb_ref[:, :middle], low_ref[...]) + dot_nt(cb_ref[:, middle:], high_ref[...])
+    dg_ref[...] = (grad * up * sig * (1.0 + gate * (1.0 - sig))).astype(bf16)
+    du_ref[...] = (grad * swish).astype(bf16)
+    back = dot_nt(dg_ref[...], wg_ref[...]) + dot_nt(du_ref[...], wu_ref[...])
+    e_ref[...] = back.astype(bf16)
+
+
+def inverse_norm(values):
+    return lax.rsqrt(jnp.mean(values * values, axis=-1, keepdims=True) + norm_epsilon)
+
+
+def norm_back(values, inverse, grad):
+    return inverse * grad - values * inverse**3 * jnp.mean(grad * values, axis=-1, keepdims=True)
+
+
+def body_fast(
+    inputs,
+    cotangent,
+    doc_ids,
+    positions,
+    gain_first,
+    query_weight,
+    key_weight,
+    value_weight,
+    output_weight,
+    gain_second,
+    gate_weight,
+    up_weight,
+    down_weight,
+):
+    rows = inputs.shape[0]
+    own = query_weight.shape[0]
+    hidden_block = down_weight.shape[0]
+    width = 4 * hidden_block
+    total_rows = 8 * rows
+    steps = total_rows // BLOCK
+    gain_one = gain_first.reshape(own, 1)
+    gain_two = gain_second.reshape(own, 1)
+
+    marks = jnp.stack([positions // 128, positions % 128], axis=1).astype(bf16)
+    marks = jnp.pad(marks, ((0, 0), (0, LANES - 2)))
+    marked = jnp.concatenate([inputs, marks], axis=1)
+
+    heads_in = [whole(own, 1), whole(own, D), whole(own, D // 2), whole(own, D // 2)]
+    feed_in = [whole(own, 1), whole(own, 8 * width), whole(own, 8 * width)]
+    (parts,) = call(
+        pack_heads, 1, heads_in, [(whole(8, own, PAD_COLS), (8, own, PAD_COLS), bf16)]
+    )(gain_one, query_weight, key_weight, value_weight)
+    (both,) = call(
+        pack_feed, 1, feed_in, [(whole(8, own, 2 * width), (8, own, 2 * width), bf16)]
+    )(gain_two, gate_weight, up_weight)
+    rows_all = gather_rows(marked)
+    w_out = gather_bit(gather_bit(output_weight, "c", 0), "zl", 0)
+    parts, both, w_out, cotangent = together(exchange(parts), both, w_out, cotangent)
+    cot_all = gather_rows(cotangent)
+    parts = parts.reshape(8 * own, PAD_COLS)
+    w_query, w_kv = parts[:, :QUERY_COLS], parts[:, QUERY_COLS:]
+    w_query, w_kv = together(gather_bit(w_query, "y", 0), gather_bit(w_kv, "x", 0))
+    w_query = gather_bit(w_query, "x", 1).reshape(D, QUERY_COLS)
+    w_kv = gather_bit(w_kv, "y", 0).reshape(D, 2 * LANES)
+    w_out = across(w_out)
+    rows_all, w_query, w_kv, w_out, both = together(rows_all, w_query, w_kv, w_out, both)
+    w_out = jnp.pad(w_out, ((0, 0), (0, 0), (0, LANES // 2 - own), (0, 0)))
+    w_out = w_out.reshape(QUERY_COLS, D)
+
+    lane = jnp.arange(LANES) % (LANES // 2)
+    freq = rotary_base ** (-lane.astype(f32) * 2.0 / HEAD)
+    freq = jnp.where(lane < HALF, freq, 0.0).reshape(1, LANES)
+
+    def rows_out(cols, kind):
+        return (rows_of(cols), (total_rows, cols), kind)
+
+    normed, query, key, value, cosine, sine, row_first = call(
+        project,
+        steps,
+        [rows_of(D + LANES), whole(D, QUERY_COLS), whole(D, 2 * LANES), whole(1, LANES)],
+        [
+            rows_out(D, bf16),
+            rows_out(QUERY_COLS, bf16),
+            rows_out(LANES, bf16),
+            rows_out(LANES, bf16),
+            rows_out(LANES, f32),
+            rows_out(LANES, f32),
+            rows_out(1, f32),
+        ],
+        flops=3 << 30,
+    )(rows_all, w_query, w_kv, freq)
+    mixed, lse, term = call(
+        attend,
+        steps,
+        [
+            rows_of(QUERY_COLS),
+            whole(total_rows, LANES),
+            whole(total_rows, LANES),
+            rows_of(1),
+            whole(QUERY_COLS, D),
+        ],
+        [rows_out(QUERY_COLS, bf16), rows_out(PAIR, f32), rows_out(D, bf16)],
+        flops=6 << 30,
+    )(query, key, value, row_first, w_out)
+    term, both, cot_all, down_weight = together(term, exchange(both), cot_all, down_weight)
+    attended = scatter_rows(term)
+    both = both.reshape(8 * own, 2 * width)
+    attended, feed_low, feed_high, down_weight = together(
+        attended,
+        gather_bit(both[:, :width], "y", 0),
+        gather_bit(both[:, width:], "x", 0),
+        down_weight,
+    )
+    x_float = inputs.astype(f32)
+    middle = x_float + attended.astype(f32)
+
+    inverse_two = inverse_norm(middle)
+    normed_two = gather_rows((middle * inverse_two).astype(bf16))
+    w_gate = gather_bit(feed_low, "x", 1).reshape(D, width)
+    w_up = gather_bit(feed_high, "y", 0).reshape(D, width)
+    w_down = gather_yx(down_weight)
+    normed_two, w_gate, w_up, *w_down = together(normed_two, w_gate, w_up, *w_down)
+    inner, grad_gate, grad_up, out_term, back_term = call(
+        feed,
+        steps,
+        [
+            rows_of(D),
+            rows_of(D),
+            whole(D, width),
+            whole(D, width),
+            whole(width, D // 2),
+            whole(width, D // 2),
+        ],
+        [
+            rows_out(width, bf16),
+            rows_out(width, bf16),
+            rows_out(width, bf16),
+            rows_out(D, bf16),
+            rows_out(D, bf16),
+        ],
+    )(normed_two, cot_all, w_gate, w_up, *w_down)
+    back_two = scatter_rows(back_term)
+    inner, normed_two, out_term, back_term = together(inner, normed_two, out_term, back_term)
+    feed_one = reduce_one(
+        dot_tn(normed_two, grad_gate).astype(bf16), dot_tn(normed_two, grad_up).astype(bf16)
+    )
+    down_one = reduce_one(
+        dot_tn(inner, cot_all[:, : D // 2]).astype(bf16),
+        dot_tn(inner, cot_all[:, D // 2 :]).astype(bf16),
+    )
+    back_two, *rest = together(back_two, *feed_one, *down_one)
+    feed_one, down_one = rest[:4], rest[4:]
+    cot_float = cotangent.astype(f32)
+    grad_middle = cot_float + norm_back(middle, inverse_two, back_two.astype(f32))
+    middle_all = gather_rows(grad_middle.astype(bf16))
+    feed_two, down_two = reduce_two(feed_one), reduce_two(down_one)
+    feed_two = together(*feed_two)
+    both_sum = exchange(reduced(feed_two).astype(bf16).reshape(8, own, 2 * width))
+    middle_all, out_term, both_sum, *down_two = together(
+        middle_all, out_term, both_sum, *down_two
+    )
+    outputs = scatter_rows(out_term)
+
+    grad_query, grad_kv = call(
+        attend_back,
+        steps,
+        [
+            rows_of(D),
+            whole(QUERY_COLS, D),
+            rows_of(QUERY_COLS),
+            whole(total_rows, LANES),
+            whole(total_rows, LANES),
+            rows_of(QUERY_COLS),
+            rows_of(PAIR),
+            rows_of(1),
+            whole(total_rows, LANES),
+            whole(total_rows, LANES),
+        ],
+        [
+            rows_out(QUERY_COLS, bf16),
+            (whole(total_rows, 2 * LANES), (total_rows, 2 * LANES), bf16),
+        ],
+        scratch=[
+            pltpu.VMEM((total_rows, LANES), f32),
+            pltpu.VMEM((total_rows, LANES), f32),
+            pltpu.VMEM((BLOCK, QUERY_COLS), f32),
+        ],
+        flops=6 << 30,
+    )(middle_all, w_out, query, key, value, mixed, lse, row_first, cosine, sine)
+    first_term = (dot_nt(grad_query, w_query) + dot_nt(grad_kv, w_kv)).astype(bf16)
+    head_one = reduce_one(
+        dot_tn(normed, grad_query).astype(bf16), dot_tn(normed, grad_kv).astype(bf16)
+    )
+    head_two = reduce_two(together(*head_one))
+    first_term, outputs, mixed, *rest = together(first_term, outputs, mixed, *head_two, *down_two)
+    head_two, down_two = rest[:4], rest[4:]
+    first_sum = scatter_rows(first_term).astype(f32)
+    head_term = exchange(reduced(head_two).astype(bf16).reshape(8, own, PAD_COLS))
+    out_part = dot_tn(mixed, middle_all).astype(bf16).reshape(2, 2, LANES // 2, D)[:, :, :own]
+    head_term, *out_pair = together(head_term, *halves(out_part, "y", 1))
+    out_pair = halves(total(out_pair), "x", 0)
+    output_grad = across(total(out_pair).astype(bf16)).astype(f32)
+    down_grad = reduced(down_two)
+    outputs = (middle + outputs.astype(f32)).astype(bf16)
+    inputs_grad = (grad_middle + norm_back(x_float, inverse_norm(x_float), first_sum)).astype(bf16)
+
+    wide = (whole(own, 8 * width), (own, 8 * width), f32)
+    column = (whole(own, 1), (own, 1), f32)
+    gate_grad, up_grad, second_grad = call(
+        unpack_feed,
+        1,
+        [*feed_in, whole(8, own, 2 * width)],
+        [wide, wide, column],
+    )(gain_two, gate_weight, up_weight, both_sum)
+    query_grad, key_grad, value_grad, first_grad = call(
+        unpack_heads,
+        1,
+        [*heads_in, whole(8, own, PAD_COLS)],
+        [
+            (whole(own, D), (own, D), f32),
+            (whole(own, D // 2), (own, D // 2), f32),
+            (whole(own, D // 2), (own, D // 2), f32),
+            column,
+        ],
+    )(gain_one, query_weight, key_weight, value_weight, head_term)
+    return (
+        outputs,
+        inputs_grad,
+        first_grad.reshape(own),
+        query_grad,
+        key_grad,
+        value_grad,
+        output_grad,
+        second_grad.reshape(own),
+        gate_grad,
+        up_grad,
+        down_grad,
+    )
+
 
 def solution(mesh):
-    placed = (
-        P(("dp", "seq"), None),
-        P(("dp", "seq"), None),
-        P(("dp", "seq")),
-        P(("dp", "seq")),
-        P(("dp", "seq")),
-        P(("dp", "seq"), None),
-        P(("dp", "seq"), None),
-        P(("dp", "seq"), None),
-        P(("dp", "seq"), None),
-        P(("dp", "seq")),
-        P(("dp", "seq"), None),
-        P(("dp", "seq"), None),
-        P(("dp", "seq"), None),
-    )
+    shape = dict(mesh.shape)
+    step, axes = body, ("dp", "seq")
+    if shape["dp"] == 4 and shape["seq"] == KV_HEADS:
+        step, axes = body_fast, AXES
+        mesh = Mesh(mesh.devices.reshape(2, 2, 2, 2, 2), AXES)
+    wide, line = P(axes, None), P(axes)
     return jax.shard_map(
-        body,
+        step,
         mesh=mesh,
-        in_specs=placed,
-        out_specs=(
-            P(("dp", "seq"), None),
-            P(("dp", "seq"), None),
-            P(("dp", "seq")),
-            P(("dp", "seq"), None),
-            P(("dp", "seq"), None),
-            P(("dp", "seq"), None),
-            P(("dp", "seq"), None),
-            P(("dp", "seq")),
-            P(("dp", "seq"), None),
-            P(("dp", "seq"), None),
-            P(("dp", "seq"), None),
-        ),
+        in_specs=(wide, wide, line, line, line, wide, wide, wide, wide, line, wide, wide, wide),
+        out_specs=(wide, wide, line, wide, wide, wide, wide, line, wide, wide, wide),
         check_vma=False,
     )

time: 2000 us -> 416 us (0.21)
  waiting for transfers between devices: 1640 us -> 226 us
  matrix products: 173 us -> 18.1 us
  blocking collectives: 121 us -> 0 us
  starting transfers between devices: 1.32 us -> 55.1 us
  Pallas kernels: 0 us -> 52 us
    reduce_scatter x7 -> x4, waiting for transfers between devices: 1130 us -> 41.6 us  [scatter_rows(): return lax.psum_scatter(value, SEQUENCE, scatter_dimension=0, tiled=True)]
    all_gather x11 -> x4, waiting for transfers between devices: 505 us -> 20.8 us  [gather_rows(): return lax.all_gather(value, SEQUENCE, axis=0, tiled=True)]
    dot_general x28 -> x9, matrix products: 173 us -> 18.1 us  [the longest x7 14.4 us: dot_tn(): lax.dot_general(left, right, (((0,), (0,)), ((), ())), preferred_element_...]
    ppermute x0 -> x30, waiting for transfers between devices: none -> 110 us  [the longest x28 110 us: swap(): return lax.ppermute(value, axis, [(0, 1), (1, 0)])]
    unnamed x2 -> x0, blocking collectives: 82 us -> none
    all_to_all x0 -> x4, waiting for transfers between devices: none -> 53.6 us  [exchange(): return lax.all_to_all(parts, SEQUENCE, 0, 0, tiled=True)]
    pallas_call x0 -> x8, Pallas kernels: none -> 52 us  [the longest x1 15.5 us: body_fast(): call(feed, steps, [rows_of(D), rows_of(D), whole(D, width), whole(D, widt...]
    ppermute x0 -> x30, starting transfers between devices: none -> 39.3 us  [the longest x28 37.8 us: swap(): return lax.ppermute(value, axis, [(0, 1), (1, 0)])]
  transfers between devices with their start and end apart: 18 -> 42, of which waited for: 16 -> 30; matrix products, arithmetic and copies ran while one was open for 9% -> 12% of each run, Pallas kernels for 0% -> 9%
where the time goes in v3:
time: 416 us; the launch traced here: 415 us
  waiting for transfers between devices  226 us (54%)
  starting transfers between devices  55.1 us (13%)
  Pallas kernels  52 us (12%)
  other arithmetic  33.1 us (8%)
  matrix products  18.1 us (4%)
  local copies, waits for them, and re-layouts  15.1 us (4%)
  between operations  14.9 us (4%)
    ppermute x28, waiting for transfers between devices, swap(): return lax.ppermute(value, axis, [(0, 1), (1, 0)])  110 us
    all_to_all x4, waiting for transfers between devices, exchange(): return lax.all_to_all(parts, SEQUENCE, 0, 0, tiled=True)  53.6 us
    reduce_scatter x4, waiting for transfers between devices, scatter_rows(): return lax.psum_scatter(value, SEQUENCE, scatter_dimension=0, tiled=True)  41.6 us
    ppermute x28, starting transfers between devices, swap(): return lax.ppermute(value, axis, [(0, 1), (1, 0)])  37.8 us
    all_gather x4, waiting for transfers between devices, gather_rows(): return lax.all_gather(value, SEQUENCE, axis=0, tiled=True)  20.8 us
    pallas_call x1, Pallas kernels, body_fast(): call(feed, steps, [rows_of(D), rows_of(D), whole(D, width), whole(D, widt...  15.5 us
    all_to_all x4, starting transfers between devices, exchange(): return lax.all_to_all(parts, SEQUENCE, 0, 0, tiled=True)  15.1 us
    dot_general x7, matrix products, dot_tn(): lax.dot_general(left, right, (((0,), (0,)), ((), ())), preferred_element_...  14.4 us
  transfers between devices with their start and end apart: 42, of which 30 were waited for; matrix products, arithmetic and copies ran while one was open for 12% of the time, Pallas kernels for 9%

profile of v3, /device:TPU:0, one launch (start us, length us, event | category | flops | bytes accessed | tf_op | source)
XLA Modules:
  0.0 414.6 jit_solution(4302760739051927986)
XLA Ops:
  12.6 3.0 collective-permute-start.1
  16.3 2.3 pack_heads.1
  18.5 3.9 all-to-all-start
  23.2 2.2 pack_feed.1
  25.5 19.9 %all-to-all-done = bf16[8,48,512]{2,1,0:T(8,128)(2,1)S(1)} async-done(((bf16[8,48,512]{2,1,0:T(8,128)(2,1)}), bf16[8,48,512]{2,1,0:T(8,128)(2,1)S(1)}, u32[]{:S(2)}, u32[]{:S(2)}) %all-to-all-start) | async-done | bytes 393248 | tf_op jit(solution)/shard_map/all_to_all | solution.py:453
  48.6 3.2 collective-permute-done.2
  57.2 17.0 %collective-permute-done.4 = bf16[2,384,256]{2,1,0:T(8,128)(2,1)S(1)} collective-permute-done((bf16[2,384,256]{2,1,0:T(8,128)(2,1)S(1)}, bf16[2,384,256]{2,1,0:T(8,128)(2,1)S(1)}, u32[]{:S(2)}, u32[]{:S(2)}) %collective-permute-start.4) | collective-permute-done | bytes 393248 | tf_op jit(solution)/shard_map/ppermute | solution.py:397
  76.4 4.2 %all-to-all-start.1 = ((bf16[8,48,1024]{2,1,0:T(8,128)(2,1)}), bf16[8,48,1024]{2,1,0:T(8,128)(2,1)S(1)}, u32[]{:S(2)}, u32[]{:S(2)}) async-start(bf16[8,48,1024]{2,1,0:T(8,128)(2,1)} %pack_feed.1), calls=%async_computation.1 | async-start | bytes 1572864 | tf_op jit(solution)/shard_map/all_to_all | solution.py:453
  82.1 7.7 %project.1 = (bf16[1024,1536]{1,0:T(8,128)(2,1)}, bf16[1024,256]{1,0:T(8,128)(2,1)}, bf16[1024,128]{1,0:T(8,128)(2,1)}, bf16[1024,128]{1,0:T(8,128)(2,1)}, f32[1...) custom-call(bf16[1024,1664]{1,0:T(8,128)(2,1)} %all-gather.5.cloned.1.call-done.x_ref, ...), custom_call_target="tpu_custom_call" | custom-call | flops 3221225472 | bytes 6442450 | tf_op jit(solution)/shard_map/project/pallas_call | solution.py:770
  89.8 7.9 %attend.1 = (bf16[1024,256]{1,0:T(8,128)(2,1)}, f32[1024,2]{1,0:T(8,128)}, bf16[1024,1536]{1,0:T(8,128)(2,1)}) custom-call(bf16[1024,256]{1,0:T(8,128)(2,1)} %get-tuple-element.108.q_ref, bf16[1024,128]{1,0:T(8,128)(2,1)} %get-tuple-element.109.k_ref, bf16[1024,128]{1,0:T(8,128)(2,1)} %get-tuple-element.110.v_ref, f32[1024,1]{1,0:T(8,128)} %get-tuple-element.111.first_ref, ...), custom_call_target="tpu_custom_call" | custom-call | flops 6442450944 | bytes 12884901 | tf_op jit(solution)/shard_map/attend/pallas_call | solution.py:785
  97.8 19.0 %all-gather.7.cloned.1.call-done.cb_ref = bf16[1024,1536]{1,0:T(8,128)(2,1)} async-done(((bf16[128,1536]{1,0:T(8,128)(2,1)}), bf16[1024,1536]{1,0:T(8,128)(2,1)}) %all-gather.7.cloned.1.call-update) | async-done | bytes 3145744 | tf_op jit(solution)/shard_map/all_gather | solution.py:445
  117.0 2.0 collective-permute-start.7
  120.4 8.1 %collective-permute-done.7 = bf16[384,512]{1,0:T(8,128)(2,1)S(1)} collective-permute-done((bf16[384,512]{1,0:T(8,128)(2,1)S(1)}, bf16[384,512]{1,0:T(8,128)(2,1)S(1)}, u32[]{:S(2)}, u32[]{:S(2)}) %collective-permute-start.7) | collective-permute-done | bytes 393248 | tf_op jit(solution)/shard_map/ppermute | solution.py:397
  130.2 28.4 %reduce-scatter.5.cloned.1.call-done = bf16[128,1536]{1,0:T(8,128)(2,1)} async-done(((bf16[1024,1536]{1,0:T(8,128)(2,1)}), bf16[128,1536]{1,0:T(8,128)(2,1)}) %reduce-scatter.5.cloned.1.call-update) | async-done | bytes 393232 | tf_op jit(solution)/shard_map/reduce_scatter | solution.py:449
  159.9 1.9 multiply_convert_fusion
  165.1 2.7 collective-permute-done.11
  167.8 2.9 collective-permute-done.13
  175.0 7.9 %collective-permute-done.12 = bf16[2,128,768]{2,1,0:T(8,128)(2,1)S(1)} collective-permute-done((bf16[2,128,768]{2,1,0:T(8,128)(2,1)S(1)}, bf16[2,128,768]{2,1,0:T(8,128)(2,1)S(1)}, u32[]{:S(2)}, u32[]{:S(2)}) %collective-permute-start.12) | collective-permute-done | bytes 393248 | tf_op jit(solution)/shard_map/ppermute | solution.py:397
  186.1 8.4 %collective-permute-done.9 = bf16[2,384,512]{2,1,0:T(8,128)(2,1)S(1)} collective-permute-done((bf16[2,384,512]{2,1,0:T(8,128)(2,1)S(1)}, bf16[2,384,512]{2,1,0:T(8,128)(2,1)S(1)}, u32[]{:S(2)}, u32[]{:S(2)}) %collective-permute-start.9) | collective-permute-done | bytes 786464 | tf_op jit(solution)/shard_map/ppermute | solution.py:397
  197.5 1.8 all-gather.9.cloned.1.call-done.hn_ref
  199.3 15.5 %feed.1 = (bf16[1024,512]{1,0:T(8,128)(2,1)}, bf16[1024,512]{1,0:T(8,128)(2,1)}, bf16[1024,512]{1,0:T(8,128)(2,1)}, bf16[1024,1536]{1,0:T(8,128)(2,1)}, bf16[1024,1536]{1,0:T(8,128)(2,1)}) custom-call(bf16[1024,1536]{1,0:T(8,128)(2,1)} %all-gather.9.cloned.1.call-done.hn_ref, bf16[1024,1536]{1,0:T(8,128)(2,1)} %all-gather.7.cloned.1.call-done.cb_ref, ...), custom_call_target="tpu_custom_call" | custom-call | tf_op jit(solution)/shard_map/feed/pallas_call | solution.py:816
  214.9 1.8 copy-done.5
  216.7 2.4 fusion.7
  221.5 1.8 convolution_convert_fusion
  224.9 1.8 convolution_convert_fusion.1
  231.9 23.7 %collective-permute-done.17 = bf16[2,128,768]{2,1,0:T(8,128)(2,1)S(1)} collective-permute-done((bf16[2,128,768]{2,1,0:T(8,128)(2,1)S(1)}, bf16[2,128,768]{2,1,0:T(8,128)(2,1)S(1)}, u32[]{:S(2)}, u32[]{:S(2)}) %collective-permute-start.17) | collective-permute-done | bytes 393248 | tf_op jit(solution)/shard_map/ppermute | solution.py:397
  257.0 2.1 fusion.31
  265.0 5.8 %collective-permute-done.20 = bf16[384,512]{1,0:T(8,128)(2,1)S(1)} collective-permute-done((bf16[384,512]{1,0:T(8,128)(2,1)S(1)}, bf16[384,512]{1,0:T(8,128)(2,1)S(1)}, u32[]{:S(2)}, u32[]{:S(2)}) %collective-permute-start.20) | collective-permute-done | bytes 393248 | tf_op jit(solution)/shard_map/ppermute | solution.py:397
  270.8 2.7 collective-permute-done.19
  274.8 3.5 all-to-all-start.2
  281.0 4.9 %collective-permute-done.22 = bf16[128,768]{1,0:T(8,128)(2,1)S(1)} collective-permute-done((bf16[128,768]{1,0:T(8,128)(2,1)S(1)}, bf16[128,768]{1,0:T(8,128)(2,1)S(1)}, u32[]{:S(2)}, u32[]{:S(2)}) %collective-permute-start.22) | collective-permute-done | bytes 196640 | tf_op jit(solution)/shard_map/ppermute | solution.py:397
  286.5 25.0 %all-to-all-done.2.in_ref = bf16[8,48,1024]{2,1,0:T(8,128)(2,1)S(1)} async-done(((bf16[8,48,1024]{2,1,0:T(8,128)(2,1)}), bf16[8,48,1024]{2,1,0:T(8,128)(2,1)S(1)}, u32[]{:S(2)}, u32[]{:S(2)}) %all-to-all-start.2) | async-done | bytes 786464 | tf_op jit(solution)/shard_map/all_to_all | solution.py:453
  312.5 11.1 %attend_back.1 = (bf16[1024,256]{1,0:T(8,128)(2,1)}, bf16[1024,256]{1,0:T(8,128)(2,1)}) custom-call(bf16[1024,1536]{1,0:T(8,128)(2,1)} %all-gather.11.cloned.1.call-done.mb_ref, bf16[256,1536]{1,0:T(8,128)(2,1)} %bitcast.173, bf16[1024,256]{1,0:T(8,128)(2,1)} %get-tuple-element.108.q_ref, bf16[1024,128]{1,0:T(8,128)(2,1)} %get-tuple-element.109.k_ref, ...), custom_call_target="tpu_custom_call" | custom-call | flops 6442450944 | bytes 12884901 | tf_op jit(solution)/shard_map/attend_back/pallas_call | solution.py:857
  323.6 3.2 convolution_convert_fusion.3
  333.5 2.7 add_convert_fusion
  336.1 2.8 collective-permute-done.24
  338.9 3.0 collective-permute-done.23
  346.6 2.2 collective-permute-done.26
  348.8 2.7 collective-permute-done.25
  353.0 3.1 convolution_convert_fusion.2
  357.9 3.5 all-to-all-start.3
  364.3 2.9 unpack_feed.1
  369.6 2.2 collective-permute-done.27
  371.8 8.6 %all-to-all-done.3.in_ref = bf16[8,48,512]{2,1,0:T(8,128)(2,1)S(1)} async-done(((bf16[8,48,512]{2,1,0:T(8,128)(2,1)}), bf16[8,48,512]{2,1,0:T(8,128)(2,1)S(1)}, u32[]{:S(2)}, u32[]{:S(2)}) %all-to-all-start.3) | async-done | bytes 393248 | tf_op jit(solution)/shard_map/all_to_all | solution.py:453
  382.0 3.9 collective-permute-done.28
  387.8 2.4 unpack_heads.1
  392.3 11.8 %reduce-scatter.11.cloned.1.call-done = bf16[128,1536]{1,0:T(8,128)(2,1)} async-done(((bf16[1024,1536]{1,0:T(8,128)(2,1)}), bf16[128,1536]{1,0:T(8,128)(2,1)}) %reduce-scatter.11.cloned.1.call-update) | async-done | bytes 393232 | tf_op jit(solution)/shard_map/reduce_scatter | solution.py:449
  405.3 2.5 fusion.16
  (214 shorter events, 85.5 us)
Async XLA Ops:
  7.2 69.2 %all-gather.5.cloned.1.call-start = ((), (), s32[]{:S(2)}) async-start(), calls=%async_computation.8 | async-start | bytes 3833856 | tf_op jit(solution)/shard_map/all_gather | solution.py:445
  9.9 1.7 collective-permute-start
  12.6 12.8 %collective-permute-start.1 = (bf16[2,48,1536]{2,1,0:T(8,128)(2,1)S(1)}, bf16[2,48,1536]{2,1,0:T(8,128)(2,1)S(1)}, u32[]{:S(2)}, u32[]{:S(2)}) collective-permute-start(bf16[2,48,1536]{2,1,0:T(8,128)(2,1)S(1)} %pad_maximum_fusion.16), channel_id=1, source_target_pairs={{0,2},{2,0},{1,3},{3,1},{4,6},{6,4},{5,7},{7,5},{8,10},{10,8},{9,1... | collective-permute-start | bytes 884744 | tf_op jit(solution)/shard_map/ppermute | solution.py:397
  18.5 26.9 %all-to-all-start = ((bf16[8,48,512]{2,1,0:T(8,128)(2,1)}), bf16[8,48,512]{2,1,0:T(8,128)(2,1)S(1)}, u32[]{:S(2)}, u32[]{:S(2)}) async-start(bf16[8,48,512]{2,1,0:T(8,128)(2,1)} %pack_heads.1), calls=%async_computation | async-start | bytes 786432 | tf_op jit(solution)/shard_map/all_to_all | solution.py:453
  22.4 94.4 %all-gather.7.cloned.1.call-start = ((), (), s32[]{:S(2)}) async-start(), calls=%async_computation.9 | async-start | bytes 3538944 | tf_op jit(solution)/shard_map/all_gather | solution.py:445
  45.5 6.3 %collective-permute-start.2 = (bf16[384,256]{1,0:T(8,128)(2,1)S(1)}, bf16[384,256]{1,0:T(8,128)(2,1)S(1)}, u32[]{:S(2)}, u32[]{:S(2)}) collective-permute-start(bf16[384,256]{1,0:T(8,128)(2,1)S(1)} %get-tuple-element.244), channel_id=1, source_target_pairs={{0,16},{16,0},{1,17},{17,1},{2,18},{18,2},{3,19},{19,3},{4,20},{20... | collective-permute-start | bytes 589832 | tf_op jit(solution)/shard_map/ppermute | solution.py:397
  47.1 6.0 %collective-permute-start.3 = (bf16[384,256]{1,0:T(8,128)(2,1)S(1)}, bf16[384,256]{1,0:T(8,128)(2,1)S(1)}, u32[]{:S(2)}, u32[]{:S(2)}) collective-permute-start(bf16[384,256]{1,0:T(8,128)(2,1)S(1)} %get-tuple-element.243), channel_id=1, source_target_pairs={{0,8},{8,0},{1,9},{9,1},{2,10},{10,2},{3,11},{11,3},{4,12},{12,4},... | collective-permute-start | bytes 589832 | tf_op jit(solution)/shard_map/ppermute | solution.py:397
  53.2 21.1 %collective-permute-start.4 = (bf16[2,384,256]{2,1,0:T(8,128)(2,1)S(1)}, bf16[2,384,256]{2,1,0:T(8,128)(2,1)S(1)}, u32[]{:S(2)}, u32[]{:S(2)}) collective-permute-start(bf16[2,384,256]{2,1,0:T(8,128)(2,1)S(1)} %get-tuple-element.101), channel_id=1, source_target_pairs={{0,8},{8,0},{1,9},{9,1},{2,10},{10,2},{3,11},{11,3},{4,12},{12,4},... | collective-permute-start | bytes 1179656 | tf_op jit(solution)/shard_map/ppermute | solution.py:397
  54.7 21.6 %collective-permute-start.6 = (bf16[2,2,48,1536]{3,2,1,0:T(8,128)(2,1)S(1)}, bf16[2,2,48,1536]{3,2,1,0:T(8,128)(2,1)S(1)}, u32[]{:S(2)}, u32[]{:S(2)}) collective-permute-start(bf16[2,2,48,1536]{3,2,1,0:T(8,128)(2,1)S(1)} %pad_maximum_fusion.10), channel_id=1, source_target_pairs={{0,0},{1,16},{2,8},{3,24},{4,4},{5,20},{6,12},{7,28},{8,2},{9,18},... | collective-permute-start | bytes 1769480 | tf_op jit(solution)/shard_map/ppermute | solution.py:441
  55.4 19.9 %collective-permute-start.5 = (bf16[2,384,256]{2,1,0:T(8,128)(2,1)S(1)}, bf16[2,384,256]{2,1,0:T(8,128)(2,1)S(1)}, u32[]{:S(2)}, u32[]{:S(2)}) collective-permute-start(bf16[2,384,256]{2,1,0:T(8,128)(2,1)S(1)} %get-tuple-element.102), channel_id=1, source_target_pairs={{0,16},{16,0},{1,17},{17,1},{2,18},{18,2},{3,19},{19,3},{4,20},{20... | collective-permute-start | bytes 1179656 | tf_op jit(solution)/shard_map/ppermute | solution.py:397
  76.4 40.4 %all-to-all-start.1 = ((bf16[8,48,1024]{2,1,0:T(8,128)(2,1)}), bf16[8,48,1024]{2,1,0:T(8,128)(2,1)S(1)}, u32[]{:S(2)}, u32[]{:S(2)}) async-start(bf16[8,48,1024]{2,1,0:T(8,128)(2,1)} %pack_feed.1), calls=%async_computation.1 | async-start | bytes 1572864 | tf_op jit(solution)/shard_map/all_to_all | solution.py:453
  80.6 78.1 %reduce-scatter.5.cloned.1.call-start = ((), (), s32[]{:S(2)}) async-start(), calls=%async_computation.10 | async-start | bytes 3538944 | tf_op jit(solution)/shard_map/reduce_scatter | solution.py:449
  116.8 82.5 %all-gather.9.cloned.1.call-start = ((), (), s32[]{:S(2)}) async-start(), calls=%async_computation.11 | async-start | bytes 3538944 | tf_op jit(solution)/shard_map/all_gather | solution.py:445
  117.0 11.5 %collective-permute-start.7 = (bf16[384,512]{1,0:T(8,128)(2,1)S(1)}, bf16[384,512]{1,0:T(8,128)(2,1)S(1)}, u32[]{:S(2)}, u32[]{:S(2)}) collective-permute-start(bf16[384,512]{1,0:T(8,128)(2,1)S(1)} %get-tuple-element.220), channel_id=1, source_target_pairs={{0,16},{16,0},{1,17},{17,1},{2,18},{18,2},{3,19},{19,3},{4,20},{20... | collective-permute-start | bytes 1179656 | tf_op jit(solution)/shard_map/ppermute | solution.py:397
  119.0 11.0 %collective-permute-start.8 = (bf16[384,512]{1,0:T(8,128)(2,1)S(1)}, bf16[384,512]{1,0:T(8,128)(2,1)S(1)}, u32[]{:S(2)}, u32[]{:S(2)}) collective-permute-start(bf16[384,512]{1,0:T(8,128)(2,1)S(1)} %get-tuple-element.219), channel_id=1, source_target_pairs={{0,8},{8,0},{1,9},{9,1},{2,10},{10,2},{3,11},{11,3},{4,12},{12,4},... | collective-permute-start | bytes 1179656 | tf_op jit(solution)/shard_map/ppermute | solution.py:397
  130.1 28.6 %copy-start = (bf16[128,1536]{1,0:T(8,128)(2,1)S(1)}, bf16[128,1536]{1,0:T(8,128)(2,1)}, u32[]{:S(2)}) copy-start(bf16[128,1536]{1,0:T(8,128)(2,1)} %param.13) | copy-start | bytes 1179652
  130.2 31.8 %copy-start.11 = (bf16[128,1536]{1,0:T(8,128)(2,1)S(1)}, bf16[128,1536]{1,0:T(8,128)(2,1)}, u32[]{:S(2)}) copy-start(bf16[128,1536]{1,0:T(8,128)(2,1)} %param.24) | copy-start | bytes 1179652
  161.8 93.8 %reduce-scatter.7.cloned.1.call-start = ((), (), s32[]{:S(2)}) async-start(), calls=%async_computation.12 | async-start | bytes 3538944 | tf_op jit(solution)/shard_map/reduce_scatter | solution.py:449
  162.1 5.7 %collective-permute-start.11 = (bf16[128,768]{1,0:T(8,128)(2,1)S(1)}, bf16[128,768]{1,0:T(8,128)(2,1)S(1)}, u32[]{:S(2)}, u32[]{:S(2)}) collective-permute-start(bf16[128,768]{1,0:T(8,128)(2,1)S(1)} %get-tuple-element.240), channel_id=1, source_target_pairs={{0,16},{16,0},{1,17},{17,1},{2,18},{18,2},{3,19},{19,3},{4,20},{20... | collective-permute-start | bytes 589832 | tf_op jit(solution)/shard_map/ppermute | solution.py:397
  163.6 7.1 %collective-permute-start.13 = (bf16[128,768]{1,0:T(8,128)(2,1)S(1)}, bf16[128,768]{1,0:T(8,128)(2,1)S(1)}, u32[]{:S(2)}, u32[]{:S(2)}) collective-permute-start(bf16[128,768]{1,0:T(8,128)(2,1)S(1)} %get-tuple-element.239), channel_id=1, source_target_pairs={{0,8},{8,0},{1,9},{9,1},{2,10},{10,2},{3,11},{11,3},{4,12},{12,4},... | collective-permute-start | bytes 589832 | tf_op jit(solution)/shard_map/ppermute | solution.py:397
  170.8 12.1 %collective-permute-start.12 = (bf16[2,128,768]{2,1,0:T(8,128)(2,1)S(1)}, bf16[2,128,768]{2,1,0:T(8,128)(2,1)S(1)}, u32[]{:S(2)}, u32[]{:S(2)}) collective-permute-start(bf16[2,128,768]{2,1,0:T(8,128)(2,1)S(1)} %pad_maximum_fusion.13), channel_id=1, source_target_pairs={{0,8},{8,0},{1,9},{9,1},{2,10},{10,2},{3,11},{11,3},{4,12},{12,4},... | collective-permute-start | bytes 1179656 | tf_op jit(solution)/shard_map/ppermute | solution.py:397
  172.3 22.2 %collective-permute-start.9 = (bf16[2,384,512]{2,1,0:T(8,128)(2,1)S(1)}, bf16[2,384,512]{2,1,0:T(8,128)(2,1)S(1)}, u32[]{:S(2)}, u32[]{:S(2)}) collective-permute-start(bf16[2,384,512]{2,1,0:T(8,128)(2,1)S(1)} %pad_maximum_fusion.4), channel_id=1, source_target_pairs={{0,8},{8,0},{1,9},{9,1},{2,10},{10,2},{3,11},{11,3},{4,12},{12,4},... | collective-permute-start | bytes 2359304 | tf_op jit(solution)/shard_map/ppermute | solution.py:397
  172.9 12.1 %collective-permute-start.14 = (bf16[2,128,768]{2,1,0:T(8,128)(2,1)S(1)}, bf16[2,128,768]{2,1,0:T(8,128)(2,1)S(1)}, u32[]{:S(2)}, u32[]{:S(2)}) collective-permute-start(bf16[2,128,768]{2,1,0:T(8,128)(2,1)S(1)} %pad_maximum_fusion.14), channel_id=1, source_target_pairs={{0,16},{16,0},{1,17},{17,1},{2,18},{18,2},{3,19},{19,3},{4,20},{20... | collective-permute-start | bytes 1179656 | tf_op jit(solution)/shard_map/ppermute | solution.py:397
  173.6 22.5 %collective-permute-start.10 = (bf16[2,384,512]{2,1,0:T(8,128)(2,1)S(1)}, bf16[2,384,512]{2,1,0:T(8,128)(2,1)S(1)}, u32[]{:S(2)}, u32[]{:S(2)}) collective-permute-start(bf16[2,384,512]{2,1,0:T(8,128)(2,1)S(1)} %pad_maximum_fusion.5), channel_id=1, source_target_pairs={{0,16},{16,0},{1,17},{17,1},{2,18},{18,2},{3,19},{19,3},{4,20},{20... | collective-permute-start | bytes 2359304 | tf_op jit(solution)/shard_map/ppermute | solution.py:397
  214.9 96.7 %all-gather.11.cloned.1.call-start = ((), (), s32[]{:S(2)}) async-start(), calls=%async_computation.13 | async-start | bytes 3538944 | tf_op jit(solution)/shard_map/all_gather | solution.py:445
  220.0 11.9 %collective-permute-start.18 = (bf16[2,128,768]{2,1,0:T(8,128)(2,1)S(1)}, bf16[2,128,768]{2,1,0:T(8,128)(2,1)S(1)}, u32[]{:S(2)}, u32[]{:S(2)}) collective-permute-start(bf16[2,128,768]{2,1,0:T(8,128)(2,1)S(1)} %get-tuple-element.209), channel_id=1, source_target_pairs={{0,8},{8,0},{1,9},{9,1},{2,10},{10,2},{3,11},{11,3},{4,12},{12,4},... | collective-permute-start | bytes 1179656 | tf_op jit(solution)/shard_map/ppermute | solution.py:397
  224.4 31.2 %collective-permute-start.16 = (bf16[2,384,512]{2,1,0:T(8,128)(2,1)S(1)}, bf16[2,384,512]{2,1,0:T(8,128)(2,1)}, u32[]{:S(2)}, u32[]{:S(2)}) collective-permute-start(bf16[2,384,512]{2,1,0:T(8,128)(2,1)S(1)} %get-tuple-element.191), channel_id=1, source_target_pairs={{0,8},{8,0},{1,9},{9,1},{2,10},{10,2},{3,11},{11,3},{4,12},{12,4},... | collective-permute-start | bytes 2359304 | tf_op jit(solution)/shard_map/ppermute | solution.py:397
  227.8 27.8 %collective-permute-start.15 = (bf16[2,384,512]{2,1,0:T(8,128)(2,1)S(1)}, bf16[2,384,512]{2,1,0:T(8,128)(2,1)}, u32[]{:S(2)}, u32[]{:S(2)}) collective-permute-start(bf16[2,384,512]{2,1,0:T(8,128)(2,1)S(1)} %get-tuple-element.193), channel_id=1, source_target_pairs={{0,16},{16,0},{1,17},{17,1},{2,18},{18,2},{3,19},{19,3},{4,20},{20... | collective-permute-start | bytes 2359304 | tf_op jit(solution)/shard_map/ppermute | solution.py:397
  230.3 25.3 %copy-start.1 = (bf16[128,1536]{1,0:T(8,128)(2,1)S(1)}, bf16[128,1536]{1,0:T(8,128)(2,1)}, u32[]{:S(2)}) copy-start(bf16[128,1536]{1,0:T(8,128)(2,1)} %reduce-scatter.5.cloned.1.call-done) | copy-start | bytes 1179652
  230.3 26.7 %copy-start.2 = (bf16[128,1536]{1,0:T(8,128)(2,1)S(1)}, bf16[128,1536]{1,0:T(8,128)(2,1)}, u32[]{:S(2)}) copy-start(bf16[128,1536]{1,0:T(8,128)(2,1)} %param.14) | copy-start | bytes 1179652
  230.4 25.2 %collective-permute-start.17 = (bf16[2,128,768]{2,1,0:T(8,128)(2,1)S(1)}, bf16[2,128,768]{2,1,0:T(8,128)(2,1)S(1)}, u32[]{:S(2)}, u32[]{:S(2)}) collective-permute-start(bf16[2,128,768]{2,1,0:T(8,128)(2,1)S(1)} %get-tuple-element.211), channel_id=1, source_target_pairs={{0,16},{16,0},{1,17},{17,1},{2,18},{18,2},{3,19},{19,3},{4,20},{20... | collective-permute-start | bytes 1179656 | tf_op jit(solution)/shard_map/ppermute | solution.py:397
  231.9 23.7 %copy-start.18 = (bf16[2,128,768]{2,1,0:T(8,128)(2,1)}, bf16[2,128,768]{2,1,0:T(8,128)(2,1)S(1)}, u32[]{:S(2)}) copy-start(bf16[2,128,768]{2,1,0:T(8,128)(2,1)S(1)} %collective-permute-done.18) | copy-start | bytes 1179652
  260.7 10.2 %collective-permute-start.20 = (bf16[384,512]{1,0:T(8,128)(2,1)S(1)}, bf16[384,512]{1,0:T(8,128)(2,1)S(1)}, u32[]{:S(2)}, u32[]{:S(2)}) collective-permute-start(bf16[384,512]{1,0:T(8,128)(2,1)S(1)} %fusion.22), channel_id=1, source_target_pairs={{0,16},{16,0},{1,17},{17,1},{2,18},{18,2},{3,19},{19,3},{4,20},{20... | collective-permute-start | bytes 1179656 | tf_op jit(solution)/shard_map/ppermute | solution.py:397
  263.6 9.9 %collective-permute-start.19 = (bf16[384,512]{1,0:T(8,128)(2,1)S(1)}, bf16[384,512]{1,0:T(8,128)(2,1)S(1)}, u32[]{:S(2)}, u32[]{:S(2)}) collective-permute-start(bf16[384,512]{1,0:T(8,128)(2,1)S(1)} %fusion.21), channel_id=1, source_target_pairs={{0,8},{8,0},{1,9},{9,1},{2,10},{10,2},{3,11},{11,3},{4,12},{12,4},... | collective-permute-start | bytes 1179656 | tf_op jit(solution)/shard_map/ppermute | solution.py:397
  274.8 36.8 %all-to-all-start.2 = ((bf16[8,48,1024]{2,1,0:T(8,128)(2,1)}), bf16[8,48,1024]{2,1,0:T(8,128)(2,1)S(1)}, u32[]{:S(2)}, u32[]{:S(2)}) async-start(bf16[8,48,1024]{2,1,0:T(8,128)(2,1)} %pad_maximum_fusion.8), calls=%async_computation.4 | async-start | bytes 1572864 | tf_op jit(solution)/shard_map/all_to_all | solution.py:453
  278.4 74.6 %reduce-scatter.9.cloned.1.call-start = ((), (), s32[]{:S(2)}) async-start(), calls=%async_computation.14 | async-start | bytes 3538944 | tf_op jit(solution)/shard_map/reduce_scatter | solution.py:449
  278.8 7.1 %collective-permute-start.22 = (bf16[128,768]{1,0:T(8,128)(2,1)S(1)}, bf16[128,768]{1,0:T(8,128)(2,1)S(1)}, u32[]{:S(2)}, u32[]{:S(2)}) collective-permute-start(bf16[128,768]{1,0:T(8,128)(2,1)S(1)} %fusion.25), channel_id=1, source_target_pairs={{0,16},{16,0},{1,17},{17,1},{2,18},{18,2},{3,19},{19,3},{4,20},{20... | collective-permute-start | bytes 589832 | tf_op jit(solution)/shard_map/ppermute | solution.py:397
  279.5 7.0 %collective-permute-start.21 = (bf16[128,768]{1,0:T(8,128)(2,1)S(1)}, bf16[128,768]{1,0:T(8,128)(2,1)S(1)}, u32[]{:S(2)}, u32[]{:S(2)}) collective-permute-start(bf16[128,768]{1,0:T(8,128)(2,1)S(1)} %fusion.24), channel_id=1, source_target_pairs={{0,8},{8,0},{1,9},{9,1},{2,10},{10,2},{3,11},{11,3},{4,12},{12,4},... | collective-permute-start | bytes 589832 | tf_op jit(solution)/shard_map/ppermute | solution.py:397
  286.5 25.1 %copy-start.23 = (bf16[128,768]{1,0:T(8,128)(2,1)}, bf16[128,768]{1,0:T(8,128)(2,1)S(1)}, u32[]{:S(2)}) copy-start(bf16[128,768]{1,0:T(8,128)(2,1)S(1)} %collective-permute-done.21) | copy-start | bytes 589828
  312.5 91.6 %reduce-scatter.11.cloned.1.call-start = ((), (), s32[]{:S(2)}) async-start(), calls=%async_computation.15 | async-start | bytes 3538944 | tf_op jit(solution)/shard_map/reduce_scatter | solution.py:449
  327.6 11.3 %collective-permute-start.24 = (bf16[2,384,256]{2,1,0:T(8,128)(2,1)}, bf16[2,384,256]{2,1,0:T(8,128)(2,1)}, u32[]{:S(2)}, u32[]{:S(2)}) collective-permute-start(bf16[2,384,256]{2,1,0:T(8,128)(2,1)} %get-tuple-element.205), channel_id=1, source_target_pairs={{0,8},{8,0},{1,9},{9,1},{2,10},{10,2},{3,11},{11,3},{4,12},{12,4},... | collective-permute-start | bytes 1179656 | tf_op jit(solution)/shard_map/ppermute | solution.py:397
  331.0 11.0 %collective-permute-start.23 = (bf16[2,384,256]{2,1,0:T(8,128)(2,1)}, bf16[2,384,256]{2,1,0:T(8,128)(2,1)}, u32[]{:S(2)}, u32[]{:S(2)}) collective-permute-start(bf16[2,384,256]{2,1,0:T(8,128)(2,1)} %get-tuple-element.207), channel_id=1, source_target_pairs={{0,16},{16,0},{1,17},{17,1},{2,18},{18,2},{3,19},{19,3},{4,20},{20... | collective-permute-start | bytes 1179656 | tf_op jit(solution)/shard_map/ppermute | solution.py:397
  343.1 5.7 %collective-permute-start.26 = (bf16[384,256]{1,0:T(8,128)(2,1)S(1)}, bf16[384,256]{1,0:T(8,128)(2,1)S(1)}, u32[]{:S(2)}, u32[]{:S(2)}) collective-permute-start(bf16[384,256]{1,0:T(8,128)(2,1)S(1)} %fusion.27), channel_id=1, source_target_pairs={{0,16},{16,0},{1,17},{17,1},{2,18},{18,2},{3,19},{19,3},{4,20},{20... | collective-permute-start | bytes 589832 | tf_op jit(solution)/shard_map/ppermute | solution.py:397
  345.8 5.7 %collective-permute-start.25 = (bf16[384,256]{1,0:T(8,128)(2,1)S(1)}, bf16[384,256]{1,0:T(8,128)(2,1)S(1)}, u32[]{:S(2)}, u32[]{:S(2)}) collective-permute-start(bf16[384,256]{1,0:T(8,128)(2,1)S(1)} %fusion.26), channel_id=1, source_target_pairs={{0,8},{8,0},{1,9},{9,1},{2,10},{10,2},{3,11},{11,3},{4,12},{12,4},... | collective-permute-start | bytes 589832 | tf_op jit(solution)/shard_map/ppermute | solution.py:397
  357.9 22.5 %all-to-all-start.3 = ((bf16[8,48,512]{2,1,0:T(8,128)(2,1)}), bf16[8,48,512]{2,1,0:T(8,128)(2,1)S(1)}, u32[]{:S(2)}, u32[]{:S(2)}) async-start(bf16[8,48,512]{2,1,0:T(8,128)(2,1)} %pad_maximum_fusion.15), calls=%async_computation.7 | async-start | bytes 786432 | tf_op jit(solution)/shard_map/all_to_all | solution.py:453
  362.2 9.5 %collective-permute-start.27 = (bf16[2,48,1536]{2,1,0:T(8,128)(2,1)}, bf16[2,48,1536]{2,1,0:T(8,128)(2,1)S(1)}, u32[]{:S(2)}, u32[]{:S(2)}) collective-permute-start(bf16[2,48,1536]{2,1,0:T(8,128)(2,1)} %get-tuple-element.225), channel_id=1, source_target_pairs={{0,16},{16,0},{1,17},{17,1},{2,18},{18,2},{3,19},{19,3},{4,20},{20... | collective-permute-start | bytes 884744 | tf_op jit(solution)/shard_map/ppermute | solution.py:397
  380.5 5.5 %collective-permute-start.28 = (bf16[48,1536]{1,0:T(8,128)(2,1)S(1)}, bf16[48,1536]{1,0:T(8,128)(2,1)S(1)}, u32[]{:S(2)}, u32[]{:S(2)}) collective-permute-start(bf16[48,1536]{1,0:T(8,128)(2,1)S(1)} %fusion.28), channel_id=1, source_target_pairs={{0,8},{8,0},{1,9},{9,1},{2,10},{10,2},{3,11},{11,3},{4,12},{12,4},... | collective-permute-start | bytes 442376 | tf_op jit(solution)/shard_map/ppermute | solution.py:397
  386.1 5.5 %collective-permute-start.29 = (bf16[48,1536]{1,0:T(8,128)(2,1)S(1)}, bf16[48,1536]{1,0:T(8,128)(2,1)S(1)}, u32[]{:S(2)}, u32[]{:S(2)}) collective-permute-start(bf16[48,1536]{1,0:T(8,128)(2,1)S(1)} %fusion.23), channel_id=1, source_target_pairs={{0,0},{1,16},{2,8},{3,24},{4,4},{5,20},{6,12},{7,28},{8,2},{9,18},... | collective-permute-start | bytes 442376 | tf_op jit(solution)/shard_map/ppermute | solution.py:441
  (26 other events, 188.7 us)
Sparse Core Ops, SparseCore 0:
  10.2 51.6 all-gather.4
  63.6 53.2 all-gather.6
  119.1 39.5 reduce-scatter.4
  161.9 37.3 all-gather.8
  215.0 40.1 reduce-scatter.6
  259.3 51.4 all-gather.10
  313.1 39.8 reduce-scatter.8
  355.2 48.8 reduce-scatter.10
